TPU v7x, 768 devices: a whole 4x8x12 slice. The times are simulated.
768 devices in a mesh: curve: 128 (over z_hi, y, x), dp: 6 (over z_lo, core).
Axes of the slice: x: 4, y: 8, z: 12 (z_hi: 4, z_lo: 3; z = z_hi * 3 + z_lo), core: 2. Of those that a mesh axis runs over, the one named last changes fastest.
Arguments:
- queries: bfloat16 [32768, 3072], P('curve', 'dp'), may hold values from -40 to 40
- keys: bfloat16 [32768, 3072], P('curve', 'dp'), may hold values from -40 to 40
- values: bfloat16 [32768, 3072], P('curve', 'dp'), may hold values from -64 to 64
- cotangent: bfloat16 [32768, 3072], P('curve', 'dp'), may hold values from -6 to 6
- gain: float32 [3072], P('dp'), may hold values from 0.5 to 1.5
- neighbour_ids: int32 [256, 3], replicated, may hold values from 0 to 255, as said below
- neighbour_counts: int32 [256], replicated, may hold values from 1 to 3, as said below
Outputs:
- normed: bfloat16 [32768, 3072], P('curve', 'dp')
- grad_queries: bfloat16 [32768, 3072], P('curve', 'dp')
- grad_keys: bfloat16 [32768, 3072], P('curve', 'dp')
- grad_values: bfloat16 [32768, 3072], P('curve', 'dp')
Inputs may be any that keep to these rules, and one draw needn't show every extreme that they name: `neighbour_ids`: row a belongs to query block a: slot 0 holds a; slots 1 to neighbour_counts[a] - 1 hold distinct blocks b other than a with |b - a| <= 1; later slots hold a. `neighbour_counts`: the number of used slots of each row of neighbour_ids.
All inputs are finite; a program needn't handle non-finite values.
Results may differ from a plain program's by a relative error of at most 0.017.
Values may be sent and summed in bfloat16 or wider, within the bound.
No kernel may reach another device: no remote copies, remote signals or barrier semaphores. Data moves between devices by JAX's collectives and lax.ppermute only.
A program may use at most 32 MiB of HBM per device.

v0:
```python
import math

import jax
import jax.numpy as jnp
from jax import lax
from jax.sharding import PartitionSpec as P

HEADS = 24
HD = 128
BLK = 128
RIM = 1
GB = 2
NBR = 3


EPS = 1e-06


def with_halo(cells, sides, width):
    for axis, dim in sides:
        count = lax.axis_size(axis)
        ends = count - 1
        head = lax.slice_in_dim(cells, 0, width, axis=dim)
        tail = lax.slice_in_dim(cells, cells.shape[dim] - width, cells.shape[dim], axis=dim)
        cells = jnp.concatenate(
            [
                lax.ppermute(tail, axis, [(i, (i + 1) % count) for i in range(ends)]),
                cells,
                lax.ppermute(head, axis, [((i + 1) % count, i) for i in range(ends)]),
            ],
            axis=dim,
        )
    return cells


def passed_along(x, axis, by):
    peers = lax.axis_size(axis)
    pairs = [(i, i + by) for i in range(peers) if 0 <= i + by < peers]
    return lax.ppermute(x, axis, pairs)


def pick_blocks(window, where_idx):
    chosen = window[where_idx]
    return chosen.reshape(
        where_idx.shape[0], where_idx.shape[1] * window.shape[1], window.shape[2], window.shape[3]
    )


def masked_scores(query_group, key_group, usable):
    scores = jnp.einsum(
        "gqhe,gkhe->ghqk", query_group, key_group, preferred_element_type=jnp.float32
    )
    scores = scores * (1.0 / math.sqrt(query_group.shape[3]))
    keep = jnp.repeat(usable, key_group.shape[1] // usable.shape[1], axis=1)
    return jnp.where(keep[:, None, None, :], scores, -jnp.inf)


def attend_group(query_group, where_idx, usable, key_window, value_window):
    key_group = pick_blocks(key_window, where_idx)
    value_group = pick_blocks(value_window, where_idx)
    scores = masked_scores(query_group, key_group, usable)
    top = jnp.max(scores, axis=3, keepdims=True)
    shifted = jnp.exp(scores - top)
    total = jnp.sum(shifted, axis=3, keepdims=True)
    weights = (shifted / total).astype(jnp.bfloat16)
    log_total = top + jnp.log(total)
    attended = jnp.einsum(
        "ghqk,gkhe->gqhe", weights, value_group, preferred_element_type=jnp.float32
    )
    return (attended, log_total[..., 0])


def grads_group(
    query_group, dout_group, lse_group, delta_group, where_idx, usable, key_window, value_window
):
    key_group = pick_blocks(key_window, where_idx)
    value_group = pick_blocks(value_window, where_idx)
    scores = masked_scores(query_group, key_group, usable)
    probs = jnp.exp(scores - lse_group[..., None])
    dprob = jnp.einsum(
        "gqhe,gkhe->ghqk", dout_group, value_group, preferred_element_type=jnp.float32
    )
    factor = 1.0 / math.sqrt(query_group.shape[3])
    dscore = (probs * (dprob - delta_group[..., None]) * factor).astype(jnp.bfloat16)
    grad_q = jnp.einsum("ghqk,gkhe->gqhe", dscore, key_group, preferred_element_type=jnp.float32)
    grad_k = jnp.einsum("ghqk,gqhe->gkhe", dscore, query_group, preferred_element_type=jnp.float32)
    grad_v = jnp.einsum(
        "ghqk,gqhe->gkhe",
        probs.astype(jnp.bfloat16),
        dout_group,
        preferred_element_type=jnp.float32,
    )
    return (grad_q, grad_k, grad_v)


def window_slots(ids, counts, base, low, high, span):
    slots = jnp.arange(ids.shape[1], dtype=jnp.int32)
    usable = (slots[None, :] < counts[:, None]) & (ids >= low) & (ids < high)
    where_idx = jnp.clip(ids - base, 0, span - 1)
    return (where_idx, usable)


def to_groups(row_array, heads):
    return row_array.reshape(-1, GB, BLK, heads, HD)


def stats_to_groups(stat_rows):
    heads = stat_rows.shape[1]
    return stat_rows.reshape(-1, GB, BLK, heads).transpose(0, 1, 3, 2)


def stats_to_rows(stat_groups):
    heads = stat_groups.shape[2]
    return stat_groups.transpose(0, 1, 3, 2).reshape(-1, heads)


def shards(queries, keys, values, cotangent, gain, neighbour_ids, neighbour_counts):
    f32 = jnp.float32
    tok_rows, feat_dev = queries.shape
    heads_dev = feat_dev // HD
    own_blocks = tok_rows // BLK
    span = own_blocks + 2 * RIM
    rim_rows = RIM * BLK
    first = lax.axis_index("curve") * own_blocks
    base = first - RIM
    padded_ids = jnp.pad(neighbour_ids, ((RIM, RIM), (0, 0)))
    padded_counts = jnp.pad(neighbour_counts, (RIM, RIM))
    wide_keys, wide_values = (
        with_halo(keys, (("curve", 0),), rim_rows),
        with_halo(values, (("curve", 0),), rim_rows),
    )
    key_window = wide_keys.reshape(span, BLK, heads_dev, HD)
    value_window = wide_values.reshape(span, BLK, heads_dev, HD)
    own_ids = lax.dynamic_slice_in_dim(padded_ids, first + RIM, own_blocks, 0)
    own_counts = lax.dynamic_slice_in_dim(padded_counts, first + RIM, own_blocks, 0)
    own_idx, own_usable = window_slots(own_ids, own_counts, base, base, base + span, span)
    groups = own_blocks // GB

    def forward_step(inputs):
        query_group, where_idx, usable = inputs
        return attend_group(query_group, where_idx, usable, key_window, value_window)

    attended, log_totals = lax.map(
        forward_step,
        (
            to_groups(queries, heads_dev),
            own_idx.reshape(groups, GB, NBR),
            own_usable.reshape(groups, GB, NBR),
        ),
    )
    attended = attended.reshape(tok_rows, feat_dev)
    lse_rows = stats_to_rows(log_totals)
    weighted = cotangent.astype(f32) * gain
    squares = jnp.sum(attended * attended, axis=1)
    crosses = jnp.sum(weighted * attended, axis=1)
    total_feat = HEADS * HD
    square_total = lax.psum(squares, "dp")
    rinv = lax.rsqrt(square_total / total_feat + EPS)[:, None]
    normed = (gain * attended * rinv).astype(jnp.bfloat16)
    cross_mean = lax.psum(crosses, "dp") / total_feat
    d_attended = (weighted * rinv - attended * (rinv * rinv * rinv) * cross_mean[:, None]).astype(
        jnp.bfloat16
    )
    delta_rows = jnp.sum(
        (d_attended.astype(f32) * attended).reshape(tok_rows, heads_dev, HD), axis=2
    )
    n_groups = queries.shape[0] // BLK // GB
    where_idx, usable = window_slots(own_ids, own_counts, base, base, base + span, span)
    empty = jnp.zeros((span, BLK, heads_dev, HD), f32)

    def step(carry, inputs):
        key_acc, value_acc = carry
        query_group, dout_group, lse_group, delta_group, idx_group, use_group = inputs
        grad_q, grad_k, grad_v = grads_group(
            query_group,
            dout_group,
            lse_group,
            delta_group,
            idx_group,
            use_group,
            key_window,
            value_window,
        )
        flat = idx_group.reshape(-1)
        key_acc = key_acc.at[flat].add(grad_k.reshape(-1, BLK, heads_dev, HD))
        value_acc = value_acc.at[flat].add(grad_v.reshape(-1, BLK, heads_dev, HD))
        return ((key_acc, value_acc), grad_q.astype(jnp.bfloat16))

    inputs = (
        to_groups(queries, heads_dev),
        to_groups(d_attended, heads_dev),
        stats_to_groups(lse_rows),
        stats_to_groups(delta_rows),
        where_idx.reshape(n_groups, GB, NBR),
        usable.reshape(n_groups, GB, NBR),
    )
    (key_acc, value_acc), grad_q = lax.scan(step, (empty, empty), inputs)
    key_acc, value_acc, grad_queries = (
        key_acc.reshape(span * BLK, feat_dev),
        value_acc.reshape(span * BLK, feat_dev),
        grad_q.reshape(-1, feat_dev),
    )
    from_next_k, from_next_v = (
        passed_along(key_acc[:rim_rows].astype(jnp.bfloat16), "curve", -1).astype(jnp.float32),
        passed_along(value_acc[:rim_rows].astype(jnp.bfloat16), "curve", -1).astype(jnp.float32),
    )
    from_prev_k, from_prev_v = (
        passed_along(key_acc[span * BLK - rim_rows :].astype(jnp.bfloat16), "curve", 1).astype(
            jnp.float32
        ),
        passed_along(value_acc[span * BLK - rim_rows :].astype(jnp.bfloat16), "curve", 1).astype(
            jnp.float32
        ),
    )
    grad_keys = key_acc[rim_rows : rim_rows + tok_rows]
    grad_values = value_acc[rim_rows : rim_rows + tok_rows]
    grad_keys = grad_keys.at[:rim_rows].add(from_prev_k).at[tok_rows - rim_rows :].add(from_next_k)
    grad_values = (
        grad_values.at[:rim_rows].add(from_prev_v).at[tok_rows - rim_rows :].add(from_next_v)
    )
    return (normed, grad_queries, grad_keys.astype(jnp.bfloat16), grad_values.astype(jnp.bfloat16))


def solution(mesh):
    placed = (
        P("curve", "dp"),
        P("curve", "dp"),
        P("curve", "dp"),
        P("curve", "dp"),
        P("dp"),
        P(),
        P(),
    )
    return jax.shard_map(
        shards,
        mesh=mesh,
        in_specs=placed,
        out_specs=(P("curve", "dp"), P("curve", "dp"), P("curve", "dp"), P("curve", "dp")),
        check_vma=False,
    )
```

profile of v0, /device:TPU:382, one launch (start us, length us, event | category | flops | bytes accessed | tf_op | source)
XLA Modules:
  0.0 115.2 jit_solution(15282323268412599315)
XLA Ops:
  0.6 1.0 fusion.28
  1.7 2.7 %collective-permute-start.3 = (bf16[128,512]{1,0:T(8,128)(2,1)S(1)}, bf16[128,512]{1,0:T(8,128)(2,1)S(1)}, u32[]{:S(2)}, u32[]{:S(2)}) collective-permute-start(bf16[128,512]{1,0:T(8,128)(2,1)S(1)} %get-tuple-element.126), channel_id=1, source_target_pairs={{6,0},{12,6},{18,12},{24,18},{30,24},{36,30},{42,36},{48,42},{54,4... | collective-permute-start | bytes 393224 | tf_op jit(solution)/shard_map/ppermute | solution.py:29
  4.4 10.3 %collective-permute-start.2 = (bf16[128,512]{1,0:T(8,128)(2,1)S(1)}, bf16[128,512]{1,0:T(8,128)(2,1)S(1)}, u32[]{:S(2)}, u32[]{:S(2)}) collective-permute-start(bf16[128,512]{1,0:T(8,128)(2,1)S(1)} %get-tuple-element.125), channel_id=1, source_target_pairs={{0,6},{6,12},{12,18},{18,24},{24,30},{30,36},{36,42},{42,48},{48,5... | collective-permute-start | bytes 393224 | tf_op jit(solution)/shard_map/ppermute | solution.py:27
  14.8 1.0 fusion.27
  15.8 1.9 %collective-permute-start.1 = (bf16[128,512]{1,0:T(8,128)(2,1)S(1)}, bf16[128,512]{1,0:T(8,128)(2,1)S(1)}, u32[]{:S(2)}, u32[]{:S(2)}) collective-permute-start(bf16[128,512]{1,0:T(8,128)(2,1)S(1)} %get-tuple-element.124), channel_id=1, source_target_pairs={{6,0},{12,6},{18,12},{24,18},{30,24},{36,30},{42,36},{48,42},{54,4... | collective-permute-start | bytes 393224 | tf_op jit(solution)/shard_map/ppermute | solution.py:29
  17.7 11.1 %collective-permute-start = (bf16[128,512]{1,0:T(8,128)(2,1)S(1)}, bf16[128,512]{1,0:T(8,128)(2,1)S(1)}, u32[]{:S(2)}, u32[]{:S(2)}) collective-permute-start(bf16[128,512]{1,0:T(8,128)(2,1)S(1)} %get-tuple-element.123), channel_id=1, source_target_pairs={{0,6},{6,12},{12,18},{18,24},{24,30},{30,36},{36,42},{42,48},{48,5... | collective-permute-start | bytes 393224 | tf_op jit(solution)/shard_map/ppermute | solution.py:27
  28.8 0.8 pad_dynamic-slice_fusion.1
  29.6 0.8 compare_select_fusion
  30.4 0.8 fusion.22
  31.7 1.0 squeeze.28
  36.1 1.4 %multiply_reduce_fusion = (f32[2,128]{1,0:T(2,128)S(1)}, f32[2,128,4,128]{1,3,2,0:T(8,128)}) fusion(f32[2,4,384,128]{3,2,1,0:T(8,128)S(1)} %get-tuple-element.130, f32[2,4,128]{2,1,0:T(4,128)S(1)} %fusion.3, f32[2,4,128]{2,1,0:T(4,128)S(1)} %get-tuple-element.129, bf16[2,384,4,128]{3,1,0,2:T(8,128)(2,1)S(1)} %bitcast.106), kind=kOutput, calls=%fused_computation.39 | convolution fusion | flops 102104832 | bytes 2892800 | tf_op jit(solution)/shard_map/while/body/eval_jaxpr/ghqk,gkhe->gqhe/dot_general | solution.py:67
  37.5 1.3 %copy.145 = f32[2,128,4,128]{3,2,1,0:T(4,128)S(1)} copy(f32[2,128,4,128]{1,3,2,0:T(8,128)} %get-tuple-element.132) | data formatting | bytes 1048576 | tf_op jit(solution)/shard_map/while/body/eval_jaxpr/ghqk,gkhe->gqhe/transpose | solution.py:67
  38.9 8.7 %all-reduce.2 = (f32[256]{0:T(256)S(1)}, f32[256]{0:T(256)S(1)}) all-reduce(f32[256]{0:T(256)S(1)} %bitcast.119, f32[256]{0:T(256)S(1)} %fusion.16), channel_id=1, replica_groups=mesh['curve'=128,'dp'=6] {'dp'}, use_global_device_ids=true, to_apply=%region_3.4 | all-reduce | flops 512 | bytes 4096 | tf_op jit(solution)/shard_map/psum | solution.py:157
  47.7 2.0 %bitcast_multiply_fusion = (f32[256,512]{1,0:T(8,128)S(1)}, bf16[256,512]{1,0:T(8,128)(2,1)}, bf16[256,512]{1,0:T(8,128)(2,1)}) fusion(f32[32,8,4,128]{3,2,1,0:T(4,128)S(1)} %bitcast.96, f32[256]{0:T(256)S(1)} %get-tuple-element.133, f32[256]{0:T(256)S(1)} %get-tuple-element.127, f32[256]{0:T(256)S(1)} %get-tuple-element.128, f32[512]{0:T(512)S(1)} %copy-done.12, ...), kind=kLoop, calls=%fused_computation.26 | loop fusion | flops 1572864 | bytes 1840128 | tf_op jit(solution)/shard_map/mul | solution.py:165
  49.6 1.0 squeeze.29
  50.7 0.9 copy.164
  52.2 1.7 %multiply_convert_fusion = bf16[2,4,128,384]{2,3,1,0:T(8,128)(2,1)S(1)} fusion(bf16[2,128,4,128]{1,3,2,0:T(8,128)(2,1)} %copy.164, f32[2,4,384,128]{3,2,1,0:T(8,128)S(1)} %get-tuple-element.130, f32[2,4,128]{2,1,0:T(4,128)S(1)} %bitcast.117, f32[2,4,128]{2,1,0:T(4,128)S(1)} %bitcast.115, bf16[2,384,4,128]{3,1,0,2:T(8,128)(2,1)} %bitcast.107), kind=kOutput, calls=%fused_computation.9 | convolution fusion | flops 102629376 | bytes 3416064 | tf_op jit(solution)/shard_map/while/body/eval_jaxpr/gqhe,gkhe->ghqk/dot_general | solution.py:80
  55.5 1.5 %scatter_fusion = f32[4,128,4,128]{3,1,2,0:T(8,128)S(1)} fusion(f32[4,128,4,128]{3,1,2,0:T(8,128)S(1)} %broadcast_in_dim.79.clone, s32[6]{0:T(128)S(1)} %fusion.23, f32[6,128,4,128]{3,1,2,0:T(8,128)S(1)} %copy.156), kind=kCustom, calls=%fused_computation.2 | custom fusion | flops 393216 | bytes 4718616 | tf_op jit(solution)/shard_map/while/body/eval_jaxpr/scatter-add | solution.py:185
  57.1 0.7 slice.145
  57.8 0.9 convert.8
  59.2 1.6 %copy.166 = f32[2,384,4,128]{3,1,0,2:T(8,128)} copy(f32[2,384,4,128]{1,3,2,0:T(8,128)S(1)} %convolution_bitcast_fusion) | data formatting | bytes 3145728 | tf_op jit(solution)/shard_map/while/body/eval_jaxpr/ghqk,gqhe->gkhe/transpose | solution.py:87
  60.8 1.5 %copy.167 = f32[6,128,4,128]{3,1,2,0:T(8,128)S(1)} copy(f32[6,128,4,128]{3,1,0,2:T(8,128)} %bitcast.94) | data formatting | bytes 3145728 | tf_op jit(solution)/shard_map/while/body/eval_jaxpr/reshape | solution.py:186
  62.5 1.5 %scatter_fusion.1 = f32[4,128,4,128]{3,1,2,0:T(8,128)S(1)} fusion(f32[4,128,4,128]{3,1,2,0:T(8,128)S(1)} %broadcast_in_dim.79.clone.1, s32[6]{0:T(128)S(1)} %fusion.23, f32[6,128,4,128]{3,1,2,0:T(8,128)S(1)} %copy.167), kind=kCustom, calls=%fused_computation.3 | custom fusion | flops 393216 | bytes 4718616 | tf_op jit(solution)/shard_map/while/body/eval_jaxpr/scatter-add | solution.py:186
  65.1 0.7 copy.217
  67.2 14.0 %collective-permute-start.4 = (bf16[128,512]{1,0:T(8,128)(2,1)S(1)}, bf16[128,512]{1,0:T(8,128)(2,1)S(1)}, u32[]{:S(2)}, u32[]{:S(2)}) collective-permute-start(bf16[128,512]{1,0:T(8,128)(2,1)S(1)} %copy.160), channel_id=1, source_target_pairs={{0,6},{6,12},{12,18},{18,24},{24,30},{30,36},{36,42},{42,48},{48,5... | collective-permute-start | bytes 393224 | tf_op jit(solution)/shard_map/ppermute | solution.py:39
  81.5 1.9 %collective-permute-start.5 = (bf16[128,512]{1,0:T(8,128)(2,1)S(1)}, bf16[128,512]{1,0:T(8,128)(2,1)S(1)}, u32[]{:S(2)}, u32[]{:S(2)}) collective-permute-start(bf16[128,512]{1,0:T(8,128)(2,1)S(1)} %copy.163), channel_id=1, source_target_pairs={{6,0},{12,6},{18,12},{24,18},{30,24},{36,30},{42,36},{48,42},{54,4... | collective-permute-start | bytes 393224 | tf_op jit(solution)/shard_map/ppermute | solution.py:39
  84.4 11.1 %collective-permute-start.6 = (bf16[128,512]{1,0:T(8,128)(2,1)S(1)}, bf16[128,512]{1,0:T(8,128)(2,1)S(1)}, u32[]{:S(2)}, u32[]{:S(2)}) collective-permute-start(bf16[128,512]{1,0:T(8,128)(2,1)S(1)} %copy.171), channel_id=1, source_target_pairs={{0,6},{6,12},{12,18},{18,24},{24,30},{30,36},{36,42},{42,48},{48,5... | collective-permute-start | bytes 393224 | tf_op jit(solution)/shard_map/ppermute | solution.py:39
  95.8 1.9 %collective-permute-start.7 = (bf16[128,512]{1,0:T(8,128)(2,1)S(1)}, bf16[128,512]{1,0:T(8,128)(2,1)S(1)}, u32[]{:S(2)}, u32[]{:S(2)}) collective-permute-start(bf16[128,512]{1,0:T(8,128)(2,1)S(1)} %copy.174), channel_id=1, source_target_pairs={{6,0},{12,6},{18,12},{24,18},{30,24},{36,30},{42,36},{48,42},{54,4... | collective-permute-start | bytes 393224 | tf_op jit(solution)/shard_map/ppermute | solution.py:39
  97.8 0.7 convert_element_type.77
  98.6 3.1 %collective-permute-done.6 = bf16[128,512]{1,0:T(8,128)(2,1)S(1)} collective-permute-done((bf16[128,512]{1,0:T(8,128)(2,1)S(1)}, bf16[128,512]{1,0:T(8,128)(2,1)S(1)}, u32[]{:S(2)}, u32[]{:S(2)}) %collective-permute-start.6) | collective-permute-done | bytes 131104 | tf_op jit(solution)/shard_map/ppermute | solution.py:39
  101.7 12.7 %collective-permute-done.7 = bf16[128,512]{1,0:T(8,128)(2,1)S(1)} collective-permute-done((bf16[128,512]{1,0:T(8,128)(2,1)S(1)}, bf16[128,512]{1,0:T(8,128)(2,1)S(1)}, u32[]{:S(2)}, u32[]{:S(2)}) %collective-permute-start.7) | collective-permute-done | bytes 131104 | tf_op jit(solution)/shard_map/ppermute | solution.py:39
  114.4 0.7 convert_element_type.83
  (93 shorter events, 10.8 us)
Async XLA Ops:
  0.6 32.1 %copy-start.8 = (bf16[256,512]{1,0:T(8,128)(2,1)S(1)}, bf16[256,512]{1,0:T(8,128)(2,1)}, u32[]{:S(2)}) copy-start(bf16[256,512]{1,0:T(8,128)(2,1)} %param.16) | copy-start | bytes 786436
  1.7 31.1 %collective-permute-start.3 = (bf16[128,512]{1,0:T(8,128)(2,1)S(1)}, bf16[128,512]{1,0:T(8,128)(2,1)S(1)}, u32[]{:S(2)}, u32[]{:S(2)}) collective-permute-start(bf16[128,512]{1,0:T(8,128)(2,1)S(1)} %get-tuple-element.126), channel_id=1, source_target_pairs={{6,0},{12,6},{18,12},{24,18},{30,24},{36,30},{42,36},{48,42},{54,4... | collective-permute-start | bytes 393224 | tf_op jit(solution)/shard_map/ppermute | solution.py:29
  4.4 28.3 %collective-permute-start.2 = (bf16[128,512]{1,0:T(8,128)(2,1)S(1)}, bf16[128,512]{1,0:T(8,128)(2,1)S(1)}, u32[]{:S(2)}, u32[]{:S(2)}) collective-permute-start(bf16[128,512]{1,0:T(8,128)(2,1)S(1)} %get-tuple-element.125), channel_id=1, source_target_pairs={{0,6},{6,12},{12,18},{18,24},{24,30},{30,36},{36,42},{42,48},{48,5... | collective-permute-start | bytes 393224 | tf_op jit(solution)/shard_map/ppermute | solution.py:27
  15.8 18.1 %collective-permute-start.1 = (bf16[128,512]{1,0:T(8,128)(2,1)S(1)}, bf16[128,512]{1,0:T(8,128)(2,1)S(1)}, u32[]{:S(2)}, u32[]{:S(2)}) collective-permute-start(bf16[128,512]{1,0:T(8,128)(2,1)S(1)} %get-tuple-element.124), channel_id=1, source_target_pairs={{6,0},{12,6},{18,12},{24,18},{30,24},{36,30},{42,36},{48,42},{54,4... | collective-permute-start | bytes 393224 | tf_op jit(solution)/shard_map/ppermute | solution.py:29
  17.7 16.5 %collective-permute-start = (bf16[128,512]{1,0:T(8,128)(2,1)S(1)}, bf16[128,512]{1,0:T(8,128)(2,1)S(1)}, u32[]{:S(2)}, u32[]{:S(2)}) collective-permute-start(bf16[128,512]{1,0:T(8,128)(2,1)S(1)} %get-tuple-element.123), channel_id=1, source_target_pairs={{0,6},{6,12},{12,18},{18,24},{24,30},{30,36},{36,42},{42,48},{48,5... | collective-permute-start | bytes 393224 | tf_op jit(solution)/shard_map/ppermute | solution.py:27
  32.7 2.5 %copy-start.4 = (bf16[2,128,4,128]{3,2,1,0:T(4,128)(2,1)}, bf16[2,128,4,128]{3,2,1,0:T(4,128)(2,1)S(1)}, u32[]{:S(2)}) copy-start(bf16[2,128,4,128]{3,2,1,0:T(4,128)(2,1)S(1)} %squeeze.28) | copy-start | bytes 786436
  33.1 1.1 copy-start.9
  35.2 0.9 copy-start.11
  35.7 16.5 %copy-start = (f32[2,4,384,128]{3,2,1,0:T(8,128)}, f32[2,4,384,128]{3,2,1,0:T(8,128)S(1)}, u32[]{:S(2)}) copy-start(f32[2,4,384,128]{3,2,1,0:T(8,128)S(1)} %get-tuple-element.130) | copy-start | bytes 4718596
  36.1 2.6 %copy-start.3 = (bf16[256,512]{1,0:T(8,128)(2,1)S(1)}, bf16[256,512]{1,0:T(8,128)(2,1)}, u32[]{:S(2)}) copy-start(bf16[256,512]{1,0:T(8,128)(2,1)} %param.18) | copy-start | bytes 786436
  36.1 2.6 %copy-start.12 = (f32[512]{0:T(512)S(1)}, f32[512]{0:T(512)}, u32[]{:S(2)}) copy-start(f32[512]{0:T(512)} %param.19) | copy-start | bytes 6148
  53.8 1.0 copy-start.5
  57.1 1.7 %copy-start.1 = (f32[2,4,384,128]{3,2,1,0:T(8,128)S(1)}, f32[2,4,384,128]{3,2,1,0:T(8,128)}, u32[]{:S(2)}) copy-start(f32[2,4,384,128]{3,2,1,0:T(8,128)} %copy-done) | copy-start | bytes 4718596
  57.1 1.7 %copy-start.10 = (bf16[2,128,4,128]{1,3,2,0:T(8,128)(2,1)S(1)}, bf16[2,128,4,128]{1,3,2,0:T(8,128)(2,1)}, u32[]{:S(2)}) copy-start(bf16[2,128,4,128]{1,3,2,0:T(8,128)(2,1)} %copy.164) | copy-start | bytes 786436
  65.1 1.1 copy-start.7
  65.8 1.1 copy-start.2
  66.9 16.9 %copy-start.6 = (f32[1,128,4,128]{3,1,2,0:T(8,128)S(1)}, f32[1,128,4,128]{3,1,2,0:T(8,128)}, u32[]{:S(2)}) copy-start(f32[1,128,4,128]{3,1,2,0:T(8,128)} %slice.150) | copy-start | bytes 786436
  67.2 30.5 %collective-permute-start.4 = (bf16[128,512]{1,0:T(8,128)(2,1)S(1)}, bf16[128,512]{1,0:T(8,128)(2,1)S(1)}, u32[]{:S(2)}, u32[]{:S(2)}) collective-permute-start(bf16[128,512]{1,0:T(8,128)(2,1)S(1)} %copy.160), channel_id=1, source_target_pairs={{0,6},{6,12},{12,18},{18,24},{24,30},{30,36},{36,42},{42,48},{48,5... | collective-permute-start | bytes 393224 | tf_op jit(solution)/shard_map/ppermute | solution.py:39
  81.5 16.3 %collective-permute-start.5 = (bf16[128,512]{1,0:T(8,128)(2,1)S(1)}, bf16[128,512]{1,0:T(8,128)(2,1)S(1)}, u32[]{:S(2)}, u32[]{:S(2)}) collective-permute-start(bf16[128,512]{1,0:T(8,128)(2,1)S(1)} %copy.163), channel_id=1, source_target_pairs={{6,0},{12,6},{18,12},{24,18},{30,24},{36,30},{42,36},{48,42},{54,4... | collective-permute-start | bytes 393224 | tf_op jit(solution)/shard_map/ppermute | solution.py:39
  84.4 17.3 %collective-permute-start.6 = (bf16[128,512]{1,0:T(8,128)(2,1)S(1)}, bf16[128,512]{1,0:T(8,128)(2,1)S(1)}, u32[]{:S(2)}, u32[]{:S(2)}) collective-permute-start(bf16[128,512]{1,0:T(8,128)(2,1)S(1)} %copy.171), channel_id=1, source_target_pairs={{0,6},{6,12},{12,18},{18,24},{24,30},{30,36},{36,42},{42,48},{48,5... | collective-permute-start | bytes 393224 | tf_op jit(solution)/shard_map/ppermute | solution.py:39
  95.8 18.6 %collective-permute-start.7 = (bf16[128,512]{1,0:T(8,128)(2,1)S(1)}, bf16[128,512]{1,0:T(8,128)(2,1)S(1)}, u32[]{:S(2)}, u32[]{:S(2)}) collective-permute-start(bf16[128,512]{1,0:T(8,128)(2,1)S(1)} %copy.174), channel_id=1, source_target_pairs={{6,0},{12,6},{18,12},{24,18},{30,24},{36,30},{42,36},{48,42},{54,4... | collective-permute-start | bytes 393224 | tf_op jit(solution)/shard_map/ppermute | solution.py:39
where the time goes:
time: 116 us; the launch traced here: 115 us
  starting transfers between devices  55.2 us (48%)
  local copies, waits for them, and re-layouts  19.2 us (17%)
  waiting for transfers between devices  16.1 us (14%)
  other arithmetic  10 us (9%)
  blocking collectives  8.73 us (8%)
  matrix products  4.7 us (4%)
  between operations  1.25 us (1%)
    ppermute x4, starting transfers between devices, passed_along(): return lax.ppermute(x, axis, pairs)  29 us
    ppermute x2, starting transfers between devices, with_halo(): lax.ppermute(tail, axis, [(i, (i + 1) % count) for i in range(ends)])  21.5 us
    ppermute x4, waiting for transfers between devices, passed_along(): return lax.ppermute(x, axis, pairs)  15.8 us
    psum x1, blocking collectives, shards(): square_total = lax.psum(squares, 'dp')  8.73 us
    ppermute x2, starting transfers between devices, with_halo(): lax.ppermute(head, axis, [((i + 1) % count, i) for i in range(ends)])  4.66 us
    squeeze x3, local copies, waits for them, and re-layouts, shards(): lax.map(forward_step, (to_groups(queries, heads_dev), own_idx.reshape(gro...  2.9 us
  transfers between devices with their start and end apart: 8, of which 3 were waited for; matrix products, arithmetic and copies ran while one was open for 7% of the time, Pallas kernels for 0%

commit v1 on v0

v1 whole, which is shorter than its diff:
```python
import functools
import math

import jax
import jax.numpy as jnp
from jax import lax
from jax.experimental import pallas as pl
from jax.experimental.pallas import tpu as pltpu
from jax.sharding import PartitionSpec as P

FEAT = 3072
HD = 128
BLK = 128
NBR = 3
BLOCKS = 256
EPS = 1e-06
SCALE = 1.0 / math.sqrt(HD)
NEG = -1e30
F32 = jnp.float32
BF16 = jnp.bfloat16


def mm(a, b):
    return lax.dot_general(a, b, (((1,), (0,)), ((), ())), preferred_element_type=F32)


def mm_t(a, b):
    return lax.dot_general(a, b, (((1,), (1,)), ((), ())), preferred_element_type=F32)


def t_mm(a, b):
    return lax.dot_general(a, b, (((0,), (0,)), ((), ())), preferred_element_type=F32)


def sees(ids_ref, cnt_ref, a, b):
    inside = jnp.logical_and(a >= 0, a < BLOCKS)
    row = jnp.clip(a, 0, BLOCKS - 1)
    hit = jnp.bool_(False)
    for j in range(NBR):
        hit = jnp.logical_or(hit, jnp.logical_and(j < cnt_ref[row], ids_ref[row, j] == b))
    return jnp.where(jnp.logical_and(hit, inside), F32(0.0), F32(NEG))


def own_bias(ids_ref, cnt_ref, first):
    up = sees(ids_ref, cnt_ref, first, first + 1)
    down = sees(ids_ref, cnt_ref, first + 1, first)
    row = lax.broadcasted_iota(jnp.int32, (2 * BLK, 2 * BLK), 0) >= BLK
    col = lax.broadcasted_iota(jnp.int32, (2 * BLK, 2 * BLK), 1) >= BLK
    off = jnp.where(row, down, up)
    return jnp.where(row == col, F32(0.0), off)


def side_of(index, side):
    even = 1 - lax.rem(index, 2)
    edge = even if side == 0 else 1 - even
    return edge, 2 * edge - 1


def head_cols(h, base=0):
    return slice(base + h * HD, base + (h + 1) * HD)


def own_kernel(heads, ids_ref, cnt_ref, q_ref, k_ref, v_ref, c_ref, send0_ref, send1_ref, o_ref, lse_ref):
    index = lax.axis_index("curve")
    feat = heads * HD
    bias = own_bias(ids_ref, cnt_ref, 2 * index)
    lane = lax.broadcasted_iota(jnp.int32, (2 * BLK, 128), 1)
    stats = jnp.zeros((2 * BLK, 128), F32)
    for h in range(heads):
        hs = head_cols(h)
        s = mm_t(q_ref[:, hs], k_ref[:, hs]) * SCALE + bias
        top = jnp.max(s, axis=1, keepdims=True)
        p = jnp.exp(s - top)
        total = jnp.sum(p, axis=1, keepdims=True)
        o_ref[:, hs] = mm(p.astype(BF16), v_ref[:, hs]) / total
        stats = jnp.where(lax.rem(lane, heads) == h, top + jnp.log(total), stats)
    lse_ref[...] = stats
    hi = stats.astype(BF16).astype(F32)
    mid = (stats - hi).astype(BF16).astype(F32)
    low = stats - hi - mid
    parts = jnp.where(lane < heads, hi, jnp.where(lane < 2 * heads, mid, low))
    parts = jnp.where(lane < 3 * heads, parts, 0.0)
    stat_rows = parts.astype(BF16)
    lse_rows = (stat_rows[:BLK], stat_rows[BLK:])
    for side, send in enumerate((send0_ref, send1_ref)):
        edge, _ = side_of(index, side)
        rows = pl.ds(pl.multiple_of(edge * BLK, BLK), BLK)
        for n, ref in enumerate((k_ref, v_ref, q_ref, c_ref)):
            send[:, n * feat : (n + 1) * feat] = ref[rows, :]
        send[:, 4 * feat : 5 * feat] = o_ref[rows, :].astype(BF16)
        send[:, 5 * feat :] = jnp.where(edge == 1, lse_rows[1].astype(F32), lse_rows[0].astype(F32)).astype(BF16)


def merge(s, lse_part, o_part, values):
    top = jnp.maximum(jnp.max(s, axis=1, keepdims=True), lse_part)
    p = jnp.exp(s - top)
    rest = jnp.exp(lse_part - top)
    total = jnp.sum(p, axis=1, keepdims=True) + rest
    out = (mm(p.astype(BF16), values) + rest * o_part) / total
    return out, top + jnp.log(total)


def side_bias(ids_ref, cnt_ref, index, edge, step):
    block = 2 * index + edge
    return sees(ids_ref, cnt_ref, block, block + step), sees(ids_ref, cnt_ref, block + step, block)


def join_kernel(
    heads, ids_ref, cnt_ref, q_ref, k_ref, v_ref, c_ref, gain_ref, o_ref, lse_in_ref, recv0_ref, recv1_ref,
    a_ref, lse_ref, sums_ref,
):
    index = lax.axis_index("curve")
    feat = heads * HD
    lane = lax.broadcasted_iota(jnp.int32, (BLK, 128), 1)
    gain = gain_ref[...]
    for side, recv in enumerate((recv0_ref, recv1_ref)):
        edge, step = side_of(index, side)
        rows = pl.ds(pl.multiple_of(edge * BLK, BLK), BLK)
        out_bias, in_bias = side_bias(ids_ref, cnt_ref, index, edge, step)
        lse_own = lse_in_ref[rows, :]
        far = recv[:, 5 * feat :].astype(F32)
        far_rows = slice((2 + side) * BLK, (3 + side) * BLK)
        own_stats = jnp.zeros((BLK, 128), F32)
        far_stats = jnp.zeros((BLK, 128), F32)
        sq_own = jnp.zeros((BLK, HD), F32)
        cr_own = jnp.zeros((BLK, HD), F32)
        sq_far = jnp.zeros((BLK, HD), F32)
        cr_far = jnp.zeros((BLK, HD), F32)
        for h in range(heads):
            hs = head_cols(h)
            g = gain[:, hs]
            s = mm_t(q_ref[rows, hs], recv[:, head_cols(h)]) * SCALE + out_bias
            a, lse = merge(s, lse_own[:, h : h + 1], o_ref[rows, hs], recv[:, head_cols(h, feat)])
            a_ref[rows, hs] = a
            own_stats = jnp.where(lane == h, lse, own_stats)
            sq_own += a * a
            cr_own += c_ref[rows, hs].astype(F32) * g * a
            s = mm_t(recv[:, head_cols(h, 2 * feat)], k_ref[rows, hs]) * SCALE + in_bias
            far_lse = far[:, h : h + 1] + far[:, heads + h : heads + h + 1] + far[:, 2 * heads + h : 2 * heads + h + 1]
            a, lse = merge(s, far_lse, recv[:, head_cols(h, 4 * feat)].astype(F32), v_ref[rows, hs])
            a_ref[far_rows, hs] = a
            far_stats = jnp.where(lane == h, lse, far_stats)
            sq_far += a * a
            cr_far += recv[:, head_cols(h, 3 * feat)].astype(F32) * g * a
        lse_ref[rows, :] = own_stats
        lse_ref[far_rows, :] = far_stats
        for row, squares, crosses in ((edge, sq_own, cr_own), (2 + side, sq_far, cr_far)):
            both = jnp.where(
                lane == 0,
                jnp.sum(squares, axis=1, keepdims=True),
                jnp.sum(crosses, axis=1, keepdims=True),
            ).T
            for j in range(sums_ref.shape[0]):
                sums_ref[j, pl.ds(row, 1), :] = both[0:1]
                sums_ref[j, pl.ds(4 + row, 1), :] = both[1:2]


def grad_kernel(
    heads, ids_ref, cnt_ref, q_ref, k_ref, v_ref, c_ref, gain_ref, a_ref, lse_ref, recv0_ref, recv1_ref, sums_ref,
    normed_ref, gq_out, gk_out, gv_out, gq_ref, gk_ref, gv_ref, d_ref,
):
    index = lax.axis_index("curve")
    feat = heads * HD
    gain = gain_ref[...]
    total = jnp.sum(sums_ref[...], axis=0) / FEAT
    rinv = lax.rsqrt(total[0:4] + EPS)
    turn = rinv * rinv * rinv * total[4:8]
    columns = jnp.concatenate([rinv, turn, jnp.zeros((BLK - 8, 128), F32)], axis=0).T
    deltas = []
    for b in range(4):
        rows = slice(b * BLK, (b + 1) * BLK)
        a = a_ref[rows, :]
        r, t = columns[:, b : b + 1], columns[:, 4 + b : 5 + b]
        if b < 2:
            normed_ref[rows, :] = (gain * a * r).astype(BF16)
            cot = c_ref[rows, :]
        else:
            cot = (recv0_ref, recv1_ref)[b - 2][:, 3 * feat : 4 * feat]
        d = (cot.astype(F32) * gain * r - a * t).astype(BF16)
        d_ref[rows, :] = d
        both = d.astype(F32) * a
        deltas.append([jnp.sum(both[:, head_cols(h)], axis=1, keepdims=True) for h in range(heads)])
    bias = own_bias(ids_ref, cnt_ref, 2 * index)
    own = slice(0, 2 * BLK)
    for h in range(heads):
        hs = head_cols(h)
        q, k, v, d = q_ref[:, hs], k_ref[:, hs], v_ref[:, hs], d_ref[own, hs]
        delta = jnp.concatenate([deltas[0][h], deltas[1][h]], axis=0)
        p = jnp.exp(mm_t(q, k) * SCALE + bias - lse_ref[own, h : h + 1])
        ds = (p * (mm_t(d, v) - delta) * SCALE).astype(BF16)
        gq_ref[:, hs] = mm(ds, k)
        gk_ref[:, hs] = t_mm(ds, q)
        gv_ref[:, hs] = t_mm(p.astype(BF16), d)
    for side, recv in enumerate((recv0_ref, recv1_ref)):
        edge, step = side_of(index, side)
        rows = pl.ds(pl.multiple_of(edge * BLK, BLK), BLK)
        far_rows = slice((2 + side) * BLK, (3 + side) * BLK)
        out_bias, in_bias = side_bias(ids_ref, cnt_ref, index, edge, step)
        for h in range(heads):
            hs = head_cols(h)
            far_k, far_v, far_q = (recv[:, head_cols(h, n * feat)] for n in range(3))
            d = d_ref[rows, hs]
            delta = jnp.where(edge == 1, deltas[1][h], deltas[0][h])
            p = jnp.exp(mm_t(q_ref[rows, hs], far_k) * SCALE + out_bias - lse_ref[rows, h : h + 1])
            ds = (p * (mm_t(d, far_v) - delta) * SCALE).astype(BF16)
            gq_out[rows, hs] = (gq_ref[rows, hs] + mm(ds, far_k)).astype(BF16)
            d = d_ref[far_rows, hs]
            p = jnp.exp(mm_t(far_q, k_ref[rows, hs]) * SCALE + in_bias - lse_ref[far_rows, h : h + 1])
            ds = (p * (mm_t(d, v_ref[rows, hs]) - deltas[2 + side][h]) * SCALE).astype(BF16)
            gk_out[rows, hs] = (gk_ref[rows, hs] + t_mm(ds, far_q)).astype(BF16)
            gv_out[rows, hs] = (gv_ref[rows, hs] + t_mm(p.astype(BF16), d)).astype(BF16)


SMEM = pl.BlockSpec(memory_space=pltpu.SMEM)
VMEM = pl.BlockSpec(memory_space=pltpu.VMEM)
PARAMS = pltpu.CompilerParams(vmem_limit_bytes=32 * 1024 * 1024)


def call(kernel, name, n_vmem, outs, scratch=()):
    return pl.pallas_call(
        kernel,
        name=name,
        out_shape=outs,
        in_specs=[SMEM, SMEM] + [VMEM] * n_vmem,
        out_specs=tuple(VMEM for _ in outs),
        scratch_shapes=list(scratch),
        compiler_params=PARAMS,
    )


def shards(queries, keys, values, cotangent, gain, neighbour_ids, neighbour_counts):
    rows, feat = queries.shape
    heads = feat // HD
    count = lax.axis_size("curve")
    peers = lax.axis_size("dp")
    width = 5 * feat + 128
    shape = jax.ShapeDtypeStruct
    lists = (neighbour_ids, neighbour_counts)
    gain = gain.reshape(1, feat)
    send0, send1, o_own, lse_own = call(
        functools.partial(own_kernel, heads), "own", 4,
        (shape((BLK, width), BF16), shape((BLK, width), BF16), shape((rows, feat), F32), shape((rows, 128), F32)),
    )(*lists, queries, keys, values, cotangent)
    odd = [(i, i + 1) for i in range(1, count - 1, 2)]
    even = [(i, i + 1) for i in range(0, count, 2)]
    recv1 = lax.ppermute(send1, "curve", odd + [(b, a) for a, b in odd])
    recv0 = lax.ppermute(send0, "curve", even + [(b, a) for a, b in even])
    attended, lse, sums = call(
        functools.partial(join_kernel, heads), "join", 9,
        (shape((2 * rows, feat), F32), shape((2 * rows, 128), F32), shape((peers, 8, 128), F32)),
    )(*lists, queries, keys, values, cotangent, gain, o_own, lse_own, recv0, recv1)
    sums = lax.all_to_all(sums, "dp", 0, 0, tiled=True)
    return call(
        functools.partial(grad_kernel, heads), "grads", 10,
        tuple(shape((rows, feat), BF16) for _ in range(4)),
        [pltpu.VMEM((rows, feat), F32)] * 3 + [pltpu.VMEM((2 * rows, feat), BF16)],
    )(*lists, queries, keys, values, cotangent, gain, attended, lse, recv0, recv1, sums)


def solution(mesh):
    wide = P("curve", "dp")
    return jax.shard_map(
        shards,
        mesh=mesh,
        in_specs=(wide, wide, wide, wide, P("dp"), P(), P()),
        out_specs=(wide, wide, wide, wide),
        check_vma=False,
    )
```

time: 116 us -> 95 us (0.82)
  the two profiles are of different devices: /device:TPU:382 before, /device:TPU:192 now
where the time goes in v1:
time: 95 us; the launch traced here: 94.7 us
  waiting for transfers between devices  43.9 us (46%)
  Pallas kernels  20.1 us (21%)
  blocking collectives  17.1 us (18%)
  starting transfers between devices  7.58 us (8%)
  local copies, waits for them, and re-layouts  5.3 us (6%)
    ppermute x1, waiting for transfers between devices, shards(): recv1 = lax.ppermute(send1, 'curve', odd + [(b, a) for a, b in odd])  32.4 us
    all_to_all x1, blocking collectives, shards(): sums = lax.all_to_all(sums, 'dp', 0, 0, tiled=True)  17.1 us
    ppermute x1, waiting for transfers between devices, shards(): recv0 = lax.ppermute(send0, 'curve', even + [(b, a) for a, b in even])  11.5 us
    pallas_call x1, Pallas kernels, shards(): call(functools.partial(grad_kernel, heads), 'grads', 10, tuple((shape((ro...  8.35 us
    pallas_call x1, Pallas kernels, shards(): call(functools.partial(join_kernel, heads), 'join', 9, (shape((2 * rows,...  8.13 us
    unnamed x13, local copies, waits for them, and re-layouts  5.3 us
    ppermute x1, starting transfers between devices, shards(): recv1 = lax.ppermute(send1, 'curve', odd + [(b, a) for a, b in odd])  4.18 us
    pallas_call x1, Pallas kernels, shards(): call(functools.partial(own_kernel, heads), 'own', 4, (shape((BLK, width),...  3.68 us
  transfers between devices with their start and end apart: 2, of which 2 were waited for; matrix products, arithmetic and copies ran while one was open for 0% of the time, Pallas kernels for 0%

profile of v1, /device:TPU:192, one launch (start us, length us, event | category | flops | bytes accessed | tf_op | source)
XLA Modules:
  0.0 94.7 jit_solution(2167826003055799815)
XLA Ops:
  0.6 0.0 copy-start.4
  0.6 0.8 copy.13.ids_ref
  1.5 0.0 copy-done.4
  1.5 0.0 copy-start
  1.5 0.9 copy-done
  2.4 0.0 copy-start.1
  2.4 0.9 %copy-done.1 = bf16[256,512]{1,0:T(8,128)(2,1)S(1)} copy-done((bf16[256,512]{1,0:T(8,128)(2,1)S(1)}, bf16[256,512]{1,0:T(8,128)(2,1)}, u32[]{:S(2)}) %copy-start.1) | copy-done | bytes 262168
  3.4 0.0 copy-start.2
  3.4 0.9 %copy-done.2 = bf16[256,512]{1,0:T(8,128)(2,1)S(1)} copy-done((bf16[256,512]{1,0:T(8,128)(2,1)S(1)}, bf16[256,512]{1,0:T(8,128)(2,1)}, u32[]{:S(2)}) %copy-start.2) | copy-done | bytes 262168
  4.3 0.0 copy-start.3
  4.3 0.9 %copy-done.3 = bf16[256,512]{1,0:T(8,128)(2,1)S(1)} copy-done((bf16[256,512]{1,0:T(8,128)(2,1)S(1)}, bf16[256,512]{1,0:T(8,128)(2,1)}, u32[]{:S(2)}) %copy-start.3) | copy-done | bytes 262168
  5.3 3.7 %own.1 = (bf16[128,2688]{1,0:T(8,128)(2,1)S(1)}, bf16[128,2688]{1,0:T(8,128)(2,1)S(1)}, f32[256,512]{1,0:T(8,128)S(1)}, f32[256,128]{1,0:T(8,128)S(1)}) custom-call(s32[256,3]{1,0:T(8,128)S(1)} %copy.13.ids_ref, s32[256]{0:T(256)S(1)} %copy-done.4, bf16[256,512]{1,0:T(8,128)(2,1)S(1)} %copy-done, bf16[256,512]{1,0:T(8,128)(2,1)S(1)} %copy-done.1, ...), custom_call_target="tpu_custom_call" | custom-call | tf_op jit(solution)/shard_map/own/pallas_call | solution.py:240
  9.0 3.4 %collective-permute-start = (bf16[128,2688]{1,0:T(8,128)(2,1)S(1)}, bf16[128,2688]{1,0:T(8,128)(2,1)S(1)}, u32[]{:S(2)}, u32[]{:S(2)}) collective-permute-start(bf16[128,2688]{1,0:T(8,128)(2,1)S(1)} %get-tuple-element.13), channel_id=1, source_target_pairs={{0,6},{12,18},{24,30},{36,42},{48,54},{60,66},{72,78},{84,90},{96,... | collective-permute-start | bytes 2064392 | tf_op jit(solution)/shard_map/ppermute | solution.py:247
  12.4 4.2 %collective-permute-start.1 = (bf16[128,2688]{1,0:T(8,128)(2,1)S(1)}, bf16[128,2688]{1,0:T(8,128)(2,1)S(1)}, u32[]{:S(2)}, u32[]{:S(2)}) collective-permute-start(bf16[128,2688]{1,0:T(8,128)(2,1)S(1)} %get-tuple-element.14), channel_id=1, source_target_pairs={{6,12},{18,24},{30,36},{42,48},{54,60},{66,72},{78,84},{90,96},{10... | collective-permute-start | bytes 2064392 | tf_op jit(solution)/shard_map/ppermute | solution.py:246
  16.6 11.5 %collective-permute-done.recv0_ref = bf16[128,2688]{1,0:T(8,128)(2,1)S(1)} collective-permute-done((bf16[128,2688]{1,0:T(8,128)(2,1)S(1)}, bf16[128,2688]{1,0:T(8,128)(2,1)S(1)}, u32[]{:S(2)}, u32[]{:S(2)}) %collective-permute-start) | collective-permute-done | bytes 688160 | tf_op jit(solution)/shard_map/ppermute | solution.py:247
  28.0 32.4 %collective-permute-done.1.recv1_ref = bf16[128,2688]{1,0:T(8,128)(2,1)S(1)} collective-permute-done((bf16[128,2688]{1,0:T(8,128)(2,1)S(1)}, bf16[128,2688]{1,0:T(8,128)(2,1)S(1)}, u32[]{:S(2)}, u32[]{:S(2)}) %collective-permute-start.1) | collective-permute-done | bytes 688160 | tf_op jit(solution)/shard_map/ppermute | solution.py:246
  60.4 0.0 copy-start.5
  60.4 0.7 copy-done.5
  61.1 8.1 %join.1 = (f32[512,512]{1,0:T(8,128)S(1)}, f32[512,128]{1,0:T(8,128)S(1)}, f32[6,8,128]{2,1,0:T(8,128)S(1)}) custom-call(s32[256,3]{1,0:T(8,128)S(1)} %copy.13.ids_ref, s32[256]{0:T(256)S(1)} %copy-done.4, bf16[256,512]{1,0:T(8,128)(2,1)S(1)} %copy-done, bf16[256,512]{1,0:T(8,128)(2,1)S(1)} %copy-done.1, bf16[256,512]{1,0:T(8,128)(2,1)S(1)} %copy-done.2, ...), custom_call_target="tpu_custom_call" | custom-call | tf_op jit(solution)/shard_map/join/pallas_call | solution.py:248
  69.3 17.1 %all_to_all.5.sums_ref = f32[6,8,128]{2,1,0:T(8,128)S(1)} all-to-all(f32[6,8,128]{2,1,0:T(8,128)S(1)} %get-tuple-element.17), channel_id=1, replica_groups=mesh['curve'=128,'dp'=6] {'dp'}, dimensions={0} | all-to-all | bytes 49152 | tf_op jit(solution)/shard_map/all_to_all | solution.py:252
  86.3 8.3 %grads.1 = (bf16[256,512]{1,0:T(8,128)(2,1)}, bf16[256,512]{1,0:T(8,128)(2,1)}, bf16[256,512]{1,0:T(8,128)(2,1)}, bf16[256,512]{1,0:T(8,128)(2,1)}) custom-call(s32[256,3]{1,0:T(8,128)S(1)} %copy.13.ids_ref, s32[256]{0:T(256)S(1)} %copy-done.4, bf16[256,512]{1,0:T(8,128)(2,1)S(1)} %copy-done, bf16[256,512]{1,0:T(8,128)(2,1)S(1)} %copy-done.1, ...), custom_call_target="tpu_custom_call" | custom-call | tf_op jit(solution)/shard_map/grads/pallas_call | solution.py:253
Async XLA Ops:
  0.6 0.8 copy-start.4
  1.5 1.0 %copy-start = (bf16[256,512]{1,0:T(8,128)(2,1)S(1)}, bf16[256,512]{1,0:T(8,128)(2,1)}, u32[]{:S(2)}) copy-start(bf16[256,512]{1,0:T(8,128)(2,1)} %q_ref.5) | copy-start | bytes 786436
  2.4 0.9 %copy-start.1 = (bf16[256,512]{1,0:T(8,128)(2,1)S(1)}, bf16[256,512]{1,0:T(8,128)(2,1)}, u32[]{:S(2)}) copy-start(bf16[256,512]{1,0:T(8,128)(2,1)} %k_ref.5) | copy-start | bytes 786436
  3.4 0.9 %copy-start.2 = (bf16[256,512]{1,0:T(8,128)(2,1)S(1)}, bf16[256,512]{1,0:T(8,128)(2,1)}, u32[]{:S(2)}) copy-start(bf16[256,512]{1,0:T(8,128)(2,1)} %v_ref.5) | copy-start | bytes 786436
  4.3 0.9 %copy-start.3 = (bf16[256,512]{1,0:T(8,128)(2,1)S(1)}, bf16[256,512]{1,0:T(8,128)(2,1)}, u32[]{:S(2)}) copy-start(bf16[256,512]{1,0:T(8,128)(2,1)} %c_ref.5) | copy-start | bytes 786436
  9.0 19.1 %collective-permute-start = (bf16[128,2688]{1,0:T(8,128)(2,1)S(1)}, bf16[128,2688]{1,0:T(8,128)(2,1)S(1)}, u32[]{:S(2)}, u32[]{:S(2)}) collective-permute-start(bf16[128,2688]{1,0:T(8,128)(2,1)S(1)} %get-tuple-element.13), channel_id=1, source_target_pairs={{0,6},{12,18},{24,30},{36,42},{48,54},{60,66},{72,78},{84,90},{96,... | collective-permute-start | bytes 2064392 | tf_op jit(solution)/shard_map/ppermute | solution.py:247
  12.4 48.1 %collective-permute-start.1 = (bf16[128,2688]{1,0:T(8,128)(2,1)S(1)}, bf16[128,2688]{1,0:T(8,128)(2,1)S(1)}, u32[]{:S(2)}, u32[]{:S(2)}) collective-permute-start(bf16[128,2688]{1,0:T(8,128)(2,1)S(1)} %get-tuple-element.14), channel_id=1, source_target_pairs={{6,12},{18,24},{30,36},{42,48},{54,60},{66,72},{78,84},{90,96},{10... | collective-permute-start | bytes 2064392 | tf_op jit(solution)/shard_map/ppermute | solution.py:246
  60.4 0.7 copy-start.5

commit v2 on v1

v2 whole, which is shorter than its diff:
```python
import functools
import math

import jax
import jax.numpy as jnp
from jax import lax
from jax.experimental import pallas as pl
from jax.experimental.pallas import tpu as pltpu
from jax.sharding import PartitionSpec as P

FEAT = 3072
HD = 128
BLK = 128
NBR = 3
BLOCKS = 256
EPS = 1e-06
SCALE = 1.0 / math.sqrt(HD)
NEG = -1e30
F32 = jnp.float32
BF16 = jnp.bfloat16


def mm(a, b):
    return lax.dot_general(a, b, (((1,), (0,)), ((), ())), preferred_element_type=F32)


def mm_t(a, b):
    return lax.dot_general(a, b, (((1,), (1,)), ((), ())), preferred_element_type=F32)


def t_mm(a, b):
    return lax.dot_general(a, b, (((0,), (0,)), ((), ())), preferred_element_type=F32)


def sees(ids_ref, cnt_ref, a, b):
    inside = jnp.logical_and(a >= 0, a < BLOCKS)
    row = jnp.clip(a, 0, BLOCKS - 1)
    hit = jnp.bool_(False)
    for j in range(NBR):
        hit = jnp.logical_or(hit, jnp.logical_and(j < cnt_ref[row], ids_ref[j, row] == b))
    return jnp.where(jnp.logical_and(hit, inside), F32(0.0), F32(NEG))


def own_bias(mask_ref):
    row = lax.broadcasted_iota(jnp.int32, (2 * BLK, 2 * BLK), 0) >= BLK
    col = lax.broadcasted_iota(jnp.int32, (2 * BLK, 2 * BLK), 1) >= BLK
    off = jnp.where(row, mask_ref[1], mask_ref[0])
    return jnp.where(row == col, F32(0.0), off)


def side_of(index, side):
    even = 1 - lax.rem(index, 2)
    edge = even if side == 0 else 1 - even
    return edge, 2 * edge - 1


def edge_rows(edge):
    return pl.ds(pl.multiple_of(edge * BLK, BLK), BLK)


def head_cols(h, base=0):
    return slice(base + h * HD, base + (h + 1) * HD)


def own_kernel(
    heads, ids_hbm, cnt_hbm, q_hbm, k_hbm, v_hbm, c_hbm, gain_hbm,
    send0_ref, send1_ref, chunk0_ref, chunk1_ref, o_ref, lse_ref, q_ref, k_ref, v_ref, c_ref, gain_ref, mask_ref,
    ids_ref, cnt_ref, sems,
):
    index = lax.axis_index("curve")
    feat = heads * HD
    copies = [
        pltpu.make_async_copy(src, dst, sems.at[n])
        for n, (src, dst) in enumerate(
            (
                (ids_hbm, ids_ref), (cnt_hbm, cnt_ref), (q_hbm, q_ref), (k_hbm, k_ref), (v_hbm, v_ref),
                (c_hbm, c_ref), (gain_hbm, gain_ref),
            )
        )
    ]
    for copy in copies:
        copy.start()
    for copy in copies[:2]:
        copy.wait()
    first = 2 * index
    mask_ref[0] = sees(ids_ref, cnt_ref, first, first + 1)
    mask_ref[1] = sees(ids_ref, cnt_ref, first + 1, first)
    for side in range(2):
        edge, step = side_of(index, side)
        block = first + edge
        mask_ref[2 + 2 * side] = sees(ids_ref, cnt_ref, block, block + step)
        mask_ref[3 + 2 * side] = sees(ids_ref, cnt_ref, block + step, block)
    bias = own_bias(mask_ref)
    for copy in copies[2:]:
        copy.wait()
    lane = lax.broadcasted_iota(jnp.int32, (2 * BLK, 128), 1)
    stats = jnp.zeros((2 * BLK, 128), F32)
    for h in range(heads):
        hs = head_cols(h)
        s = mm_t(q_ref[:, hs], k_ref[:, hs]) * SCALE + bias
        top = jnp.max(s, axis=1, keepdims=True)
        p = jnp.exp(s - top)
        total = jnp.sum(p, axis=1, keepdims=True)
        o_ref[:, hs] = mm(p.astype(BF16), v_ref[:, hs]) / total
        stats = jnp.where(lax.rem(lane, heads) == h, top + jnp.log(total), stats)
    lse_ref[...] = stats
    for side, send in enumerate((send0_ref, send1_ref)):
        edge, _ = side_of(index, side)
        rows = edge_rows(edge)
        for n, ref in enumerate((k_ref, v_ref, q_ref, c_ref)):
            send[:, n * feat : (n + 1) * feat] = ref[rows, :]
        send[:, 4 * feat : 5 * feat] = o_ref[rows, :].astype(BF16)
        lse = lse_ref[rows, :]
        lane = lax.broadcasted_iota(jnp.int32, (BLK, 128), 1)
        hi = lse.astype(BF16).astype(F32)
        mid = (lse - hi).astype(BF16).astype(F32)
        parts = jnp.where(lane < heads, hi, jnp.where(lane < 2 * heads, mid, lse - hi - mid))
        send[:, 5 * feat :] = parts.astype(BF16)
    cut = chunk0_ref.shape[1]
    chunk0_ref[...] = send1_ref[:, :cut]
    chunk1_ref[...] = send1_ref[:, cut:]


def stack(parts):
    return jnp.concatenate(parts, axis=0)


def join_kernel(
    heads, mask_ref, q_ref, k_ref, v_ref, c_ref, gain_ref, o_ref, lse_in_ref, recv0_ref, recv1_ref, chunk0_ref,
    chunk1_ref, a_ref, lse_ref, sums_ref, far_ref,
):
    index = lax.axis_index("curve")
    feat = heads * HD
    cut = chunk0_ref.shape[1]
    lane = lax.broadcasted_iota(jnp.int32, (BLK, 128), 1)
    far_ref[:, :cut] = recv1_ref[:, :cut] + chunk0_ref[...]
    far_ref[:, cut:] = recv1_ref[:, cut:] + chunk1_ref[...]
    for side, recv in enumerate((recv0_ref, far_ref)):
        edge, _ = side_of(index, side)
        rows = edge_rows(edge)
        far_rows = slice((2 + side) * BLK, (3 + side) * BLK)
        lse_own = lse_in_ref[rows, :]
        far = recv[:, 5 * feat :].astype(F32)
        scores = stack(
            [
                mm_t(q_ref[rows, head_cols(h)], recv[:, head_cols(h)]) * SCALE + mask_ref[2 + 2 * side]
                for h in range(heads)
            ]
            + [
                mm_t(recv[:, head_cols(h, 2 * feat)], k_ref[rows, head_cols(h)]) * SCALE + mask_ref[3 + 2 * side]
                for h in range(heads)
            ]
        )
        lse_part = stack(
            [lse_own[:, h : h + 1] for h in range(heads)]
            + [
                far[:, h : h + 1] + far[:, heads + h : heads + h + 1] + far[:, 2 * heads + h : 2 * heads + h + 1]
                for h in range(heads)
            ]
        )
        top = jnp.maximum(jnp.max(scores, axis=1, keepdims=True), lse_part)
        p = jnp.exp(scores - top)
        rest = jnp.exp(lse_part - top)
        total = jnp.sum(p, axis=1, keepdims=True) + rest
        lse = top + jnp.log(total)
        inv = 1.0 / total
        p = (p * inv).astype(BF16)
        rest = rest * inv
        own_stats = jnp.zeros((BLK, 128), F32)
        far_stats = jnp.zeros((BLK, 128), F32)
        sums = [jnp.zeros((BLK, HD), F32) for _ in range(4)]
        for h in range(heads):
            hs = head_cols(h)
            gain = gain_ref[:, hs]
            n = slice(h * BLK, (h + 1) * BLK)
            a = mm(p[n], recv[:, head_cols(h, feat)]) + rest[n] * o_ref[rows, hs]
            a_ref[rows, hs] = a
            own_stats = jnp.where(lane == h, lse[n], own_stats)
            sums[0] += a * a
            sums[1] += c_ref[rows, hs].astype(F32) * gain * a
            n = slice((heads + h) * BLK, (heads + h + 1) * BLK)
            a = mm(p[n], v_ref[rows, hs]) + rest[n] * recv[:, head_cols(h, 4 * feat)].astype(F32)
            a_ref[far_rows, hs] = a
            far_stats = jnp.where(lane == h, lse[n], far_stats)
            sums[2] += a * a
            sums[3] += recv[:, head_cols(h, 3 * feat)].astype(F32) * gain * a
        lse_ref[rows, :] = own_stats
        lse_ref[far_rows, :] = far_stats
        sums = [jnp.sum(x, axis=1, keepdims=True) for x in sums]
        both = jnp.where(
            lane < 2, jnp.where(lane == 0, sums[0], sums[1]), jnp.where(lane == 2, sums[2], sums[3])
        ).T
        for j in range(sums_ref.shape[0]):
            sums_ref[j, pl.ds(edge, 1), :] = both[0:1]
            sums_ref[j, pl.ds(4 + edge, 1), :] = both[1:2]
            sums_ref[j, 2 + side : 3 + side, :] = both[2:3]
            sums_ref[j, 6 + side : 7 + side, :] = both[3:4]


def grad_kernel(
    heads, mask_ref, q_ref, k_ref, v_ref, c_ref, gain_ref, a_ref, lse_ref, recv0_ref, recv1_ref, sums_ref,
    normed_ref, gq_out, gk_out, gv_out, gq_ref, gk_ref, gv_ref, d_ref, delta_ref,
):
    index = lax.axis_index("curve")
    feat = heads * HD
    gain = gain_ref[...]
    lane = lax.broadcasted_iota(jnp.int32, (BLK, 128), 1)
    total = jnp.sum(sums_ref[...], axis=0) / FEAT
    rinv = lax.rsqrt(total[0:4] + EPS)
    turn = rinv * rinv * rinv * total[4:8]
    columns = jnp.concatenate([rinv, turn, jnp.zeros((BLK - 8, 128), F32)], axis=0).T
    for b in range(4):
        rows = slice(b * BLK, (b + 1) * BLK)
        a = a_ref[rows, :]
        r, t = columns[:, b : b + 1], columns[:, 4 + b : 5 + b]
        if b < 2:
            normed_ref[rows, :] = (gain * a * r).astype(BF16)
            cot = c_ref[rows, :]
        else:
            cot = (recv0_ref, recv1_ref)[b - 2][:, 3 * feat : 4 * feat]
        d = (cot.astype(F32) * gain * r - a * t).astype(BF16)
        d_ref[rows, :] = d
        both = d.astype(F32) * a
        delta = jnp.zeros((BLK, 128), F32)
        for h in range(heads):
            delta = jnp.where(lane == h, jnp.sum(both[:, head_cols(h)], axis=1, keepdims=True), delta)
        delta_ref[rows, :] = delta
    bias = own_bias(mask_ref)
    own = slice(0, 2 * BLK)
    for h in range(heads):
        hs = head_cols(h)
        q, k, v, d = q_ref[:, hs], k_ref[:, hs], v_ref[:, hs], d_ref[own, hs]
        p = jnp.exp(mm_t(q, k) * SCALE + bias - lse_ref[own, h : h + 1])
        ds = (p * (mm_t(d, v) - delta_ref[own, h : h + 1]) * SCALE).astype(BF16)
        gq_ref[:, hs] = mm(ds, k)
        gk_ref[:, hs] = t_mm(ds, q)
        gv_ref[:, hs] = t_mm(p.astype(BF16), d)
    for side, recv in enumerate((recv0_ref, recv1_ref)):
        edge, _ = side_of(index, side)
        rows = edge_rows(edge)
        far_rows = slice((2 + side) * BLK, (3 + side) * BLK)
        pairs = [(h, q_ref[rows, head_cols(h)], recv[:, head_cols(h)], recv[:, head_cols(h, feat)], rows) for h in range(heads)]
        pairs += [
            (h, recv[:, head_cols(h, 2 * feat)], k_ref[rows, head_cols(h)], v_ref[rows, head_cols(h)], far_rows)
            for h in range(heads)
        ]
        scores = stack([mm_t(q, k) * SCALE + (mask_ref[2 + 2 * side] if n < heads else mask_ref[3 + 2 * side]) - lse_ref[r, h : h + 1] for n, (h, q, k, v, r) in enumerate(pairs)])
        dprob = stack([mm_t(d_ref[r, head_cols(h)], v) - delta_ref[r, h : h + 1] for h, q, k, v, r in pairs])
        p = jnp.exp(scores)
        ds = (p * dprob * SCALE).astype(BF16)
        p = p.astype(BF16)
        for h in range(heads):
            hs = head_cols(h)
            n = slice(h * BLK, (h + 1) * BLK)
            gq_out[rows, hs] = (gq_ref[rows, hs] + mm(ds[n], recv[:, hs])).astype(BF16)
            n = slice((heads + h) * BLK, (heads + h + 1) * BLK)
            gk_out[rows, hs] = (gk_ref[rows, hs] + t_mm(ds[n], recv[:, head_cols(h, 2 * feat)])).astype(BF16)
            gv_out[rows, hs] = (gv_ref[rows, hs] + t_mm(p[n], d_ref[far_rows, hs])).astype(BF16)


HBM = pl.BlockSpec(memory_space=pltpu.HBM)
SMEM = pl.BlockSpec(memory_space=pltpu.SMEM)
VMEM = pl.BlockSpec(memory_space=pltpu.VMEM)
PARAMS = pltpu.CompilerParams(vmem_limit_bytes=32 * 1024 * 1024)


def shape(dims, dtype):
    return jax.ShapeDtypeStruct(dims, dtype)


def call(kernel, name, in_specs, outs, scratch=(), mask_out=False):
    specs = [VMEM for _ in outs]
    if mask_out:
        specs[-1] = SMEM
    return pl.pallas_call(
        kernel,
        name=name,
        out_shape=tuple(outs),
        in_specs=in_specs,
        out_specs=tuple(specs),
        scratch_shapes=list(scratch),
        compiler_params=PARAMS,
    )


XS, YS, ZLO, CORES = 4, 8, 3, 2
AXES = ("curve", "dp")


def spot(x, y, z, core):
    return ((z // ZLO * YS + y) * XS + x) * (ZLO * CORES) + z % ZLO * CORES + core


def swaps(pairs):
    return pairs + [(b, a) for a, b in pairs]


def routes(count, peers):
    far = range(XS * YS - 1, count - 1, XS * YS)
    even = [(i * peers + j, (i + 1) * peers + j) for i in range(0, count, 2) for j in range(peers)]
    odd = [
        (i * peers + j, (i + 1) * peers + j)
        for i in range(1, count - 1, 2)
        for j in range(peers)
        if i not in far or j < CORES
    ]
    out, on = [], []
    x, y = XS - 1, YS - 1
    for block in range(len(far)):
        for part, (up, down) in ((1, ((x, 0), (0, y))), (2, ((0, 0), (x, y)))):
            for core in range(CORES):
                low, high = block * ZLO + part, (block + 1) * ZLO + part
                out += [(spot(x, y, low, core), spot(*up, low, core)), (spot(0, 0, high, core), spot(*down, high, core))]
                on += [(spot(*up, low, core), spot(0, 0, high, core)), (spot(*down, high, core), spot(x, y, low, core))]
    return swaps(even), swaps(odd), out, on


def shards(queries, keys, values, cotangent, gain, neighbour_ids, neighbour_counts):
    rows, feat = queries.shape
    heads = feat // HD
    peers = lax.axis_size("dp")
    width = 5 * feat + 128
    cut = 11 * 128
    even, odd, out, on = routes(lax.axis_size("curve"), peers)
    local = shape((rows, feat), BF16)
    send0, send1, chunk0, chunk1, o_own, lse_own, q, k, v, c, gain, mask = call(
        functools.partial(own_kernel, heads),
        "own",
        [HBM] * 7,
        [
            shape((BLK, width), BF16), shape((BLK, width), BF16), shape((BLK, cut), BF16),
            shape((BLK, width - cut), BF16), shape((rows, feat), F32), shape((rows, 128), F32),
            local, local, local, local, shape((1, feat), F32), shape((8,), F32),
        ],
        [pltpu.SMEM((NBR, BLOCKS), jnp.int32), pltpu.SMEM((BLOCKS,), jnp.int32), pltpu.SemaphoreType.DMA((7,))],
        mask_out=True,
    )(*(pltpu.with_memory_space_constraint(x, pltpu.HBM) for x in (neighbour_ids.T, neighbour_counts, queries, keys, values, cotangent, gain.reshape(1, feat))))
    chunk0 = lax.ppermute(chunk0, AXES, out)
    chunk1 = lax.ppermute(chunk1, AXES, out)
    recv1 = lax.ppermute(send1, AXES, odd)
    recv0 = lax.ppermute(send0, AXES, even)
    chunk0 = lax.ppermute(chunk0, AXES, on)
    chunk1 = lax.ppermute(chunk1, AXES, on)
    attended, lse, sums, recv1 = call(
        functools.partial(join_kernel, heads),
        "join",
        [SMEM] + [VMEM] * 11,
        [
            shape((2 * rows, feat), F32), shape((2 * rows, 128), F32), shape((peers, 8, 128), F32),
            shape((BLK, width), BF16),
        ],
    )(mask, q, k, v, c, gain, o_own, lse_own, recv0, recv1, chunk0, chunk1)
    sums = lax.all_to_all(sums, "dp", 0, 0, tiled=True)
    return call(
        functools.partial(grad_kernel, heads),
        "grads",
        [SMEM] + [VMEM] * 10,
        [local] * 4,
        [pltpu.VMEM((rows, feat), F32)] * 3 + [pltpu.VMEM((2 * rows, feat), BF16), pltpu.VMEM((2 * rows, 128), F32)],
    )(mask, q, k, v, c, gain, attended, lse, recv0, recv1, sums)


def solution(mesh):
    wide = P("curve", "dp")
    return jax.shard_map(
        shards,
        mesh=mesh,
        in_specs=(wide, wide, wide, wide, P("dp"), P(), P()),
        out_specs=(wide, wide, wide, wide),
        check_vma=False,
    )
```

time: 95 us -> 61.8 us (0.65)
  waiting for transfers between devices: 43.9 us -> 18.5 us
  Pallas kernels: 20.1 us -> 10.5 us
  local copies, waits for them, and re-layouts: 5.3 us -> 0 us
  blocking collectives: 17.1 us -> 21.4 us
  starting transfers between devices: 7.58 us -> 10.3 us
    ppermute x2 -> x6, waiting for transfers between devices: 43.9 us -> 18.5 us  [the longest x1 9.37 us: shards(): recv0 = lax.ppermute(send0, AXES, even)]
    pallas_call x3, Pallas kernels: 20.1 us -> 10.5 us  [the longest x1 4.7 us: shards(): call(functools.partial(grad_kernel, heads), 'grads', [SMEM] + [VMEM] * 10...]
    unnamed x13 -> x0, local copies, waits for them, and re-layouts: 5.3 us -> none
    all_to_all x1, blocking collectives: 17.1 us -> 21.4 us  [shards(): sums = lax.all_to_all(sums, 'dp', 0, 0, tiled=True)]
    ppermute x2 -> x6, starting transfers between devices: 7.58 us -> 10.3 us  [the longest x1 4.18 us: shards(): recv1 = lax.ppermute(send1, AXES, odd)]
  transfers between devices with their start and end apart: 2 -> 6, of which waited for: 2 -> 2; matrix products, arithmetic and copies ran while one was open for 0% -> 0% of each run, Pallas kernels for 0% -> 0%
where the time goes in v2:
time: 61.8 us; the launch traced here: 61.5 us
  blocking collectives  21.4 us (35%)
  waiting for transfers between devices  18.5 us (30%)
  Pallas kernels  10.5 us (17%)
  starting transfers between devices  10.3 us (17%)
  between operations  0.72 us (1%)
    all_to_all x1, blocking collectives, shards(): sums = lax.all_to_all(sums, 'dp', 0, 0, tiled=True)  21.4 us
    ppermute x1, waiting for transfers between devices, shards(): recv0 = lax.ppermute(send0, AXES, even)  9.37 us
    ppermute x1, waiting for transfers between devices, shards(): recv1 = lax.ppermute(send1, AXES, odd)  9.14 us
    pallas_call x1, Pallas kernels, shards(): call(functools.partial(grad_kernel, heads), 'grads', [SMEM] + [VMEM] * 10...  4.7 us
    ppermute x1, starting transfers between devices, shards(): recv1 = lax.ppermute(send1, AXES, odd)  4.18 us
    ppermute x1, starting transfers between devices, shards(): recv0 = lax.ppermute(send0, AXES, even)  3.4 us
    pallas_call x1, Pallas kernels, shards(): call(functools.partial(join_kernel, heads), 'join', [SMEM] + [VMEM] * 11,...  3.22 us
    pallas_call x1, Pallas kernels, shards(): call(functools.partial(own_kernel, heads), 'own', [HBM] * 7, [shape((BLK,...  2.62 us
  transfers between devices with their start and end apart: 6, of which 2 were waited for; matrix products, arithmetic and copies ran while one was open for 0% of the time, Pallas kernels for 0%

profile of v2, /device:TPU:192, one launch (start us, length us, event | category | flops | bytes accessed | tf_op | source)
XLA Modules:
  0.0 61.5 jit_solution(386197733478394693)
XLA Ops:
  0.6 2.6 %own.1 = (bf16[128,2688]{1,0:T(8,128)(2,1)S(1)}, bf16[128,2688]{1,0:T(8,128)(2,1)S(1)}, bf16[128,1408]{1,0:T(8,128)(2,1)S(1)}, bf16[128,1280]{1,0:T(8,128)(2,1)S...) custom-call(s32[3,256]{1,0:T(4,128)} %bitcast.2, ...), custom_call_target="tpu_custom_call" | custom-call | tf_op jit(solution)/shard_map/own/pallas_call | solution.py:326
  3.3 0.7 %collective-permute-start.2 = (bf16[128,1408]{1,0:T(8,128)(2,1)S(1)}, bf16[128,1408]{1,0:T(8,128)(2,1)S(1)}, u32[]{:S(2)}, u32[]{:S(2)}) collective-permute-start(bf16[128,1408]{1,0:T(8,128)(2,1)S(1)} %get-tuple-element.30), channel_id=1, source_target_pairs={{188,20},{194,362},{189,21},{195,363},{190,4},{196,382},{191,5},{1... | collective-permute-start | bytes 1081352 | tf_op jit(solution)/shard_map/ppermute | solution.py:338
  4.0 3.4 %collective-permute-start = (bf16[128,2688]{1,0:T(8,128)(2,1)S(1)}, bf16[128,2688]{1,0:T(8,128)(2,1)S(1)}, u32[]{:S(2)}, u32[]{:S(2)}) collective-permute-start(bf16[128,2688]{1,0:T(8,128)(2,1)S(1)} %get-tuple-element.28), channel_id=1, source_target_pairs={{0,6},{1,7},{2,8},{3,9},{4,10},{5,11},{12,18},{13,19},{14,20},{15,... | collective-permute-start | bytes 2064392 | tf_op jit(solution)/shard_map/ppermute | solution.py:341
  7.4 4.2 %collective-permute-start.1 = (bf16[128,2688]{1,0:T(8,128)(2,1)S(1)}, bf16[128,2688]{1,0:T(8,128)(2,1)S(1)}, u32[]{:S(2)}, u32[]{:S(2)}) collective-permute-start(bf16[128,2688]{1,0:T(8,128)(2,1)S(1)} %get-tuple-element.29), channel_id=1, source_target_pairs={{6,12},{7,13},{8,14},{9,15},{10,16},{11,17},{18,24},{19,25},{20,26... | collective-permute-start | bytes 2064392 | tf_op jit(solution)/shard_map/ppermute | solution.py:340
  11.6 0.7 %collective-permute-start.4 = (bf16[128,1280]{1,0:T(8,128)(2,1)S(1)}, bf16[128,1280]{1,0:T(8,128)(2,1)S(1)}, u32[]{:S(2)}, u32[]{:S(2)}) collective-permute-start(bf16[128,1280]{1,0:T(8,128)(2,1)S(1)} %get-tuple-element.31), channel_id=1, source_target_pairs={{188,20},{194,362},{189,21},{195,363},{190,4},{196,382},{191,5},{1... | collective-permute-start | bytes 983048 | tf_op jit(solution)/shard_map/ppermute | solution.py:339
  12.2 0.0 collective-permute-done.2
  12.2 0.7 %collective-permute-start.3 = (bf16[128,1408]{1,0:T(8,128)(2,1)S(1)}, bf16[128,1408]{1,0:T(8,128)(2,1)S(1)}, u32[]{:S(2)}, u32[]{:S(2)}) collective-permute-start(bf16[128,1408]{1,0:T(8,128)(2,1)S(1)} %collective-permute-done.2), channel_id=1, source_target_pairs={{20,194},{362,188},{21,195},{363,189},{4,196},{382,190},{5,197},{3... | collective-permute-start | bytes 1081352 | tf_op jit(solution)/shard_map/ppermute | solution.py:342
  12.9 0.0 collective-permute-done.4
  13.0 0.7 %collective-permute-start.5 = (bf16[128,1280]{1,0:T(8,128)(2,1)S(1)}, bf16[128,1280]{1,0:T(8,128)(2,1)S(1)}, u32[]{:S(2)}, u32[]{:S(2)}) collective-permute-start(bf16[128,1280]{1,0:T(8,128)(2,1)S(1)} %collective-permute-done.4), channel_id=1, source_target_pairs={{20,194},{362,188},{21,195},{363,189},{4,196},{382,190},{5,197},{3... | collective-permute-start | bytes 983048 | tf_op jit(solution)/shard_map/ppermute | solution.py:343
  13.6 0.0 collective-permute-done.5.chunk1_ref
  13.7 9.4 %collective-permute-done.recv0_ref = bf16[128,2688]{1,0:T(8,128)(2,1)S(1)} collective-permute-done((bf16[128,2688]{1,0:T(8,128)(2,1)S(1)}, bf16[128,2688]{1,0:T(8,128)(2,1)S(1)}, u32[]{:S(2)}, u32[]{:S(2)}) %collective-permute-start) | collective-permute-done | bytes 688160 | tf_op jit(solution)/shard_map/ppermute | solution.py:341
  23.0 9.1 %collective-permute-done.1.recv1_ref = bf16[128,2688]{1,0:T(8,128)(2,1)S(1)} collective-permute-done((bf16[128,2688]{1,0:T(8,128)(2,1)S(1)}, bf16[128,2688]{1,0:T(8,128)(2,1)S(1)}, u32[]{:S(2)}, u32[]{:S(2)}) %collective-permute-start.1) | collective-permute-done | bytes 688160 | tf_op jit(solution)/shard_map/ppermute | solution.py:340
  32.2 0.0 collective-permute-done.3.chunk0_ref
  32.2 3.2 %join.1 = (f32[512,512]{1,0:T(8,128)S(1)}, f32[512,128]{1,0:T(8,128)S(1)}, f32[6,8,128]{2,1,0:T(8,128)S(1)}, bf16[128,2688]{1,0:T(8,128)(2,1)S(1)}) custom-call(f32[8]{0:T(128)S(1)} %get-tuple-element.20.mask_ref, bf16[256,512]{1,0:T(8,128)(2,1)S(1)} %get-tuple-element.21.q_ref, bf16[256,512]{1,0:T(8,128)(2,1)S(1)} %get-tuple-element.22.k_ref, ...), custom_call_target="tpu_custom_call" | custom-call | tf_op jit(solution)/shard_map/join/pallas_call | solution.py:344
  35.4 21.4 %all_to_all.5.sums_ref = f32[6,8,128]{2,1,0:T(8,128)S(1)} all-to-all(f32[6,8,128]{2,1,0:T(8,128)S(1)} %get-tuple-element.35), channel_id=1, replica_groups=mesh['curve'=128,'dp'=6] {'dp'}, dimensions={0} | all-to-all | bytes 49152 | tf_op jit(solution)/shard_map/all_to_all | solution.py:353
  56.8 4.7 %grads.1 = (bf16[256,512]{1,0:T(8,128)(2,1)}, bf16[256,512]{1,0:T(8,128)(2,1)}, bf16[256,512]{1,0:T(8,128)(2,1)}, bf16[256,512]{1,0:T(8,128)(2,1)}) custom-call(f32[8]{0:T(128)S(1)} %get-tuple-element.20.mask_ref, bf16[256,512]{1,0:T(8,128)(2,1)S(1)} %get-tuple-element.21.q_ref, bf16[256,512]{1,0:T(8,128)(2,1)S(1)} %get-tuple-element.22.k_ref, ...), custom_call_target="tpu_custom_call" | custom-call | tf_op jit(solution)/shard_map/grads/pallas_call | solution.py:354
Async XLA Ops:
  3.3 9.0 %collective-permute-start.2 = (bf16[128,1408]{1,0:T(8,128)(2,1)S(1)}, bf16[128,1408]{1,0:T(8,128)(2,1)S(1)}, u32[]{:S(2)}, u32[]{:S(2)}) collective-permute-start(bf16[128,1408]{1,0:T(8,128)(2,1)S(1)} %get-tuple-element.30), channel_id=1, source_target_pairs={{188,20},{194,362},{189,21},{195,363},{190,4},{196,382},{191,5},{1... | collective-permute-start | bytes 1081352 | tf_op jit(solution)/shard_map/ppermute | solution.py:338
  4.0 19.1 %collective-permute-start = (bf16[128,2688]{1,0:T(8,128)(2,1)S(1)}, bf16[128,2688]{1,0:T(8,128)(2,1)S(1)}, u32[]{:S(2)}, u32[]{:S(2)}) collective-permute-start(bf16[128,2688]{1,0:T(8,128)(2,1)S(1)} %get-tuple-element.28), channel_id=1, source_target_pairs={{0,6},{1,7},{2,8},{3,9},{4,10},{5,11},{12,18},{13,19},{14,20},{15,... | collective-permute-start | bytes 2064392 | tf_op jit(solution)/shard_map/ppermute | solution.py:341
  7.4 24.8 %collective-permute-start.1 = (bf16[128,2688]{1,0:T(8,128)(2,1)S(1)}, bf16[128,2688]{1,0:T(8,128)(2,1)S(1)}, u32[]{:S(2)}, u32[]{:S(2)}) collective-permute-start(bf16[128,2688]{1,0:T(8,128)(2,1)S(1)} %get-tuple-element.29), channel_id=1, source_target_pairs={{6,12},{7,13},{8,14},{9,15},{10,16},{11,17},{18,24},{19,25},{20,26... | collective-permute-start | bytes 2064392 | tf_op jit(solution)/shard_map/ppermute | solution.py:340
  11.6 1.4 %collective-permute-start.4 = (bf16[128,1280]{1,0:T(8,128)(2,1)S(1)}, bf16[128,1280]{1,0:T(8,128)(2,1)S(1)}, u32[]{:S(2)}, u32[]{:S(2)}) collective-permute-start(bf16[128,1280]{1,0:T(8,128)(2,1)S(1)} %get-tuple-element.31), channel_id=1, source_target_pairs={{188,20},{194,362},{189,21},{195,363},{190,4},{196,382},{191,5},{1... | collective-permute-start | bytes 983048 | tf_op jit(solution)/shard_map/ppermute | solution.py:339
  12.2 19.9 %collective-permute-start.3 = (bf16[128,1408]{1,0:T(8,128)(2,1)S(1)}, bf16[128,1408]{1,0:T(8,128)(2,1)S(1)}, u32[]{:S(2)}, u32[]{:S(2)}) collective-permute-start(bf16[128,1408]{1,0:T(8,128)(2,1)S(1)} %collective-permute-done.2), channel_id=1, source_target_pairs={{20,194},{362,188},{21,195},{363,189},{4,196},{382,190},{5,197},{3... | collective-permute-start | bytes 1081352 | tf_op jit(solution)/shard_map/ppermute | solution.py:342
  13.0 0.7 %collective-permute-start.5 = (bf16[128,1280]{1,0:T(8,128)(2,1)S(1)}, bf16[128,1280]{1,0:T(8,128)(2,1)S(1)}, u32[]{:S(2)}, u32[]{:S(2)}) collective-permute-start(bf16[128,1280]{1,0:T(8,128)(2,1)S(1)} %collective-permute-done.4), channel_id=1, source_target_pairs={{20,194},{362,188},{21,195},{363,189},{4,196},{382,190},{5,197},{3... | collective-permute-start | bytes 983048 | tf_op jit(solution)/shard_map/ppermute | solution.py:343

commit v3 on v2

--- a/solution.py
+++ b/solution.py
@@ -64,7 +64,7 @@
 
 def own_kernel(
     heads, ids_hbm, cnt_hbm, q_hbm, k_hbm, v_hbm, c_hbm, gain_hbm,
-    send0_ref, send1_ref, chunk0_ref, chunk1_ref, o_ref, lse_ref, q_ref, k_ref, v_ref, c_ref, gain_ref, mask_ref,
+    send1_ref, send0_ref, chunk0_ref, chunk1_ref, o_ref, lse_ref, q_ref, k_ref, v_ref, c_ref, gain_ref, mask_ref,
     ids_ref, cnt_ref, sems,
 ):
     index = lax.axis_index("curve")
@@ -118,7 +118,7 @@
         send[:, 5 * feat :] = parts.astype(BF16)
     cut = chunk0_ref.shape[1]
     chunk0_ref[...] = send1_ref[:, :cut]
-    chunk1_ref[...] = send1_ref[:, cut:]
+    chunk1_ref[...] = send1_ref[:, -cut:]
 
 
 def stack(parts):
@@ -134,7 +134,7 @@
     cut = chunk0_ref.shape[1]
     lane = lax.broadcasted_iota(jnp.int32, (BLK, 128), 1)
     far_ref[:, :cut] = recv1_ref[:, :cut] + chunk0_ref[...]
-    far_ref[:, cut:] = recv1_ref[:, cut:] + chunk1_ref[...]
+    far_ref[:, cut:] = recv1_ref[:, cut:] + chunk1_ref[:, 2 * cut - recv1_ref.shape[1] :]
     for side, recv in enumerate((recv0_ref, far_ref)):
         edge, _ = side_of(index, side)
         rows = edge_rows(edge)
@@ -302,12 +302,12 @@
         (i * peers + j, (i + 1) * peers + j)
         for i in range(1, count - 1, 2)
         for j in range(peers)
-        if i not in far or j < CORES
+        if i not in far or j >= (ZLO - 1) * CORES
     ]
     out, on = [], []
     x, y = XS - 1, YS - 1
     for block in range(len(far)):
-        for part, (up, down) in ((1, ((x, 0), (0, y))), (2, ((0, 0), (x, y)))):
+        for part, (up, down) in ((0, ((x, y - 1), (0, 1))), (1, ((x, 0), (0, y)))):
             for core in range(CORES):
                 low, high = block * ZLO + part, (block + 1) * ZLO + part
                 out += [(spot(x, y, low, core), spot(*up, low, core)), (spot(0, 0, high, core), spot(*down, high, core))]
@@ -323,13 +323,13 @@
     cut = 11 * 128
     even, odd, out, on = routes(lax.axis_size("curve"), peers)
     local = shape((rows, feat), BF16)
-    send0, send1, chunk0, chunk1, o_own, lse_own, q, k, v, c, gain, mask = call(
+    send1, send0, chunk0, chunk1, o_own, lse_own, q, k, v, c, gain, mask = call(
         functools.partial(own_kernel, heads),
         "own",
         [HBM] * 7,
         [
             shape((BLK, width), BF16), shape((BLK, width), BF16), shape((BLK, cut), BF16),
-            shape((BLK, width - cut), BF16), shape((rows, feat), F32), shape((rows, 128), F32),
+            shape((BLK, cut), BF16), shape((rows, feat), F32), shape((rows, 128), F32),
             local, local, local, local, shape((1, feat), F32), shape((8,), F32),
         ],
         [pltpu.SMEM((NBR, BLOCKS), jnp.int32), pltpu.SMEM((BLOCKS,), jnp.int32), pltpu.SemaphoreType.DMA((7,))],

time: 61.8 us -> 61.1 us (0.989)
  the two profiles are of different devices: /device:TPU:192 before, /device:TPU:440 now
where the time goes in v3:
time: 61.1 us; the launch traced here: 60.8 us
  waiting for transfers between devices  29.8 us (49%)
  starting transfers between devices  11.3 us (18%)
  Pallas kernels  10.6 us (17%)
  blocking collectives  8.45 us (14%)
  between operations  0.71 us (1%)
    ppermute x1, waiting for transfers between devices, shards(): recv1 = lax.ppermute(send1, AXES, odd)  20.7 us
    ppermute x1, waiting for transfers between devices, shards(): recv0 = lax.ppermute(send0, AXES, even)  9.06 us
    all_to_all x1, blocking collectives, shards(): sums = lax.all_to_all(sums, 'dp', 0, 0, tiled=True)  8.45 us
    ppermute x1, starting transfers between devices, shards(): recv1 = lax.ppermute(send1, AXES, odd)  5.19 us
    pallas_call x1, Pallas kernels, shards(): call(functools.partial(grad_kernel, heads), 'grads', [SMEM] + [VMEM] * 10...  4.7 us
    ppermute x1, starting transfers between devices, shards(): recv0 = lax.ppermute(send0, AXES, even)  3.4 us
    pallas_call x1, Pallas kernels, shards(): call(functools.partial(join_kernel, heads), 'join', [SMEM] + [VMEM] * 11,...  3.22 us
    pallas_call x1, Pallas kernels, shards(): call(functools.partial(own_kernel, heads), 'own', [HBM] * 7, [shape((BLK,...  2.64 us
  transfers between devices with their start and end apart: 6, of which 2 were waited for; matrix products, arithmetic and copies ran while one was open for 0% of the time, Pallas kernels for 0%

profile of v3, /device:TPU:440, one launch (start us, length us, event | category | flops | bytes accessed | tf_op | source)
XLA Modules:
  0.0 60.8 jit_solution(4532352242505711438)
XLA Ops:
  0.6 2.6 %own.1 = (bf16[128,2688]{1,0:T(8,128)(2,1)S(1)}, bf16[128,2688]{1,0:T(8,128)(2,1)S(1)}, bf16[128,1408]{1,0:T(8,128)(2,1)S(1)}, bf16[128,1408]{1,0:T(8,128)(2,1)S...) custom-call(s32[3,256]{1,0:T(4,128)} %bitcast.2, ...), custom_call_target="tpu_custom_call" | custom-call | tf_op jit(solution)/shard_map/own/pallas_call | solution.py:326
  3.3 0.7 %collective-permute-start.2 = (bf16[128,1408]{1,0:T(8,128)(2,1)S(1)}, bf16[128,1408]{1,0:T(8,128)(2,1)S(1)}, u32[]{:S(2)}, u32[]{:S(2)}) collective-permute-start(bf16[128,1408]{1,0:T(8,128)(2,1)S(1)} %get-tuple-element.30), channel_id=1, source_target_pairs={{186,162},{192,216},{187,163},{193,217},{188,20},{194,362},{189,21... | collective-permute-start | bytes 1081352 | tf_op jit(solution)/shard_map/ppermute | solution.py:338
  4.0 0.7 %collective-permute-start.4 = (bf16[128,1408]{1,0:T(8,128)(2,1)S(1)}, bf16[128,1408]{1,0:T(8,128)(2,1)S(1)}, u32[]{:S(2)}, u32[]{:S(2)}) collective-permute-start(bf16[128,1408]{1,0:T(8,128)(2,1)S(1)} %get-tuple-element.31), channel_id=1, source_target_pairs={{186,162},{192,216},{187,163},{193,217},{188,20},{194,362},{189,21... | collective-permute-start | bytes 1081352 | tf_op jit(solution)/shard_map/ppermute | solution.py:339
  4.7 3.4 %collective-permute-start = (bf16[128,2688]{1,0:T(8,128)(2,1)S(1)}, bf16[128,2688]{1,0:T(8,128)(2,1)S(1)}, u32[]{:S(2)}, u32[]{:S(2)}) collective-permute-start(bf16[128,2688]{1,0:T(8,128)(2,1)S(1)} %get-tuple-element.28), channel_id=1, source_target_pairs={{0,6},{1,7},{2,8},{3,9},{4,10},{5,11},{12,18},{13,19},{14,20},{15,... | collective-permute-start | bytes 2064392 | tf_op jit(solution)/shard_map/ppermute | solution.py:341
  8.1 5.2 %collective-permute-start.1 = (bf16[128,2688]{1,0:T(8,128)(2,1)S(1)}, bf16[128,2688]{1,0:T(8,128)(2,1)S(1)}, u32[]{:S(2)}, u32[]{:S(2)}) collective-permute-start(bf16[128,2688]{1,0:T(8,128)(2,1)S(1)} %get-tuple-element.29), channel_id=1, source_target_pairs={{6,12},{7,13},{8,14},{9,15},{10,16},{11,17},{18,24},{19,25},{20,26... | collective-permute-start | bytes 2064392 | tf_op jit(solution)/shard_map/ppermute | solution.py:340
  13.3 0.0 collective-permute-done.2
  13.3 0.7 %collective-permute-start.3 = (bf16[128,1408]{1,0:T(8,128)(2,1)S(1)}, bf16[128,1408]{1,0:T(8,128)(2,1)S(1)}, u32[]{:S(2)}, u32[]{:S(2)}) collective-permute-start(bf16[128,1408]{1,0:T(8,128)(2,1)S(1)} %collective-permute-done.2), channel_id=1, source_target_pairs={{162,192},{216,186},{163,193},{217,187},{20,194},{362,188},{21,195... | collective-permute-start | bytes 1081352 | tf_op jit(solution)/shard_map/ppermute | solution.py:342
  14.0 0.0 collective-permute-done.4
  14.0 0.7 %collective-permute-start.5 = (bf16[128,1408]{1,0:T(8,128)(2,1)S(1)}, bf16[128,1408]{1,0:T(8,128)(2,1)S(1)}, u32[]{:S(2)}, u32[]{:S(2)}) collective-permute-start(bf16[128,1408]{1,0:T(8,128)(2,1)S(1)} %collective-permute-done.4), channel_id=1, source_target_pairs={{162,192},{216,186},{163,193},{217,187},{20,194},{362,188},{21,195... | collective-permute-start | bytes 1081352 | tf_op jit(solution)/shard_map/ppermute | solution.py:343
  14.7 9.1 %collective-permute-done.recv0_ref = bf16[128,2688]{1,0:T(8,128)(2,1)S(1)} collective-permute-done((bf16[128,2688]{1,0:T(8,128)(2,1)S(1)}, bf16[128,2688]{1,0:T(8,128)(2,1)S(1)}, u32[]{:S(2)}, u32[]{:S(2)}) %collective-permute-start) | collective-permute-done | bytes 688160 | tf_op jit(solution)/shard_map/ppermute | solution.py:341
  23.7 20.7 %collective-permute-done.1.recv1_ref = bf16[128,2688]{1,0:T(8,128)(2,1)S(1)} collective-permute-done((bf16[128,2688]{1,0:T(8,128)(2,1)S(1)}, bf16[128,2688]{1,0:T(8,128)(2,1)S(1)}, u32[]{:S(2)}, u32[]{:S(2)}) %collective-permute-start.1) | collective-permute-done | bytes 688160 | tf_op jit(solution)/shard_map/ppermute | solution.py:340
  44.4 0.0 collective-permute-done.3.chunk0_ref
  44.4 0.0 collective-permute-done.5.chunk1_ref
  44.4 3.2 %join.1 = (f32[512,512]{1,0:T(8,128)S(1)}, f32[512,128]{1,0:T(8,128)S(1)}, f32[6,8,128]{2,1,0:T(8,128)S(1)}, bf16[128,2688]{1,0:T(8,128)(2,1)S(1)}) custom-call(f32[8]{0:T(128)S(1)} %get-tuple-element.20.mask_ref, bf16[256,512]{1,0:T(8,128)(2,1)S(1)} %get-tuple-element.21.q_ref, bf16[256,512]{1,0:T(8,128)(2,1)S(1)} %get-tuple-element.22.k_ref, ...), custom_call_target="tpu_custom_call" | custom-call | tf_op jit(solution)/shard_map/join/pallas_call | solution.py:344
  47.6 8.4 %all_to_all.5.sums_ref = f32[6,8,128]{2,1,0:T(8,128)S(1)} all-to-all(f32[6,8,128]{2,1,0:T(8,128)S(1)} %get-tuple-element.35), channel_id=1, replica_groups=mesh['curve'=128,'dp'=6] {'dp'}, dimensions={0} | all-to-all | bytes 49152 | tf_op jit(solution)/shard_map/all_to_all | solution.py:353
  56.1 4.7 %grads.1 = (bf16[256,512]{1,0:T(8,128)(2,1)}, bf16[256,512]{1,0:T(8,128)(2,1)}, bf16[256,512]{1,0:T(8,128)(2,1)}, bf16[256,512]{1,0:T(8,128)(2,1)}) custom-call(f32[8]{0:T(128)S(1)} %get-tuple-element.20.mask_ref, bf16[256,512]{1,0:T(8,128)(2,1)S(1)} %get-tuple-element.21.q_ref, bf16[256,512]{1,0:T(8,128)(2,1)S(1)} %get-tuple-element.22.k_ref, ...), custom_call_target="tpu_custom_call" | custom-call | tf_op jit(solution)/shard_map/grads/pallas_call | solution.py:354
Async XLA Ops:
  3.3 10.0 %collective-permute-start.2 = (bf16[128,1408]{1,0:T(8,128)(2,1)S(1)}, bf16[128,1408]{1,0:T(8,128)(2,1)S(1)}, u32[]{:S(2)}, u32[]{:S(2)}) collective-permute-start(bf16[128,1408]{1,0:T(8,128)(2,1)S(1)} %get-tuple-element.30), channel_id=1, source_target_pairs={{186,162},{192,216},{187,163},{193,217},{188,20},{194,362},{189,21... | collective-permute-start | bytes 1081352 | tf_op jit(solution)/shard_map/ppermute | solution.py:338
  4.0 10.0 %collective-permute-start.4 = (bf16[128,1408]{1,0:T(8,128)(2,1)S(1)}, bf16[128,1408]{1,0:T(8,128)(2,1)S(1)}, u32[]{:S(2)}, u32[]{:S(2)}) collective-permute-start(bf16[128,1408]{1,0:T(8,128)(2,1)S(1)} %get-tuple-element.31), channel_id=1, source_target_pairs={{186,162},{192,216},{187,163},{193,217},{188,20},{194,362},{189,21... | collective-permute-start | bytes 1081352 | tf_op jit(solution)/shard_map/ppermute | solution.py:339
  4.7 19.1 %collective-permute-start = (bf16[128,2688]{1,0:T(8,128)(2,1)S(1)}, bf16[128,2688]{1,0:T(8,128)(2,1)S(1)}, u32[]{:S(2)}, u32[]{:S(2)}) collective-permute-start(bf16[128,2688]{1,0:T(8,128)(2,1)S(1)} %get-tuple-element.28), channel_id=1, source_target_pairs={{0,6},{1,7},{2,8},{3,9},{4,10},{5,11},{12,18},{13,19},{14,20},{15,... | collective-permute-start | bytes 2064392 | tf_op jit(solution)/shard_map/ppermute | solution.py:341
  8.1 36.3 %collective-permute-start.1 = (bf16[128,2688]{1,0:T(8,128)(2,1)S(1)}, bf16[128,2688]{1,0:T(8,128)(2,1)S(1)}, u32[]{:S(2)}, u32[]{:S(2)}) collective-permute-start(bf16[128,2688]{1,0:T(8,128)(2,1)S(1)} %get-tuple-element.29), channel_id=1, source_target_pairs={{6,12},{7,13},{8,14},{9,15},{10,16},{11,17},{18,24},{19,25},{20,26... | collective-permute-start | bytes 2064392 | tf_op jit(solution)/shard_map/ppermute | solution.py:340
  13.3 31.1 %collective-permute-start.3 = (bf16[128,1408]{1,0:T(8,128)(2,1)S(1)}, bf16[128,1408]{1,0:T(8,128)(2,1)S(1)}, u32[]{:S(2)}, u32[]{:S(2)}) collective-permute-start(bf16[128,1408]{1,0:T(8,128)(2,1)S(1)} %collective-permute-done.2), channel_id=1, source_target_pairs={{162,192},{216,186},{163,193},{217,187},{20,194},{362,188},{21,195... | collective-permute-start | bytes 1081352 | tf_op jit(solution)/shard_map/ppermute | solution.py:342
  14.0 30.4 %collective-permute-start.5 = (bf16[128,1408]{1,0:T(8,128)(2,1)S(1)}, bf16[128,1408]{1,0:T(8,128)(2,1)S(1)}, u32[]{:S(2)}, u32[]{:S(2)}) collective-permute-start(bf16[128,1408]{1,0:T(8,128)(2,1)S(1)} %collective-permute-done.4), channel_id=1, source_target_pairs={{162,192},{216,186},{163,193},{217,187},{20,194},{362,188},{21,195... | collective-permute-start | bytes 1081352 | tf_op jit(solution)/shard_map/ppermute | solution.py:343

commit v4 on v3

--- a/solution.py
+++ b/solution.py
@@ -64,9 +64,9 @@
 
 def own_kernel(
     heads, ids_hbm, cnt_hbm, q_hbm, k_hbm, v_hbm, c_hbm, gain_hbm,
-    send1_ref, send0_ref, chunk0_ref, chunk1_ref, o_ref, lse_ref, q_ref, k_ref, v_ref, c_ref, gain_ref, mask_ref,
-    ids_ref, cnt_ref, sems,
+    send1_ref, send0_ref, o_ref, lse_ref, q_ref, k_ref, v_ref, c_ref, gain_ref, mask_ref, *rest,
 ):
+    *chunk_refs, ids_ref, cnt_ref, sems = rest
     index = lax.axis_index("curve")
     feat = heads * HD
     copies = [
@@ -116,26 +116,34 @@
         mid = (lse - hi).astype(BF16).astype(F32)
         parts = jnp.where(lane < heads, hi, jnp.where(lane < 2 * heads, mid, lse - hi - mid))
         send[:, 5 * feat :] = parts.astype(BF16)
-    cut = chunk0_ref.shape[1]
-    chunk0_ref[...] = send1_ref[:, :cut]
-    chunk1_ref[...] = send1_ref[:, -cut:]
+    cut = chunk_refs[0].shape[1]
+    for n, chunk in enumerate(chunk_refs):
+        chunk[...] = send1_ref[:, n * cut : (n + 1) * cut]
 
 
 def stack(parts):
     return jnp.concatenate(parts, axis=0)
 
 
+def merge_kernel(*refs):
+    *chunk_refs, out_ref = refs
+    cut = chunk_refs[0].shape[1]
+    for n, chunk in enumerate(chunk_refs):
+        out_ref[:, n * cut : (n + 1) * cut] = chunk[...]
+
+
+def add_kernel(a_ref, b_ref, out_ref):
+    out_ref[...] = a_ref[...] + b_ref[...]
+
+
 def join_kernel(
-    heads, mask_ref, q_ref, k_ref, v_ref, c_ref, gain_ref, o_ref, lse_in_ref, recv0_ref, recv1_ref, chunk0_ref,
-    chunk1_ref, a_ref, lse_ref, sums_ref, far_ref,
+    heads, mask_ref, q_ref, k_ref, v_ref, c_ref, gain_ref, o_ref, lse_in_ref, recv0_ref, recv1_ref,
+    a_ref, lse_ref, sums_ref,
 ):
     index = lax.axis_index("curve")
     feat = heads * HD
-    cut = chunk0_ref.shape[1]
     lane = lax.broadcasted_iota(jnp.int32, (BLK, 128), 1)
-    far_ref[:, :cut] = recv1_ref[:, :cut] + chunk0_ref[...]
-    far_ref[:, cut:] = recv1_ref[:, cut:] + chunk1_ref[:, 2 * cut - recv1_ref.shape[1] :]
-    for side, recv in enumerate((recv0_ref, far_ref)):
+    for side, recv in enumerate((recv0_ref, recv1_ref)):
         edge, _ = side_of(index, side)
         rows = edge_rows(edge)
         far_rows = slice((2 + side) * BLK, (3 + side) * BLK)
@@ -268,10 +276,10 @@
     return jax.ShapeDtypeStruct(dims, dtype)
 
 
-def call(kernel, name, in_specs, outs, scratch=(), mask_out=False):
+def call(kernel, name, in_specs, outs, scratch=(), mask_out=None, cost=None):
     specs = [VMEM for _ in outs]
-    if mask_out:
-        specs[-1] = SMEM
+    if mask_out is not None:
+        specs[mask_out] = SMEM
     return pl.pallas_call(
         kernel,
         name=name,
@@ -280,6 +288,7 @@
         out_specs=tuple(specs),
         scratch_shapes=list(scratch),
         compiler_params=PARAMS,
+        cost_estimate=cost,
     )
 
 
@@ -293,6 +302,11 @@
 
 def swaps(pairs):
     return pairs + [(b, a) for a, b in pairs]
+
+
+BESIDE, BEYOND, ACROSS = ((3, 6), (0, 1)), ((2, 6), (1, 1)), ((3, 0), (0, 7))
+RELAYS = ((BESIDE, BESIDE, BEYOND), (ACROSS, ACROSS, ACROSS))
+CHUNKS = 3
 
 
 def routes(count, peers):
@@ -302,17 +316,22 @@
         (i * peers + j, (i + 1) * peers + j)
         for i in range(1, count - 1, 2)
         for j in range(peers)
-        if i not in far or j >= (ZLO - 1) * CORES
+        if i not in far or j >= len(RELAYS) * CORES
     ]
-    out, on = [], []
-    x, y = XS - 1, YS - 1
-    for block in range(len(far)):
-        for part, (up, down) in ((0, ((x, y - 1), (0, 1))), (1, ((x, 0), (0, y)))):
-            for core in range(CORES):
+    hops = []
+    for chunk in range(CHUNKS):
+        out, on = [], []
+        for block in range(len(far)):
+            for part, relays in enumerate(RELAYS):
+                up, down = relays[chunk]
                 low, high = block * ZLO + part, (block + 1) * ZLO + part
-                out += [(spot(x, y, low, core), spot(*up, low, core)), (spot(0, 0, high, core), spot(*down, high, core))]
-                on += [(spot(*up, low, core), spot(0, 0, high, core)), (spot(*down, high, core), spot(x, y, low, core))]
-    return swaps(even), swaps(odd), out, on
+                for core in range(CORES):
+                    first, last = spot(XS - 1, YS - 1, low, core), spot(0, 0, high, core)
+                    over, back = spot(*up, low, core), spot(*down, high, core)
+                    out += [(first, over), (last, back)]
+                    on += [(over, last), (back, first)]
+        hops.append((out, on))
+    return swaps(even), swaps(odd), hops
 
 
 def shards(queries, keys, values, cotangent, gain, neighbour_ids, neighbour_counts):
@@ -320,36 +339,38 @@
     heads = feat // HD
     peers = lax.axis_size("dp")
     width = 5 * feat + 128
-    cut = 11 * 128
-    even, odd, out, on = routes(lax.axis_size("curve"), peers)
+    cut = width // CHUNKS
+    even, odd, hops = routes(lax.axis_size("curve"), peers)
     local = shape((rows, feat), BF16)
-    send1, send0, chunk0, chunk1, o_own, lse_own, q, k, v, c, gain, mask = call(
+    send1, send0, o_own, lse_own, q, k, v, c, gain, mask, *chunks = call(
         functools.partial(own_kernel, heads),
         "own",
         [HBM] * 7,
         [
-            shape((BLK, width), BF16), shape((BLK, width), BF16), shape((BLK, cut), BF16),
-            shape((BLK, cut), BF16), shape((rows, feat), F32), shape((rows, 128), F32),
+            shape((BLK, width), BF16), shape((BLK, width), BF16), shape((rows, feat), F32), shape((rows, 128), F32),
             local, local, local, local, shape((1, feat), F32), shape((8,), F32),
-        ],
+        ]
+        + [shape((BLK, cut), BF16)] * CHUNKS,
         [pltpu.SMEM((NBR, BLOCKS), jnp.int32), pltpu.SMEM((BLOCKS,), jnp.int32), pltpu.SemaphoreType.DMA((7,))],
-        mask_out=True,
+        mask_out=9,
     )(*(pltpu.with_memory_space_constraint(x, pltpu.HBM) for x in (neighbour_ids.T, neighbour_counts, queries, keys, values, cotangent, gain.reshape(1, feat))))
-    chunk0 = lax.ppermute(chunk0, AXES, out)
-    chunk1 = lax.ppermute(chunk1, AXES, out)
+    chunks = [lax.ppermute(chunk, AXES, out) for chunk, (out, _) in zip(chunks, hops)]
     recv1 = lax.ppermute(send1, AXES, odd)
     recv0 = lax.ppermute(send0, AXES, even)
-    chunk0 = lax.ppermute(chunk0, AXES, on)
-    chunk1 = lax.ppermute(chunk1, AXES, on)
-    attended, lse, sums, recv1 = call(
+    chunks = [lax.ppermute(chunk, AXES, on) for chunk, (_, on) in zip(chunks, hops)]
+    (relayed,) = call(
+        merge_kernel, "merge", [VMEM] * CHUNKS, [shape((BLK, width), BF16)],
+        cost=pl.CostEstimate(flops=4 * 10**9, bytes_accessed=4 * BLK * width, transcendentals=0),
+    )(*chunks)
+    (recv1,) = call(add_kernel, "odd", [VMEM] * 2, [shape((BLK, width), BF16)])(recv1, relayed)
+    attended, lse, sums = call(
         functools.partial(join_kernel, heads),
         "join",
-        [SMEM] + [VMEM] * 11,
+        [SMEM] + [VMEM] * 9,
         [
             shape((2 * rows, feat), F32), shape((2 * rows, 128), F32), shape((peers, 8, 128), F32),
-            shape((BLK, width), BF16),
         ],
-    )(mask, q, k, v, c, gain, o_own, lse_own, recv0, recv1, chunk0, chunk1)
+    )(mask, q, k, v, c, gain, o_own, lse_own, recv0, recv1)
     sums = lax.all_to_all(sums, "dp", 0, 0, tiled=True)
     return call(
         functools.partial(grad_kernel, heads),

time: 61.1 us -> 56.8 us (0.930)
  the two profiles are of different devices: /device:TPU:440 before, /device:TPU:192 now
where the time goes in v4:
time: 56.8 us; the launch traced here: 56.5 us
  waiting for transfers between devices  21.9 us (39%)
  starting transfers between devices  12.7 us (22%)
  blocking collectives  10.7 us (19%)
  Pallas kernels  10.6 us (19%)
  between operations  0.74 us (1%)
    ppermute x3, waiting for transfers between devices, shards(): lax.ppermute(chunk, AXES, on)  15.1 us
    all_to_all x1, blocking collectives, shards(): sums = lax.all_to_all(sums, 'dp', 0, 0, tiled=True)  10.7 us
    ppermute x3, waiting for transfers between devices, shards(): lax.ppermute(chunk, AXES, out)  6.77 us
    ppermute x3, starting transfers between devices, shards(): lax.ppermute(chunk, AXES, out)  6.1 us
    pallas_call x1, Pallas kernels, shards(): call(functools.partial(grad_kernel, heads), 'grads', [SMEM] + [VMEM] * 10...  4.68 us
    ppermute x3, starting transfers between devices, shards(): lax.ppermute(chunk, AXES, on)  3.84 us
    pallas_call x1, Pallas kernels, shards(): call(functools.partial(join_kernel, heads), 'join', [SMEM] + [VMEM] * 9,...  3.14 us
    pallas_call x1, Pallas kernels, shards(): call(functools.partial(own_kernel, heads), 'own', [HBM] * 7, [shape((BLK,...  2.63 us
  transfers between devices with their start and end apart: 8, of which 6 were waited for; matrix products, arithmetic and copies ran while one was open for 0% of the time, Pallas kernels for 0%

profile of v4, /device:TPU:192, one launch (start us, length us, event | category | flops | bytes accessed | tf_op | source)
XLA Modules:
  0.0 56.5 jit_solution(16197515838383891076)
XLA Ops:
  0.6 2.6 %own.1 = (bf16[128,2688]{1,0:T(8,128)(2,1)S(1)}, bf16[128,2688]{1,0:T(8,128)(2,1)S(1)}, f32[256,512]{1,0:T(8,128)S(1)}, f32[256,128]{1,0:T(8,128)S(1)}, bf16[256...) custom-call(s32[3,256]{1,0:T(4,128)} %bitcast.2, ...), custom_call_target="tpu_custom_call" | custom-call | tf_op jit(solution)/shard_map/own/pallas_call | solution.py:345
  3.3 3.5 %collective-permute-start.2 = (bf16[128,896]{1,0:T(8,128)(2,1)S(1)}, bf16[128,896]{1,0:T(8,128)(2,1)S(1)}, u32[]{:S(2)}, u32[]{:S(2)}) collective-permute-start(bf16[128,896]{1,0:T(8,128)(2,1)S(1)} %get-tuple-element.30), channel_id=1, source_target_pairs={{186,162},{192,216},{187,163},{193,217},{188,20},{194,362},{189,21... | collective-permute-start | bytes 688136 | tf_op jit(solution)/shard_map/ppermute | solution.py:357
  6.8 1.3 %collective-permute-start.4 = (bf16[128,896]{1,0:T(8,128)(2,1)S(1)}, bf16[128,896]{1,0:T(8,128)(2,1)S(1)}, u32[]{:S(2)}, u32[]{:S(2)}) collective-permute-start(bf16[128,896]{1,0:T(8,128)(2,1)S(1)} %get-tuple-element.31), channel_id=1, source_target_pairs={{186,162},{192,216},{187,163},{193,217},{188,20},{194,362},{189,21... | collective-permute-start | bytes 688136 | tf_op jit(solution)/shard_map/ppermute | solution.py:357
  8.1 1.3 %collective-permute-start.6 = (bf16[128,896]{1,0:T(8,128)(2,1)S(1)}, bf16[128,896]{1,0:T(8,128)(2,1)S(1)}, u32[]{:S(2)}, u32[]{:S(2)}) collective-permute-start(bf16[128,896]{1,0:T(8,128)(2,1)S(1)} %get-tuple-element.32), channel_id=1, source_target_pairs={{186,156},{192,222},{187,157},{193,223},{188,20},{194,362},{189,21... | collective-permute-start | bytes 688136 | tf_op jit(solution)/shard_map/ppermute | solution.py:357
  9.4 0.7 %collective-permute-start.1 = (bf16[128,2688]{1,0:T(8,128)(2,1)S(1)}, bf16[128,2688]{1,0:T(8,128)(2,1)S(1)}, u32[]{:S(2)}, u32[]{:S(2)}) collective-permute-start(bf16[128,2688]{1,0:T(8,128)(2,1)S(1)} %get-tuple-element.29), channel_id=1, source_target_pairs={{6,12},{7,13},{8,14},{9,15},{10,16},{11,17},{18,24},{19,25},{20,26... | collective-permute-start | bytes 2064392 | tf_op jit(solution)/shard_map/ppermute | solution.py:358
  10.1 2.0 %collective-permute-start = (bf16[128,2688]{1,0:T(8,128)(2,1)S(1)}, bf16[128,2688]{1,0:T(8,128)(2,1)S(1)}, u32[]{:S(2)}, u32[]{:S(2)}) collective-permute-start(bf16[128,2688]{1,0:T(8,128)(2,1)S(1)} %get-tuple-element.28), channel_id=1, source_target_pairs={{0,6},{1,7},{2,8},{3,9},{4,10},{5,11},{12,18},{13,19},{14,20},{15,... | collective-permute-start | bytes 2064392 | tf_op jit(solution)/shard_map/ppermute | solution.py:359
  12.1 0.6 %collective-permute-done.2 = bf16[128,896]{1,0:T(8,128)(2,1)S(1)} collective-permute-done((bf16[128,896]{1,0:T(8,128)(2,1)S(1)}, bf16[128,896]{1,0:T(8,128)(2,1)S(1)}, u32[]{:S(2)}, u32[]{:S(2)}) %collective-permute-start.2) | collective-permute-done | bytes 229408 | tf_op jit(solution)/shard_map/ppermute | solution.py:357
  12.7 1.3 %collective-permute-start.3 = (bf16[128,896]{1,0:T(8,128)(2,1)S(1)}, bf16[128,896]{1,0:T(8,128)(2,1)S(1)}, u32[]{:S(2)}, u32[]{:S(2)}) collective-permute-start(bf16[128,896]{1,0:T(8,128)(2,1)S(1)} %collective-permute-done.2), channel_id=1, source_target_pairs={{162,192},{216,186},{163,193},{217,187},{20,194},{362,188},{21,195... | collective-permute-start | bytes 688136 | tf_op jit(solution)/shard_map/ppermute | solution.py:360
  14.0 3.6 %collective-permute-done.4 = bf16[128,896]{1,0:T(8,128)(2,1)S(1)} collective-permute-done((bf16[128,896]{1,0:T(8,128)(2,1)S(1)}, bf16[128,896]{1,0:T(8,128)(2,1)S(1)}, u32[]{:S(2)}, u32[]{:S(2)}) %collective-permute-start.4) | collective-permute-done | bytes 229408 | tf_op jit(solution)/shard_map/ppermute | solution.py:357
  17.7 1.3 %collective-permute-start.5 = (bf16[128,896]{1,0:T(8,128)(2,1)S(1)}, bf16[128,896]{1,0:T(8,128)(2,1)S(1)}, u32[]{:S(2)}, u32[]{:S(2)}) collective-permute-start(bf16[128,896]{1,0:T(8,128)(2,1)S(1)} %collective-permute-done.4), channel_id=1, source_target_pairs={{162,192},{216,186},{163,193},{217,187},{20,194},{362,188},{21,195... | collective-permute-start | bytes 688136 | tf_op jit(solution)/shard_map/ppermute | solution.py:360
  19.0 2.5 %collective-permute-done.6 = bf16[128,896]{1,0:T(8,128)(2,1)S(1)} collective-permute-done((bf16[128,896]{1,0:T(8,128)(2,1)S(1)}, bf16[128,896]{1,0:T(8,128)(2,1)S(1)}, u32[]{:S(2)}, u32[]{:S(2)}) %collective-permute-start.6) | collective-permute-done | bytes 229408 | tf_op jit(solution)/shard_map/ppermute | solution.py:357
  21.5 1.3 %collective-permute-start.7 = (bf16[128,896]{1,0:T(8,128)(2,1)S(1)}, bf16[128,896]{1,0:T(8,128)(2,1)S(1)}, u32[]{:S(2)}, u32[]{:S(2)}) collective-permute-start(bf16[128,896]{1,0:T(8,128)(2,1)S(1)} %collective-permute-done.6), channel_id=1, source_target_pairs={{156,192},{222,186},{157,193},{223,187},{20,194},{362,188},{21,195... | collective-permute-start | bytes 688136 | tf_op jit(solution)/shard_map/ppermute | solution.py:360
  22.8 6.2 %collective-permute-done.3.refs_0_ = bf16[128,896]{1,0:T(8,128)(2,1)S(1)} collective-permute-done((bf16[128,896]{1,0:T(8,128)(2,1)S(1)}, bf16[128,896]{1,0:T(8,128)(2,1)S(1)}, u32[]{:S(2)}, u32[]{:S(2)}) %collective-permute-start.3) | collective-permute-done | bytes 229408 | tf_op jit(solution)/shard_map/ppermute | solution.py:360
  29.0 4.7 %collective-permute-done.5.refs_1_ = bf16[128,896]{1,0:T(8,128)(2,1)S(1)} collective-permute-done((bf16[128,896]{1,0:T(8,128)(2,1)S(1)}, bf16[128,896]{1,0:T(8,128)(2,1)S(1)}, u32[]{:S(2)}, u32[]{:S(2)}) %collective-permute-start.5) | collective-permute-done | bytes 229408 | tf_op jit(solution)/shard_map/ppermute | solution.py:360
  33.7 4.2 %collective-permute-done.7.refs_2_ = bf16[128,896]{1,0:T(8,128)(2,1)S(1)} collective-permute-done((bf16[128,896]{1,0:T(8,128)(2,1)S(1)}, bf16[128,896]{1,0:T(8,128)(2,1)S(1)}, u32[]{:S(2)}, u32[]{:S(2)}) %collective-permute-start.7) | collective-permute-done | bytes 229408 | tf_op jit(solution)/shard_map/ppermute | solution.py:360
  37.8 0.1 merge.1.b_ref
  37.9 0.0 collective-permute-done.1.a_ref
  37.9 0.1 odd.1.recv1_ref
  38.0 0.0 collective-permute-done.recv0_ref
  38.0 3.1 %join.1 = (f32[512,512]{1,0:T(8,128)S(1)}, f32[512,128]{1,0:T(8,128)S(1)}, f32[6,8,128]{2,1,0:T(8,128)S(1)}) custom-call(f32[8]{0:T(128)S(1)} %get-tuple-element.20.mask_ref, bf16[256,512]{1,0:T(8,128)(2,1)S(1)} %get-tuple-element.21.q_ref, bf16[256,512]{1,0:T(8,128)(2,1)S(1)} %get-tuple-element.22.k_ref, bf16[256,512]{1,0:T(8,128)(2,1)S(1)} %get-tuple-element.23.v_ref, ...), custom_call_target="tpu_custom_call" | custom-call | tf_op jit(solution)/shard_map/join/pallas_call | solution.py:366
  41.2 10.7 %all_to_all.5.sums_ref = f32[6,8,128]{2,1,0:T(8,128)S(1)} all-to-all(f32[6,8,128]{2,1,0:T(8,128)S(1)} %get-tuple-element.35), channel_id=1, replica_groups=mesh['curve'=128,'dp'=6] {'dp'}, dimensions={0} | all-to-all | bytes 49152 | tf_op jit(solution)/shard_map/all_to_all | solution.py:374
  51.9 4.7 %grads.1 = (bf16[256,512]{1,0:T(8,128)(2,1)}, bf16[256,512]{1,0:T(8,128)(2,1)}, bf16[256,512]{1,0:T(8,128)(2,1)}, bf16[256,512]{1,0:T(8,128)(2,1)}) custom-call(f32[8]{0:T(128)S(1)} %get-tuple-element.20.mask_ref, bf16[256,512]{1,0:T(8,128)(2,1)S(1)} %get-tuple-element.21.q_ref, bf16[256,512]{1,0:T(8,128)(2,1)S(1)} %get-tuple-element.22.k_ref, ...), custom_call_target="tpu_custom_call" | custom-call | tf_op jit(solution)/shard_map/grads/pallas_call | solution.py:375
Async XLA Ops:
  3.3 9.5 %collective-permute-start.2 = (bf16[128,896]{1,0:T(8,128)(2,1)S(1)}, bf16[128,896]{1,0:T(8,128)(2,1)S(1)}, u32[]{:S(2)}, u32[]{:S(2)}) collective-permute-start(bf16[128,896]{1,0:T(8,128)(2,1)S(1)} %get-tuple-element.30), channel_id=1, source_target_pairs={{186,162},{192,216},{187,163},{193,217},{188,20},{194,362},{189,21... | collective-permute-start | bytes 688136 | tf_op jit(solution)/shard_map/ppermute | solution.py:357
  6.8 10.9 %collective-permute-start.4 = (bf16[128,896]{1,0:T(8,128)(2,1)S(1)}, bf16[128,896]{1,0:T(8,128)(2,1)S(1)}, u32[]{:S(2)}, u32[]{:S(2)}) collective-permute-start(bf16[128,896]{1,0:T(8,128)(2,1)S(1)} %get-tuple-element.31), channel_id=1, source_target_pairs={{186,162},{192,216},{187,163},{193,217},{188,20},{194,362},{189,21... | collective-permute-start | bytes 688136 | tf_op jit(solution)/shard_map/ppermute | solution.py:357
  8.1 13.4 %collective-permute-start.6 = (bf16[128,896]{1,0:T(8,128)(2,1)S(1)}, bf16[128,896]{1,0:T(8,128)(2,1)S(1)}, u32[]{:S(2)}, u32[]{:S(2)}) collective-permute-start(bf16[128,896]{1,0:T(8,128)(2,1)S(1)} %get-tuple-element.32), channel_id=1, source_target_pairs={{186,156},{192,222},{187,157},{193,223},{188,20},{194,362},{189,21... | collective-permute-start | bytes 688136 | tf_op jit(solution)/shard_map/ppermute | solution.py:357
  9.4 28.5 %collective-permute-start.1 = (bf16[128,2688]{1,0:T(8,128)(2,1)S(1)}, bf16[128,2688]{1,0:T(8,128)(2,1)S(1)}, u32[]{:S(2)}, u32[]{:S(2)}) collective-permute-start(bf16[128,2688]{1,0:T(8,128)(2,1)S(1)} %get-tuple-element.29), channel_id=1, source_target_pairs={{6,12},{7,13},{8,14},{9,15},{10,16},{11,17},{18,24},{19,25},{20,26... | collective-permute-start | bytes 2064392 | tf_op jit(solution)/shard_map/ppermute | solution.py:358
  10.1 27.9 %collective-permute-start = (bf16[128,2688]{1,0:T(8,128)(2,1)S(1)}, bf16[128,2688]{1,0:T(8,128)(2,1)S(1)}, u32[]{:S(2)}, u32[]{:S(2)}) collective-permute-start(bf16[128,2688]{1,0:T(8,128)(2,1)S(1)} %get-tuple-element.28), channel_id=1, source_target_pairs={{0,6},{1,7},{2,8},{3,9},{4,10},{5,11},{12,18},{13,19},{14,20},{15,... | collective-permute-start | bytes 2064392 | tf_op jit(solution)/shard_map/ppermute | solution.py:359
  12.7 16.2 %collective-permute-start.3 = (bf16[128,896]{1,0:T(8,128)(2,1)S(1)}, bf16[128,896]{1,0:T(8,128)(2,1)S(1)}, u32[]{:S(2)}, u32[]{:S(2)}) collective-permute-start(bf16[128,896]{1,0:T(8,128)(2,1)S(1)} %collective-permute-done.2), channel_id=1, source_target_pairs={{162,192},{216,186},{163,193},{217,187},{20,194},{362,188},{21,195... | collective-permute-start | bytes 688136 | tf_op jit(solution)/shard_map/ppermute | solution.py:360
  17.7 16.0 %collective-permute-start.5 = (bf16[128,896]{1,0:T(8,128)(2,1)S(1)}, bf16[128,896]{1,0:T(8,128)(2,1)S(1)}, u32[]{:S(2)}, u32[]{:S(2)}) collective-permute-start(bf16[128,896]{1,0:T(8,128)(2,1)S(1)} %collective-permute-done.4), channel_id=1, source_target_pairs={{162,192},{216,186},{163,193},{217,187},{20,194},{362,188},{21,195... | collective-permute-start | bytes 688136 | tf_op jit(solution)/shard_map/ppermute | solution.py:360
  21.5 16.4 %collective-permute-start.7 = (bf16[128,896]{1,0:T(8,128)(2,1)S(1)}, bf16[128,896]{1,0:T(8,128)(2,1)S(1)}, u32[]{:S(2)}, u32[]{:S(2)}) collective-permute-start(bf16[128,896]{1,0:T(8,128)(2,1)S(1)} %collective-permute-done.6), channel_id=1, source_target_pairs={{156,192},{222,186},{157,193},{223,187},{20,194},{362,188},{21,195... | collective-permute-start | bytes 688136 | tf_op jit(solution)/shard_map/ppermute | solution.py:360

commit v5 on v4

v5 whole, which is shorter than its diff:
```python
import functools
import math

import jax
import jax.numpy as jnp
from jax import lax
from jax.experimental import pallas as pl
from jax.experimental.pallas import tpu as pltpu
from jax.sharding import PartitionSpec as P

FEAT = 3072
HD = 128
BLK = 128
NBR = 3
BLOCKS = 256
EPS = 1e-06
SCALE = 1.0 / math.sqrt(HD)
NEG = -1e30
F32 = jnp.float32
BF16 = jnp.bfloat16


def mm(a, b):
    return lax.dot_general(a, b, (((1,), (0,)), ((), ())), preferred_element_type=F32)


def mm_t(a, b):
    return lax.dot_general(a, b, (((1,), (1,)), ((), ())), preferred_element_type=F32)


def t_mm(a, b):
    return lax.dot_general(a, b, (((0,), (0,)), ((), ())), preferred_element_type=F32)


def sees(ids_ref, cnt_ref, a, b):
    inside = jnp.logical_and(a >= 0, a < BLOCKS)
    row = jnp.clip(a, 0, BLOCKS - 1)
    hit = jnp.bool_(False)
    for j in range(NBR):
        hit = jnp.logical_or(hit, jnp.logical_and(j < cnt_ref[row], ids_ref[j, row] == b))
    return jnp.where(jnp.logical_and(hit, inside), F32(0.0), F32(NEG))


def own_bias(mask_ref):
    row = lax.broadcasted_iota(jnp.int32, (2 * BLK, 2 * BLK), 0) >= BLK
    col = lax.broadcasted_iota(jnp.int32, (2 * BLK, 2 * BLK), 1) >= BLK
    off = jnp.where(row, mask_ref[1], mask_ref[0])
    return jnp.where(row == col, F32(0.0), off)


def side_of(index, side):
    even = 1 - lax.rem(index, 2)
    edge = even if side == 0 else 1 - even
    return edge, 2 * edge - 1


def edge_rows(edge):
    return pl.ds(pl.multiple_of(edge * BLK, BLK), BLK)


def head_cols(h, base=0):
    return slice(base + h * HD, base + (h + 1) * HD)


def own_kernel(
    heads, ids_hbm, cnt_hbm, q_hbm, k_hbm, v_hbm, c_hbm, gain_hbm,
    send1_ref, send0_ref, o_ref, lse_ref, p_ref, q_ref, k_ref, v_ref, c_ref, gain_ref, mask_ref, *rest,
):
    *chunk_refs, ids_ref, cnt_ref, sems = rest
    index = lax.axis_index("curve")
    feat = heads * HD
    copies = [
        pltpu.make_async_copy(src, dst, sems.at[n])
        for n, (src, dst) in enumerate(
            (
                (ids_hbm, ids_ref), (cnt_hbm, cnt_ref), (q_hbm, q_ref), (k_hbm, k_ref), (v_hbm, v_ref),
                (c_hbm, c_ref), (gain_hbm, gain_ref),
            )
        )
    ]
    for copy in copies:
        copy.start()
    for copy in copies[:2]:
        copy.wait()
    first = 2 * index
    mask_ref[0] = sees(ids_ref, cnt_ref, first, first + 1)
    mask_ref[1] = sees(ids_ref, cnt_ref, first + 1, first)
    for side in range(2):
        edge, step = side_of(index, side)
        block = first + edge
        mask_ref[2 + 2 * side] = sees(ids_ref, cnt_ref, block, block + step)
        mask_ref[3 + 2 * side] = sees(ids_ref, cnt_ref, block + step, block)
    bias = own_bias(mask_ref)
    for copy in copies[2:5]:
        copy.wait()
    lane = lax.broadcasted_iota(jnp.int32, (2 * BLK, 128), 1)
    stats = jnp.zeros((2 * BLK, 128), F32)
    for h in range(heads):
        hs = head_cols(h)
        s = mm_t(q_ref[:, hs], k_ref[:, hs]) * SCALE + bias
        top = jnp.max(s, axis=1, keepdims=True)
        p = jnp.exp(s - top)
        total = jnp.sum(p, axis=1, keepdims=True)
        p = p * (1.0 / total)
        p_ref[h] = p
        o_ref[:, hs] = mm(p.astype(BF16), v_ref[:, hs])
        stats = jnp.where(lax.rem(lane, heads) == h, top + jnp.log(total), stats)
    lse_ref[...] = stats
    for copy in copies[5:]:
        copy.wait()
    for side, send in enumerate((send0_ref, send1_ref)):
        edge, _ = side_of(index, side)
        rows = edge_rows(edge)
        for n, ref in enumerate((k_ref, v_ref, q_ref, c_ref)):
            send[:, n * feat : (n + 1) * feat] = ref[rows, :]
        send[:, 4 * feat : 5 * feat] = o_ref[rows, :].astype(BF16)
        lse = lse_ref[rows, :]
        lane = lax.broadcasted_iota(jnp.int32, (BLK, 128), 1)
        hi = lse.astype(BF16).astype(F32)
        mid = (lse - hi).astype(BF16).astype(F32)
        parts = jnp.where(lane < heads, hi, jnp.where(lane < 2 * heads, mid, lse - hi - mid))
        send[:, 5 * feat :] = parts.astype(BF16)
    cut = chunk_refs[0].shape[1]
    for n, chunk in enumerate(chunk_refs):
        chunk[...] = send1_ref[:, n * cut : (n + 1) * cut]


def stack(parts):
    return jnp.concatenate(parts, axis=0)


def merge_kernel(*refs):
    _, *chunk_refs, out_ref = refs
    cut = chunk_refs[0].shape[1]
    for n, chunk in enumerate(chunk_refs):
        out_ref[:, n * cut : (n + 1) * cut] = chunk[...]


def hold_kernel(in_ref, out_ref):
    out_ref[...] = in_ref[...]


def add_kernel(a_ref, b_ref, out_ref):
    out_ref[...] = a_ref[...] + b_ref[...]


def join_kernel(
    heads, side, mask_ref, q_ref, k_ref, v_ref, c_ref, gain_ref, o_ref, lse_in_ref, recv, *rest,
):
    *before, a_ref, p_ref, part_ref, sums_ref = rest
    index = lax.axis_index("curve")
    feat = heads * HD
    lane = lax.broadcasted_iota(jnp.int32, (BLK, 128), 1)
    edge, _ = side_of(index, side)
    rows = edge_rows(edge)
    lse_own = lse_in_ref[rows, :]
    far = recv[:, 5 * feat :].astype(F32)
    scores = stack(
        [
            mm_t(q_ref[rows, head_cols(h)], recv[:, head_cols(h)]) * SCALE + mask_ref[2 + 2 * side]
            for h in range(heads)
        ]
        + [
            mm_t(recv[:, head_cols(h, 2 * feat)], k_ref[rows, head_cols(h)]) * SCALE + mask_ref[3 + 2 * side]
            for h in range(heads)
        ]
    )
    lse_part = stack(
        [lse_own[:, h : h + 1] for h in range(heads)]
        + [
            far[:, h : h + 1] + far[:, heads + h : heads + h + 1] + far[:, 2 * heads + h : 2 * heads + h + 1]
            for h in range(heads)
        ]
    )
    top = jnp.maximum(jnp.max(scores, axis=1, keepdims=True), lse_part)
    p = jnp.exp(scores - top)
    part = jnp.exp(lse_part - top)
    inv = 1.0 / (jnp.sum(p, axis=1, keepdims=True) + part)
    p = p * inv
    part = part * inv
    p_ref[...] = p
    p = p.astype(BF16)
    own_part = jnp.zeros((BLK, 128), F32)
    sums = [jnp.zeros((BLK, HD), F32) for _ in range(4)]
    for h in range(heads):
        hs = head_cols(h)
        gain = gain_ref[:, hs]
        n = slice(h * BLK, (h + 1) * BLK)
        a = mm(p[n], recv[:, head_cols(h, feat)]) + part[n] * o_ref[rows, hs]
        a_ref[:BLK, hs] = a
        own_part = jnp.where(lane == h, part[n], own_part)
        sums[0] += a * a
        sums[1] += c_ref[rows, hs].astype(F32) * gain * a
        n = slice((heads + h) * BLK, (heads + h + 1) * BLK)
        a = mm(p[n], v_ref[rows, hs]) + part[n] * recv[:, head_cols(h, 4 * feat)].astype(F32)
        a_ref[BLK:, hs] = a
        sums[2] += a * a
        sums[3] += recv[:, head_cols(h, 3 * feat)].astype(F32) * gain * a
    part_ref[...] = own_part
    sums = [jnp.sum(x, axis=1, keepdims=True) for x in sums]
    both = jnp.where(
        lane < 2, jnp.where(lane == 0, sums[0], sums[1]), jnp.where(lane == 2, sums[2], sums[3])
    ).T
    if not before:
        sums_ref[...] = both[0:8]
        return
    other = before[0][...]
    pairs = (other, both) if side == 1 else (both, other)
    table = [x[r : r + 1] for r in (0, 2, 1, 3) for x in pairs]
    table = jnp.concatenate(table, axis=0)
    for j in range(sums_ref.shape[0]):
        sums_ref[j] = table


def grad_kernel(
    heads, q_ref, k_ref, v_ref, c_ref, gain_ref, p_ref, a0_ref, a1_ref, p0_ref, p1_ref, part0_ref, part1_ref,
    recv0_ref, recv1_ref, sums_ref, normed_hbm, gq_hbm, gk_hbm, gv_hbm,
    normed_ref, gq_out, gk_out, gv_out, gq_ref, gk_ref, gv_ref, d_ref, delta_ref, part_ref, sems,
):
    index = lax.axis_index("curve")
    feat = heads * HD
    gain = gain_ref[...]
    lane = lax.broadcasted_iota(jnp.int32, (BLK, 128), 1)
    total = jnp.sum(sums_ref[...], axis=0) / FEAT
    rinv = lax.rsqrt(total[0:4] + EPS)
    turn = rinv * rinv * rinv * total[4:8]
    columns = jnp.concatenate([rinv, turn, jnp.zeros((BLK - 8, 128), F32)], axis=0).T
    sides = []
    for side in range(2):
        edge, _ = side_of(index, side)
        sides.append(edge_rows(edge))
    for b in range(4):
        side = b % 2
        rows = sides[side] if b < 2 else slice(b * BLK, (b + 1) * BLK)
        a = (a0_ref, a1_ref)[side][:BLK, :] if b < 2 else (a0_ref, a1_ref)[side][BLK:, :]
        r, t = columns[:, b : b + 1], columns[:, 4 + b : 5 + b]
        if b < 2:
            normed_ref[rows, :] = (gain * a * r).astype(BF16)
            cot = c_ref[rows, :]
            part_ref[rows, :] = (part0_ref, part1_ref)[side][...]
        else:
            cot = (recv0_ref, recv1_ref)[side][:, 3 * feat : 4 * feat]
        d = (cot.astype(F32) * gain * r - a * t).astype(BF16)
        d_ref[rows, :] = d
        both = d.astype(F32) * a
        delta = jnp.zeros((BLK, 128), F32)
        for h in range(heads):
            delta = jnp.where(lane == h, jnp.sum(both[:, head_cols(h)], axis=1, keepdims=True), delta)
        delta_ref[rows, :] = delta
    copies = [pltpu.make_async_copy(normed_ref, normed_hbm, sems.at[0])]
    copies[0].start()
    own = slice(0, 2 * BLK)
    for h in range(heads):
        hs = head_cols(h)
        q, k, v, d = q_ref[:, hs], k_ref[:, hs], v_ref[:, hs], d_ref[own, hs]
        p = p_ref[h] * part_ref[own, h : h + 1]
        ds = (p * (mm_t(d, v) - delta_ref[own, h : h + 1]) * SCALE).astype(BF16)
        gq_ref[:, hs] = mm(ds, k)
        gk_ref[:, hs] = t_mm(ds, q)
        gv_ref[:, hs] = t_mm(p.astype(BF16), d)
    for side, recv in enumerate((recv0_ref, recv1_ref)):
        rows = sides[side]
        far_rows = slice((2 + side) * BLK, (3 + side) * BLK)
        pairs = [(h, recv[:, head_cols(h, feat)], rows) for h in range(heads)]
        pairs += [(h, v_ref[rows, head_cols(h)], far_rows) for h in range(heads)]
        dprob = stack([mm_t(d_ref[r, head_cols(h)], v) - delta_ref[r, h : h + 1] for h, v, r in pairs])
        p = (p0_ref, p1_ref)[side][...]
        ds = (p * dprob * SCALE).astype(BF16)
        p = p.astype(BF16)
        for h in range(heads):
            hs = head_cols(h)
            n = slice(h * BLK, (h + 1) * BLK)
            gq_out[rows, hs] = (gq_ref[rows, hs] + mm(ds[n], recv[:, hs])).astype(BF16)
            n = slice((heads + h) * BLK, (heads + h + 1) * BLK)
            gk_out[rows, hs] = (gk_ref[rows, hs] + t_mm(ds[n], recv[:, head_cols(h, 2 * feat)])).astype(BF16)
            gv_out[rows, hs] = (gv_ref[rows, hs] + t_mm(p[n], d_ref[far_rows, hs])).astype(BF16)
        for n, (src, dst) in enumerate(((gq_out, gq_hbm), (gk_out, gk_hbm), (gv_out, gv_hbm))):
            copy = pltpu.make_async_copy(src.at[rows, :], dst.at[rows, :], sems.at[1 + 3 * side + n])
            copy.start()
            copies.append(copy)
    for copy in copies:
        copy.wait()


HBM = pl.BlockSpec(memory_space=pltpu.HBM)
SMEM = pl.BlockSpec(memory_space=pltpu.SMEM)
VMEM = pl.BlockSpec(memory_space=pltpu.VMEM)
PARAMS = pltpu.CompilerParams(vmem_limit_bytes=32 * 1024 * 1024)


def shape(dims, dtype):
    return jax.ShapeDtypeStruct(dims, dtype)


def call(kernel, name, in_specs, outs, scratch=(), mask_out=None, cost=None, space=None):
    specs = [space or VMEM for _ in outs]
    if mask_out is not None:
        specs[mask_out] = SMEM
    return pl.pallas_call(
        kernel,
        name=name,
        out_shape=tuple(outs),
        in_specs=in_specs,
        out_specs=tuple(specs),
        scratch_shapes=list(scratch),
        compiler_params=PARAMS,
        cost_estimate=cost,
    )


XS, YS, ZLO, CORES = 4, 8, 3, 2
AXES = ("curve", "dp")


def spot(x, y, z, core):
    return ((z // ZLO * YS + y) * XS + x) * (ZLO * CORES) + z % ZLO * CORES + core


def swaps(pairs):
    return pairs + [(b, a) for a, b in pairs]


BESIDE, BEYOND, ACROSS = ((3, 6), (0, 1)), ((2, 6), (1, 1)), ((3, 0), (0, 7))
RELAYS = ((BESIDE, BESIDE, BEYOND), (ACROSS, ACROSS, ACROSS))
CHUNKS = 3
HOP_COST, ODD_COST, JOIN_COST, MERGE_COST = 10**10, 10**8, 10**6, 10**6


def routes(count, peers):
    far = range(XS * YS - 1, count - 1, XS * YS)
    even = [(i * peers + j, (i + 1) * peers + j) for i in range(0, count, 2) for j in range(peers)]
    odd = [
        (i * peers + j, (i + 1) * peers + j)
        for i in range(1, count - 1, 2)
        for j in range(peers)
        if i not in far or j >= len(RELAYS) * CORES
    ]
    hops = []
    for chunk in range(CHUNKS):
        out, on = [], []
        for block in range(len(far)):
            for part, relays in enumerate(RELAYS):
                up, down = relays[chunk]
                low, high = block * ZLO + part, (block + 1) * ZLO + part
                for core in range(CORES):
                    first, last = spot(XS - 1, YS - 1, low, core), spot(0, 0, high, core)
                    over, back = spot(*up, low, core), spot(*down, high, core)
                    out += [(first, over), (last, back)]
                    on += [(over, last), (back, first)]
        hops.append((out, on))
    return swaps(even), swaps(odd), hops


def hold(x, name, cost):
    (x,) = call(
        hold_kernel, name, [VMEM], [shape(x.shape, x.dtype)],
        cost=pl.CostEstimate(flops=cost, bytes_accessed=4 * x.size, transcendentals=0),
    )(x)
    return x


def shards(queries, keys, values, cotangent, gain, neighbour_ids, neighbour_counts):
    rows, feat = queries.shape
    heads = feat // HD
    peers = lax.axis_size("dp")
    width = 5 * feat + 128
    cut = width // CHUNKS
    even, odd, hops = routes(lax.axis_size("curve"), peers)
    local = shape((rows, feat), BF16)
    send1, send0, o_own, lse_own, p_own, q, k, v, c, gain, mask, *chunks = call(
        functools.partial(own_kernel, heads),
        "own",
        [HBM] * 7,
        [
            shape((BLK, width), BF16), shape((BLK, width), BF16), shape((rows, feat), F32), shape((rows, 128), F32),
            shape((heads, rows, rows), F32), local, local, local, local, shape((1, feat), F32), shape((8,), F32),
        ]
        + [shape((BLK, cut), BF16)] * CHUNKS,
        [pltpu.SMEM((NBR, BLOCKS), jnp.int32), pltpu.SMEM((BLOCKS,), jnp.int32), pltpu.SemaphoreType.DMA((7,))],
        mask_out=10,
    )(*(pltpu.with_memory_space_constraint(x, pltpu.HBM) for x in (neighbour_ids.T, neighbour_counts, queries, keys, values, cotangent, gain.reshape(1, feat))))
    chunks = [lax.ppermute(chunk, AXES, out) for chunk, (out, _) in zip(chunks, hops)]
    recv1 = lax.ppermute(send1, AXES, odd)
    recv0 = lax.ppermute(send0, AXES, even)
    chunks = [hold(chunk, "hop", HOP_COST) for chunk in chunks]
    chunks = [lax.ppermute(chunk, AXES, on) for chunk, (_, on) in zip(chunks, hops)]
    recv1 = hold(recv1, "odd_in", ODD_COST)
    edge = [shape((rows, feat), F32), shape((2 * heads * BLK, 128), F32), shape((BLK, 128), F32)]
    a0, p0, part0, sums = call(
        functools.partial(join_kernel, heads, 0), "join_even", [SMEM] + [VMEM] * 8, edge + [shape((8, 128), F32)],
        cost=pl.CostEstimate(flops=JOIN_COST, bytes_accessed=4 * rows * feat, transcendentals=0),
    )(mask, q, k, v, c, gain, o_own, lse_own, recv0)
    (relayed,) = call(
        merge_kernel, "merge", [VMEM] * (1 + CHUNKS), [shape((BLK, width), BF16)],
        cost=pl.CostEstimate(flops=MERGE_COST, bytes_accessed=4 * BLK * width, transcendentals=0),
    )(sums, *chunks)
    (recv1,) = call(
        add_kernel, "odd", [VMEM] * 2, [shape((BLK, width), BF16)]
    )(recv1, relayed)
    a1, p1, part1, sums = call(
        functools.partial(join_kernel, heads, 1), "join_odd", [SMEM] + [VMEM] * 9, edge + [shape((peers, 8, 128), F32)],
    )(mask, q, k, v, c, gain, o_own, lse_own, recv1, sums)
    sums = lax.all_to_all(sums, "dp", 0, 0, tiled=True)
    return call(
        functools.partial(grad_kernel, heads),
        "grads",
        [VMEM] * 15,
        [local] * 4,
        [pltpu.VMEM((rows, feat), BF16)] * 4
        + [pltpu.VMEM((rows, feat), F32)] * 3
        + [
            pltpu.VMEM((2 * rows, feat), BF16), pltpu.VMEM((2 * rows, 128), F32), pltpu.VMEM((rows, 128), F32),
            pltpu.SemaphoreType.DMA((7,)),
        ],
        space=HBM,
    )(q, k, v, c, gain, p_own, a0, a1, p0, p1, part0, part1, recv0, recv1, sums)


def solution(mesh):
    wide = P("curve", "dp")
    return jax.shard_map(
        shards,
        mesh=mesh,
        in_specs=(wide, wide, wide, wide, P("dp"), P(), P()),
        out_specs=(wide, wide, wide, wide),
        check_vma=False,
    )
```

time: 56.8 us -> 54.9 us (0.967)
  waiting for transfers between devices: 21.9 us -> 19.9 us
    ppermute x3, waiting for transfers between devices: 15.1 us -> 7.76 us  [shards(): lax.ppermute(chunk, AXES, on)]
    ppermute x1, waiting for transfers between devices: 0.01 us -> 5.38 us  [shards(): recv0 = lax.ppermute(send0, AXES, even)]
    pallas_call x3 -> x8, Pallas kernels: 7.87 us -> 7.61 us  [the longest x1 3.71 us: shards(): call(functools.partial(grad_kernel, heads), 'grads', [VMEM] * 15, [local]...]
  transfers between devices with their start and end apart: 8 -> 8, of which waited for: 6 -> 6; matrix products, arithmetic and copies ran while one was open for 0% -> 0% of each run, Pallas kernels for 0% -> 4%
where the time goes in v5:
time: 54.9 us; the launch traced here: 54.6 us
  waiting for transfers between devices  19.9 us (36%)
  starting transfers between devices  12.6 us (23%)
  blocking collectives  10.7 us (19%)
  Pallas kernels  10.6 us (19%)
  between operations  0.75 us (1%)
    all_to_all x1, blocking collectives, shards(): sums = lax.all_to_all(sums, 'dp', 0, 0, tiled=True)  10.7 us
    ppermute x3, waiting for transfers between devices, shards(): lax.ppermute(chunk, AXES, on)  7.76 us
    ppermute x3, waiting for transfers between devices, shards(): lax.ppermute(chunk, AXES, out)  6.8 us
    ppermute x3, starting transfers between devices, shards(): lax.ppermute(chunk, AXES, out)  6.1 us
    ppermute x1, waiting for transfers between devices, shards(): recv0 = lax.ppermute(send0, AXES, even)  5.38 us
    ppermute x3, starting transfers between devices, shards(): lax.ppermute(chunk, AXES, on)  3.88 us
    pallas_call x1, Pallas kernels, shards(): call(functools.partial(grad_kernel, heads), 'grads', [VMEM] * 15, [local]...  3.71 us
    pallas_call x1, Pallas kernels, shards(): call(functools.partial(own_kernel, heads), 'own', [HBM] * 7, [shape((BLK,...  2.94 us
  transfers between devices with their start and end apart: 8, of which 6 were waited for; matrix products, arithmetic and copies ran while one was open for 0% of the time, Pallas kernels for 4%

profile of v5, /device:TPU:192, one launch (start us, length us, event | category | flops | bytes accessed | tf_op | source)
XLA Modules:
  0.0 54.6 jit_solution(15349596511786321953)
XLA Ops:
  0.6 2.9 %own.1 = (bf16[128,2688]{1,0:T(8,128)(2,1)S(1)}, bf16[128,2688]{1,0:T(8,128)(2,1)S(1)}, f32[256,512]{1,0:T(8,128)S(1)}, f32[256,128]{1,0:T(8,128)S(1)}, f32[4,25...) custom-call(s32[3,256]{1,0:T(4,128)} %bitcast.2, ...), custom_call_target="tpu_custom_call" | custom-call | tf_op jit(solution)/shard_map/own/pallas_call | solution.py:370
  3.6 3.5 %collective-permute-start.2 = (bf16[128,896]{1,0:T(8,128)(2,1)S(1)}, bf16[128,896]{1,0:T(8,128)(2,1)S(1)}, u32[]{:S(2)}, u32[]{:S(2)}) collective-permute-start(bf16[128,896]{1,0:T(8,128)(2,1)S(1)} %get-tuple-element.39), channel_id=1, source_target_pairs={{186,162},{192,216},{187,163},{193,217},{188,20},{194,362},{189,21... | collective-permute-start | bytes 688136 | tf_op jit(solution)/shard_map/ppermute | solution.py:382
  7.1 1.3 %collective-permute-start.4 = (bf16[128,896]{1,0:T(8,128)(2,1)S(1)}, bf16[128,896]{1,0:T(8,128)(2,1)S(1)}, u32[]{:S(2)}, u32[]{:S(2)}) collective-permute-start(bf16[128,896]{1,0:T(8,128)(2,1)S(1)} %get-tuple-element.40), channel_id=1, source_target_pairs={{186,162},{192,216},{187,163},{193,217},{188,20},{194,362},{189,21... | collective-permute-start | bytes 688136 | tf_op jit(solution)/shard_map/ppermute | solution.py:382
  8.4 1.3 %collective-permute-start.6 = (bf16[128,896]{1,0:T(8,128)(2,1)S(1)}, bf16[128,896]{1,0:T(8,128)(2,1)S(1)}, u32[]{:S(2)}, u32[]{:S(2)}) collective-permute-start(bf16[128,896]{1,0:T(8,128)(2,1)S(1)} %get-tuple-element.41), channel_id=1, source_target_pairs={{186,156},{192,222},{187,157},{193,223},{188,20},{194,362},{189,21... | collective-permute-start | bytes 688136 | tf_op jit(solution)/shard_map/ppermute | solution.py:382
  9.7 1.9 %collective-permute-start = (bf16[128,2688]{1,0:T(8,128)(2,1)S(1)}, bf16[128,2688]{1,0:T(8,128)(2,1)S(1)}, u32[]{:S(2)}, u32[]{:S(2)}) collective-permute-start(bf16[128,2688]{1,0:T(8,128)(2,1)S(1)} %get-tuple-element.35), channel_id=1, source_target_pairs={{0,6},{1,7},{2,8},{3,9},{4,10},{5,11},{12,18},{13,19},{14,20},{15,... | collective-permute-start | bytes 2064392 | tf_op jit(solution)/shard_map/ppermute | solution.py:384
  11.6 0.7 %collective-permute-start.1 = (bf16[128,2688]{1,0:T(8,128)(2,1)S(1)}, bf16[128,2688]{1,0:T(8,128)(2,1)S(1)}, u32[]{:S(2)}, u32[]{:S(2)}) collective-permute-start(bf16[128,2688]{1,0:T(8,128)(2,1)S(1)} %get-tuple-element.37), channel_id=1, source_target_pairs={{6,12},{7,13},{8,14},{9,15},{10,16},{11,17},{18,24},{19,25},{20,26... | collective-permute-start | bytes 2064392 | tf_op jit(solution)/shard_map/ppermute | solution.py:383
  12.3 0.7 %collective-permute-done.2.in_ref = bf16[128,896]{1,0:T(8,128)(2,1)S(1)} collective-permute-done((bf16[128,896]{1,0:T(8,128)(2,1)S(1)}, bf16[128,896]{1,0:T(8,128)(2,1)S(1)}, u32[]{:S(2)}, u32[]{:S(2)}) %collective-permute-start.2) | collective-permute-done | bytes 229408 | tf_op jit(solution)/shard_map/ppermute | solution.py:382
  13.1 1.3 %collective-permute-start.3 = (bf16[128,896]{1,0:T(8,128)(2,1)S(1)}, bf16[128,896]{1,0:T(8,128)(2,1)S(1)}, u32[]{:S(2)}, u32[]{:S(2)}) collective-permute-start(bf16[128,896]{1,0:T(8,128)(2,1)S(1)} %hop.3), channel_id=1, source_target_pairs={{162,192},{216,186},{163,193},{217,187},{20,194},{362,188},{21,195... | collective-permute-start | bytes 688136 | tf_op jit(solution)/shard_map/ppermute | solution.py:386
  14.4 3.6 %collective-permute-done.4.in_ref = bf16[128,896]{1,0:T(8,128)(2,1)S(1)} collective-permute-done((bf16[128,896]{1,0:T(8,128)(2,1)S(1)}, bf16[128,896]{1,0:T(8,128)(2,1)S(1)}, u32[]{:S(2)}, u32[]{:S(2)}) %collective-permute-start.4) | collective-permute-done | bytes 229408 | tf_op jit(solution)/shard_map/ppermute | solution.py:382
  18.0 1.3 %collective-permute-start.5 = (bf16[128,896]{1,0:T(8,128)(2,1)S(1)}, bf16[128,896]{1,0:T(8,128)(2,1)S(1)}, u32[]{:S(2)}, u32[]{:S(2)}) collective-permute-start(bf16[128,896]{1,0:T(8,128)(2,1)S(1)} %hop.4), channel_id=1, source_target_pairs={{162,192},{216,186},{163,193},{217,187},{20,194},{362,188},{21,195... | collective-permute-start | bytes 688136 | tf_op jit(solution)/shard_map/ppermute | solution.py:386
  19.3 2.5 %collective-permute-done.6.in_ref = bf16[128,896]{1,0:T(8,128)(2,1)S(1)} collective-permute-done((bf16[128,896]{1,0:T(8,128)(2,1)S(1)}, bf16[128,896]{1,0:T(8,128)(2,1)S(1)}, u32[]{:S(2)}, u32[]{:S(2)}) %collective-permute-start.6) | collective-permute-done | bytes 229408 | tf_op jit(solution)/shard_map/ppermute | solution.py:382
  21.8 1.3 %collective-permute-start.7 = (bf16[128,896]{1,0:T(8,128)(2,1)S(1)}, bf16[128,896]{1,0:T(8,128)(2,1)S(1)}, u32[]{:S(2)}, u32[]{:S(2)}) collective-permute-start(bf16[128,896]{1,0:T(8,128)(2,1)S(1)} %hop.5), channel_id=1, source_target_pairs={{156,192},{222,186},{157,193},{223,187},{20,194},{362,188},{21,195... | collective-permute-start | bytes 688136 | tf_op jit(solution)/shard_map/ppermute | solution.py:386
  23.1 5.4 %collective-permute-done.recv.recv0_ref = bf16[128,2688]{1,0:T(8,128)(2,1)S(1)} collective-permute-done((bf16[128,2688]{1,0:T(8,128)(2,1)S(1)}, bf16[128,2688]{1,0:T(8,128)(2,1)S(1)}, u32[]{:S(2)}, u32[]{:S(2)}) %collective-permute-start) | collective-permute-done | bytes 688160 | tf_op jit(solution)/shard_map/ppermute | solution.py:384
  28.5 1.9 %join_even.1 = (f32[256,512]{1,0:T(8,128)S(1)}, f32[1024,128]{1,0:T(8,128)S(1)}, f32[128,128]{1,0:T(8,128)S(1)}, f32[8,128]{1,0:T(8,128)S(1)}) custom-call(f32[8]{0:T(128)S(1)} %get-tuple-element.32.mask_ref, bf16[256,512]{1,0:T(8,128)(2,1)S(1)} %get-tuple-element.26.q_ref, bf16[256,512]{1,0:T(8,128)(2,1)S(1)} %get-tuple-element.27.k_ref, ...), custom_call_target="tpu_custom_call" | custom-call | flops 1000000 | bytes 524288 | tf_op jit(solution)/shard_map/join_even/pallas_call | solution.py:389
  30.4 0.0 collective-permute-done.1.in_ref
  30.4 0.0 collective-permute-done.3.refs_1_
  30.4 3.6 %collective-permute-done.5.refs_2_ = bf16[128,896]{1,0:T(8,128)(2,1)S(1)} collective-permute-done((bf16[128,896]{1,0:T(8,128)(2,1)S(1)}, bf16[128,896]{1,0:T(8,128)(2,1)S(1)}, u32[]{:S(2)}, u32[]{:S(2)}) %collective-permute-start.5) | collective-permute-done | bytes 229408 | tf_op jit(solution)/shard_map/ppermute | solution.py:386
  34.0 4.2 %collective-permute-done.7.refs_3_ = bf16[128,896]{1,0:T(8,128)(2,1)S(1)} collective-permute-done((bf16[128,896]{1,0:T(8,128)(2,1)S(1)}, bf16[128,896]{1,0:T(8,128)(2,1)S(1)}, u32[]{:S(2)}, u32[]{:S(2)}) %collective-permute-start.7) | collective-permute-done | bytes 229408 | tf_op jit(solution)/shard_map/ppermute | solution.py:386
  38.2 0.1 merge.1.b_ref
  38.2 0.1 odd.1.recv.recv1_ref
  38.3 1.9 %join_odd.1 = (f32[256,512]{1,0:T(8,128)S(1)}, f32[1024,128]{1,0:T(8,128)S(1)}, f32[128,128]{1,0:T(8,128)S(1)}, f32[6,8,128]{2,1,0:T(8,128)S(1)}) custom-call(f32[8]{0:T(128)S(1)} %get-tuple-element.32.mask_ref, bf16[256,512]{1,0:T(8,128)(2,1)S(1)} %get-tuple-element.26.q_ref, bf16[256,512]{1,0:T(8,128)(2,1)S(1)} %get-tuple-element.27.k_ref, ...), custom_call_target="tpu_custom_call" | custom-call | tf_op jit(solution)/shard_map/join_odd/pallas_call | solution.py:400
  40.2 10.7 %all_to_all.5.sums_ref = f32[6,8,128]{2,1,0:T(8,128)S(1)} all-to-all(f32[6,8,128]{2,1,0:T(8,128)S(1)} %get-tuple-element.47), channel_id=1, replica_groups=mesh['curve'=128,'dp'=6] {'dp'}, dimensions={0} | all-to-all | bytes 49152 | tf_op jit(solution)/shard_map/all_to_all | solution.py:403
  50.9 3.7 %grads.1 = (bf16[256,512]{1,0:T(8,128)(2,1)}, bf16[256,512]{1,0:T(8,128)(2,1)}, bf16[256,512]{1,0:T(8,128)(2,1)}, bf16[256,512]{1,0:T(8,128)(2,1)}) custom-call(bf16[256,512]{1,0:T(8,128)(2,1)S(1)} %get-tuple-element.26.q_ref, bf16[256,512]{1,0:T(8,128)(2,1)S(1)} %get-tuple-element.27.k_ref, bf16[256,512]{1,0:T(8,128)(2,1)S(1)} %get-tuple-element.28.v_ref, ...), custom_call_target="tpu_custom_call" | custom-call | tf_op jit(solution)/shard_map/grads/pallas_call | solution.py:404
  (4 shorter events, 0.1 us)
Async XLA Ops:
  3.6 9.5 %collective-permute-start.2 = (bf16[128,896]{1,0:T(8,128)(2,1)S(1)}, bf16[128,896]{1,0:T(8,128)(2,1)S(1)}, u32[]{:S(2)}, u32[]{:S(2)}) collective-permute-start(bf16[128,896]{1,0:T(8,128)(2,1)S(1)} %get-tuple-element.39), channel_id=1, source_target_pairs={{186,162},{192,216},{187,163},{193,217},{188,20},{194,362},{189,21... | collective-permute-start | bytes 688136 | tf_op jit(solution)/shard_map/ppermute | solution.py:382
  7.1 10.9 %collective-permute-start.4 = (bf16[128,896]{1,0:T(8,128)(2,1)S(1)}, bf16[128,896]{1,0:T(8,128)(2,1)S(1)}, u32[]{:S(2)}, u32[]{:S(2)}) collective-permute-start(bf16[128,896]{1,0:T(8,128)(2,1)S(1)} %get-tuple-element.40), channel_id=1, source_target_pairs={{186,162},{192,216},{187,163},{193,217},{188,20},{194,362},{189,21... | collective-permute-start | bytes 688136 | tf_op jit(solution)/shard_map/ppermute | solution.py:382
  8.4 13.4 %collective-permute-start.6 = (bf16[128,896]{1,0:T(8,128)(2,1)S(1)}, bf16[128,896]{1,0:T(8,128)(2,1)S(1)}, u32[]{:S(2)}, u32[]{:S(2)}) collective-permute-start(bf16[128,896]{1,0:T(8,128)(2,1)S(1)} %get-tuple-element.41), channel_id=1, source_target_pairs={{186,156},{192,222},{187,157},{193,223},{188,20},{194,362},{189,21... | collective-permute-start | bytes 688136 | tf_op jit(solution)/shard_map/ppermute | solution.py:382
  9.7 18.8 %collective-permute-start = (bf16[128,2688]{1,0:T(8,128)(2,1)S(1)}, bf16[128,2688]{1,0:T(8,128)(2,1)S(1)}, u32[]{:S(2)}, u32[]{:S(2)}) collective-permute-start(bf16[128,2688]{1,0:T(8,128)(2,1)S(1)} %get-tuple-element.35), channel_id=1, source_target_pairs={{0,6},{1,7},{2,8},{3,9},{4,10},{5,11},{12,18},{13,19},{14,20},{15,... | collective-permute-start | bytes 2064392 | tf_op jit(solution)/shard_map/ppermute | solution.py:384
  11.6 18.7 %collective-permute-start.1 = (bf16[128,2688]{1,0:T(8,128)(2,1)S(1)}, bf16[128,2688]{1,0:T(8,128)(2,1)S(1)}, u32[]{:S(2)}, u32[]{:S(2)}) collective-permute-start(bf16[128,2688]{1,0:T(8,128)(2,1)S(1)} %get-tuple-element.37), channel_id=1, source_target_pairs={{6,12},{7,13},{8,14},{9,15},{10,16},{11,17},{18,24},{19,25},{20,26... | collective-permute-start | bytes 2064392 | tf_op jit(solution)/shard_map/ppermute | solution.py:383
  13.1 17.3 %collective-permute-start.3 = (bf16[128,896]{1,0:T(8,128)(2,1)S(1)}, bf16[128,896]{1,0:T(8,128)(2,1)S(1)}, u32[]{:S(2)}, u32[]{:S(2)}) collective-permute-start(bf16[128,896]{1,0:T(8,128)(2,1)S(1)} %hop.3), channel_id=1, source_target_pairs={{162,192},{216,186},{163,193},{217,187},{20,194},{362,188},{21,195... | collective-permute-start | bytes 688136 | tf_op jit(solution)/shard_map/ppermute | solution.py:386
  18.0 16.0 %collective-permute-start.5 = (bf16[128,896]{1,0:T(8,128)(2,1)S(1)}, bf16[128,896]{1,0:T(8,128)(2,1)S(1)}, u32[]{:S(2)}, u32[]{:S(2)}) collective-permute-start(bf16[128,896]{1,0:T(8,128)(2,1)S(1)} %hop.4), channel_id=1, source_target_pairs={{162,192},{216,186},{163,193},{217,187},{20,194},{362,188},{21,195... | collective-permute-start | bytes 688136 | tf_op jit(solution)/shard_map/ppermute | solution.py:386
  21.8 16.4 %collective-permute-start.7 = (bf16[128,896]{1,0:T(8,128)(2,1)S(1)}, bf16[128,896]{1,0:T(8,128)(2,1)S(1)}, u32[]{:S(2)}, u32[]{:S(2)}) collective-permute-start(bf16[128,896]{1,0:T(8,128)(2,1)S(1)} %hop.5), channel_id=1, source_target_pairs={{156,192},{222,186},{157,193},{223,187},{20,194},{362,188},{21,195... | collective-permute-start | bytes 688136 | tf_op jit(solution)/shard_map/ppermute | solution.py:386

commit v6 on v5

--- a/solution.py
+++ b/solution.py
@@ -320,8 +320,11 @@
     return pairs + [(b, a) for a, b in pairs]
 
 
-BESIDE, BEYOND, ACROSS = ((3, 6), (0, 1)), ((2, 6), (1, 1)), ((3, 0), (0, 7))
-RELAYS = ((BESIDE, BESIDE, BEYOND), (ACROSS, ACROSS, ACROSS))
+ACROSS = ((3, 0), (0, 7))
+RELAYS = (
+    (((3, 6), (1, 1)), ((3, 6), (0, 1)), ((2, 6), (1, 1))),
+    (((3, 0), (0, 1)), ACROSS, ACROSS),
+)
 CHUNKS = 3
 HOP_COST, ODD_COST, JOIN_COST, MERGE_COST = 10**10, 10**8, 10**6, 10**6
 

time: 54.9 us -> 54.8 us (level)
  the two profiles are of different devices: /device:TPU:192 before, /device:TPU:384 now
where the time goes in v6:
time: 54.8 us; the launch traced here: 54.5 us
  waiting for transfers between devices  21.2 us (39%)
  starting transfers between devices  13.5 us (25%)
  Pallas kernels  10.6 us (19%)
  blocking collectives  8.44 us (15%)
  between operations  0.74 us (1%)
    ppermute x3, waiting for transfers between devices, shards(): lax.ppermute(chunk, AXES, on)  8.98 us
    all_to_all x1, blocking collectives, shards(): sums = lax.all_to_all(sums, 'dp', 0, 0, tiled=True)  8.44 us
    ppermute x3, starting transfers between devices, shards(): lax.ppermute(chunk, AXES, out)  7.03 us
    ppermute x3, waiting for transfers between devices, shards(): lax.ppermute(chunk, AXES, out)  6.79 us
    ppermute x1, waiting for transfers between devices, shards(): recv0 = lax.ppermute(send0, AXES, even)  5.39 us
    ppermute x3, starting transfers between devices, shards(): lax.ppermute(chunk, AXES, on)  3.88 us
    pallas_call x1, Pallas kernels, shards(): call(functools.partial(grad_kernel, heads), 'grads', [VMEM] * 15, [local]...  3.71 us
    pallas_call x1, Pallas kernels, shards(): call(functools.partial(own_kernel, heads), 'own', [HBM] * 7, [shape((BLK,...  2.94 us
  transfers between devices with their start and end apart: 8, of which 7 were waited for; matrix products, arithmetic and copies ran while one was open for 0% of the time, Pallas kernels for 4%

profile of v6, /device:TPU:384, one launch (start us, length us, event | category | flops | bytes accessed | tf_op | source)
XLA Modules:
  0.0 54.5 jit_solution(11301657767472065680)
XLA Ops:
  0.6 2.9 %own.1 = (bf16[128,2688]{1,0:T(8,128)(2,1)S(1)}, bf16[128,2688]{1,0:T(8,128)(2,1)S(1)}, f32[256,512]{1,0:T(8,128)S(1)}, f32[256,128]{1,0:T(8,128)S(1)}, f32[4,25...) custom-call(s32[3,256]{1,0:T(4,128)} %bitcast.2, ...), custom_call_target="tpu_custom_call" | custom-call | tf_op jit(solution)/shard_map/own/pallas_call | solution.py:373
  3.6 4.4 %collective-permute-start.2 = (bf16[128,896]{1,0:T(8,128)(2,1)S(1)}, bf16[128,896]{1,0:T(8,128)(2,1)S(1)}, u32[]{:S(2)}, u32[]{:S(2)}) collective-permute-start(bf16[128,896]{1,0:T(8,128)(2,1)S(1)} %get-tuple-element.39), channel_id=1, source_target_pairs={{186,162},{192,222},{187,163},{193,223},{188,20},{194,218},{189,21... | collective-permute-start | bytes 688136 | tf_op jit(solution)/shard_map/ppermute | solution.py:385
  8.0 1.3 %collective-permute-start.4 = (bf16[128,896]{1,0:T(8,128)(2,1)S(1)}, bf16[128,896]{1,0:T(8,128)(2,1)S(1)}, u32[]{:S(2)}, u32[]{:S(2)}) collective-permute-start(bf16[128,896]{1,0:T(8,128)(2,1)S(1)} %get-tuple-element.40), channel_id=1, source_target_pairs={{186,162},{192,216},{187,163},{193,217},{188,20},{194,362},{189,21... | collective-permute-start | bytes 688136 | tf_op jit(solution)/shard_map/ppermute | solution.py:385
  9.3 1.3 %collective-permute-start.6 = (bf16[128,896]{1,0:T(8,128)(2,1)S(1)}, bf16[128,896]{1,0:T(8,128)(2,1)S(1)}, u32[]{:S(2)}, u32[]{:S(2)}) collective-permute-start(bf16[128,896]{1,0:T(8,128)(2,1)S(1)} %get-tuple-element.41), channel_id=1, source_target_pairs={{186,156},{192,222},{187,157},{193,223},{188,20},{194,362},{189,21... | collective-permute-start | bytes 688136 | tf_op jit(solution)/shard_map/ppermute | solution.py:385
  10.6 1.9 %collective-permute-start = (bf16[128,2688]{1,0:T(8,128)(2,1)S(1)}, bf16[128,2688]{1,0:T(8,128)(2,1)S(1)}, u32[]{:S(2)}, u32[]{:S(2)}) collective-permute-start(bf16[128,2688]{1,0:T(8,128)(2,1)S(1)} %get-tuple-element.35), channel_id=1, source_target_pairs={{0,6},{1,7},{2,8},{3,9},{4,10},{5,11},{12,18},{13,19},{14,20},{15,... | collective-permute-start | bytes 2064392 | tf_op jit(solution)/shard_map/ppermute | solution.py:387
  12.6 0.7 %collective-permute-start.1 = (bf16[128,2688]{1,0:T(8,128)(2,1)S(1)}, bf16[128,2688]{1,0:T(8,128)(2,1)S(1)}, u32[]{:S(2)}, u32[]{:S(2)}) collective-permute-start(bf16[128,2688]{1,0:T(8,128)(2,1)S(1)} %get-tuple-element.37), channel_id=1, source_target_pairs={{6,12},{7,13},{8,14},{9,15},{10,16},{11,17},{18,24},{19,25},{20,26... | collective-permute-start | bytes 2064392 | tf_op jit(solution)/shard_map/ppermute | solution.py:386
  13.3 0.7 %collective-permute-done.2.in_ref = bf16[128,896]{1,0:T(8,128)(2,1)S(1)} collective-permute-done((bf16[128,896]{1,0:T(8,128)(2,1)S(1)}, bf16[128,896]{1,0:T(8,128)(2,1)S(1)}, u32[]{:S(2)}, u32[]{:S(2)}) %collective-permute-start.2) | collective-permute-done | bytes 229408 | tf_op jit(solution)/shard_map/ppermute | solution.py:385
  14.0 1.3 %collective-permute-start.3 = (bf16[128,896]{1,0:T(8,128)(2,1)S(1)}, bf16[128,896]{1,0:T(8,128)(2,1)S(1)}, u32[]{:S(2)}, u32[]{:S(2)}) collective-permute-start(bf16[128,896]{1,0:T(8,128)(2,1)S(1)} %hop.3), channel_id=1, source_target_pairs={{162,192},{222,186},{163,193},{223,187},{20,194},{218,188},{21,195... | collective-permute-start | bytes 688136 | tf_op jit(solution)/shard_map/ppermute | solution.py:389
  15.3 3.6 %collective-permute-done.4.in_ref = bf16[128,896]{1,0:T(8,128)(2,1)S(1)} collective-permute-done((bf16[128,896]{1,0:T(8,128)(2,1)S(1)}, bf16[128,896]{1,0:T(8,128)(2,1)S(1)}, u32[]{:S(2)}, u32[]{:S(2)}) %collective-permute-start.4) | collective-permute-done | bytes 229408 | tf_op jit(solution)/shard_map/ppermute | solution.py:385
  18.9 1.3 %collective-permute-start.5 = (bf16[128,896]{1,0:T(8,128)(2,1)S(1)}, bf16[128,896]{1,0:T(8,128)(2,1)S(1)}, u32[]{:S(2)}, u32[]{:S(2)}) collective-permute-start(bf16[128,896]{1,0:T(8,128)(2,1)S(1)} %hop.4), channel_id=1, source_target_pairs={{162,192},{216,186},{163,193},{217,187},{20,194},{362,188},{21,195... | collective-permute-start | bytes 688136 | tf_op jit(solution)/shard_map/ppermute | solution.py:389
  20.2 2.5 %collective-permute-done.6.in_ref = bf16[128,896]{1,0:T(8,128)(2,1)S(1)} collective-permute-done((bf16[128,896]{1,0:T(8,128)(2,1)S(1)}, bf16[128,896]{1,0:T(8,128)(2,1)S(1)}, u32[]{:S(2)}, u32[]{:S(2)}) %collective-permute-start.6) | collective-permute-done | bytes 229408 | tf_op jit(solution)/shard_map/ppermute | solution.py:385
  22.7 1.3 %collective-permute-start.7 = (bf16[128,896]{1,0:T(8,128)(2,1)S(1)}, bf16[128,896]{1,0:T(8,128)(2,1)S(1)}, u32[]{:S(2)}, u32[]{:S(2)}) collective-permute-start(bf16[128,896]{1,0:T(8,128)(2,1)S(1)} %hop.5), channel_id=1, source_target_pairs={{156,192},{222,186},{157,193},{223,187},{20,194},{362,188},{21,195... | collective-permute-start | bytes 688136 | tf_op jit(solution)/shard_map/ppermute | solution.py:389
  24.0 5.4 %collective-permute-done.recv.recv0_ref = bf16[128,2688]{1,0:T(8,128)(2,1)S(1)} collective-permute-done((bf16[128,2688]{1,0:T(8,128)(2,1)S(1)}, bf16[128,2688]{1,0:T(8,128)(2,1)S(1)}, u32[]{:S(2)}, u32[]{:S(2)}) %collective-permute-start) | collective-permute-done | bytes 688160 | tf_op jit(solution)/shard_map/ppermute | solution.py:387
  29.4 1.9 %join_even.1 = (f32[256,512]{1,0:T(8,128)S(1)}, f32[1024,128]{1,0:T(8,128)S(1)}, f32[128,128]{1,0:T(8,128)S(1)}, f32[8,128]{1,0:T(8,128)S(1)}) custom-call(f32[8]{0:T(128)S(1)} %get-tuple-element.32.mask_ref, bf16[256,512]{1,0:T(8,128)(2,1)S(1)} %get-tuple-element.26.q_ref, bf16[256,512]{1,0:T(8,128)(2,1)S(1)} %get-tuple-element.27.k_ref, ...), custom_call_target="tpu_custom_call" | custom-call | flops 1000000 | bytes 524288 | tf_op jit(solution)/shard_map/join_even/pallas_call | solution.py:392
  31.3 0.0 collective-permute-done.1.in_ref
  31.3 0.1 collective-permute-done.3.refs_1_
  31.5 4.7 %collective-permute-done.5.refs_2_ = bf16[128,896]{1,0:T(8,128)(2,1)S(1)} collective-permute-done((bf16[128,896]{1,0:T(8,128)(2,1)S(1)}, bf16[128,896]{1,0:T(8,128)(2,1)S(1)}, u32[]{:S(2)}, u32[]{:S(2)}) %collective-permute-start.5) | collective-permute-done | bytes 229408 | tf_op jit(solution)/shard_map/ppermute | solution.py:389
  36.2 4.2 %collective-permute-done.7.refs_3_ = bf16[128,896]{1,0:T(8,128)(2,1)S(1)} collective-permute-done((bf16[128,896]{1,0:T(8,128)(2,1)S(1)}, bf16[128,896]{1,0:T(8,128)(2,1)S(1)}, u32[]{:S(2)}, u32[]{:S(2)}) %collective-permute-start.7) | collective-permute-done | bytes 229408 | tf_op jit(solution)/shard_map/ppermute | solution.py:389
  40.3 0.1 merge.1.b_ref
  40.4 0.1 odd.1.recv.recv1_ref
  40.5 1.9 %join_odd.1 = (f32[256,512]{1,0:T(8,128)S(1)}, f32[1024,128]{1,0:T(8,128)S(1)}, f32[128,128]{1,0:T(8,128)S(1)}, f32[6,8,128]{2,1,0:T(8,128)S(1)}) custom-call(f32[8]{0:T(128)S(1)} %get-tuple-element.32.mask_ref, bf16[256,512]{1,0:T(8,128)(2,1)S(1)} %get-tuple-element.26.q_ref, bf16[256,512]{1,0:T(8,128)(2,1)S(1)} %get-tuple-element.27.k_ref, ...), custom_call_target="tpu_custom_call" | custom-call | tf_op jit(solution)/shard_map/join_odd/pallas_call | solution.py:403
  42.3 8.4 %all_to_all.5.sums_ref = f32[6,8,128]{2,1,0:T(8,128)S(1)} all-to-all(f32[6,8,128]{2,1,0:T(8,128)S(1)} %get-tuple-element.47), channel_id=1, replica_groups=mesh['curve'=128,'dp'=6] {'dp'}, dimensions={0} | all-to-all | bytes 49152 | tf_op jit(solution)/shard_map/all_to_all | solution.py:406
  50.8 3.7 %grads.1 = (bf16[256,512]{1,0:T(8,128)(2,1)}, bf16[256,512]{1,0:T(8,128)(2,1)}, bf16[256,512]{1,0:T(8,128)(2,1)}, bf16[256,512]{1,0:T(8,128)(2,1)}) custom-call(bf16[256,512]{1,0:T(8,128)(2,1)S(1)} %get-tuple-element.26.q_ref, bf16[256,512]{1,0:T(8,128)(2,1)S(1)} %get-tuple-element.27.k_ref, bf16[256,512]{1,0:T(8,128)(2,1)S(1)} %get-tuple-element.28.v_ref, ...), custom_call_target="tpu_custom_call" | custom-call | tf_op jit(solution)/shard_map/grads/pallas_call | solution.py:407
  (4 shorter events, 0.1 us)
Async XLA Ops:
  3.6 10.4 %collective-permute-start.2 = (bf16[128,896]{1,0:T(8,128)(2,1)S(1)}, bf16[128,896]{1,0:T(8,128)(2,1)S(1)}, u32[]{:S(2)}, u32[]{:S(2)}) collective-permute-start(bf16[128,896]{1,0:T(8,128)(2,1)S(1)} %get-tuple-element.39), channel_id=1, source_target_pairs={{186,162},{192,222},{187,163},{193,223},{188,20},{194,218},{189,21... | collective-permute-start | bytes 688136 | tf_op jit(solution)/shard_map/ppermute | solution.py:385
  8.0 10.9 %collective-permute-start.4 = (bf16[128,896]{1,0:T(8,128)(2,1)S(1)}, bf16[128,896]{1,0:T(8,128)(2,1)S(1)}, u32[]{:S(2)}, u32[]{:S(2)}) collective-permute-start(bf16[128,896]{1,0:T(8,128)(2,1)S(1)} %get-tuple-element.40), channel_id=1, source_target_pairs={{186,162},{192,216},{187,163},{193,217},{188,20},{194,362},{189,21... | collective-permute-start | bytes 688136 | tf_op jit(solution)/shard_map/ppermute | solution.py:385
  9.3 13.4 %collective-permute-start.6 = (bf16[128,896]{1,0:T(8,128)(2,1)S(1)}, bf16[128,896]{1,0:T(8,128)(2,1)S(1)}, u32[]{:S(2)}, u32[]{:S(2)}) collective-permute-start(bf16[128,896]{1,0:T(8,128)(2,1)S(1)} %get-tuple-element.41), channel_id=1, source_target_pairs={{186,156},{192,222},{187,157},{193,223},{188,20},{194,362},{189,21... | collective-permute-start | bytes 688136 | tf_op jit(solution)/shard_map/ppermute | solution.py:385
  10.6 18.8 %collective-permute-start = (bf16[128,2688]{1,0:T(8,128)(2,1)S(1)}, bf16[128,2688]{1,0:T(8,128)(2,1)S(1)}, u32[]{:S(2)}, u32[]{:S(2)}) collective-permute-start(bf16[128,2688]{1,0:T(8,128)(2,1)S(1)} %get-tuple-element.35), channel_id=1, source_target_pairs={{0,6},{1,7},{2,8},{3,9},{4,10},{5,11},{12,18},{13,19},{14,20},{15,... | collective-permute-start | bytes 2064392 | tf_op jit(solution)/shard_map/ppermute | solution.py:387
  12.6 18.7 %collective-permute-start.1 = (bf16[128,2688]{1,0:T(8,128)(2,1)S(1)}, bf16[128,2688]{1,0:T(8,128)(2,1)S(1)}, u32[]{:S(2)}, u32[]{:S(2)}) collective-permute-start(bf16[128,2688]{1,0:T(8,128)(2,1)S(1)} %get-tuple-element.37), channel_id=1, source_target_pairs={{6,12},{7,13},{8,14},{9,15},{10,16},{11,17},{18,24},{19,25},{20,26... | collective-permute-start | bytes 2064392 | tf_op jit(solution)/shard_map/ppermute | solution.py:386
  14.0 17.5 %collective-permute-start.3 = (bf16[128,896]{1,0:T(8,128)(2,1)S(1)}, bf16[128,896]{1,0:T(8,128)(2,1)S(1)}, u32[]{:S(2)}, u32[]{:S(2)}) collective-permute-start(bf16[128,896]{1,0:T(8,128)(2,1)S(1)} %hop.3), channel_id=1, source_target_pairs={{162,192},{222,186},{163,193},{223,187},{20,194},{218,188},{21,195... | collective-permute-start | bytes 688136 | tf_op jit(solution)/shard_map/ppermute | solution.py:389
  18.9 17.2 %collective-permute-start.5 = (bf16[128,896]{1,0:T(8,128)(2,1)S(1)}, bf16[128,896]{1,0:T(8,128)(2,1)S(1)}, u32[]{:S(2)}, u32[]{:S(2)}) collective-permute-start(bf16[128,896]{1,0:T(8,128)(2,1)S(1)} %hop.4), channel_id=1, source_target_pairs={{162,192},{216,186},{163,193},{217,187},{20,194},{362,188},{21,195... | collective-permute-start | bytes 688136 | tf_op jit(solution)/shard_map/ppermute | solution.py:389
  22.7 17.6 %collective-permute-start.7 = (bf16[128,896]{1,0:T(8,128)(2,1)S(1)}, bf16[128,896]{1,0:T(8,128)(2,1)S(1)}, u32[]{:S(2)}, u32[]{:S(2)}) collective-permute-start(bf16[128,896]{1,0:T(8,128)(2,1)S(1)} %hop.5), channel_id=1, source_target_pairs={{156,192},{222,186},{157,193},{223,187},{20,194},{362,188},{21,195... | collective-permute-start | bytes 688136 | tf_op jit(solution)/shard_map/ppermute | solution.py:389

commit v7 on v6

--- a/solution.py
+++ b/solution.py
@@ -322,7 +322,7 @@
 
 ACROSS = ((3, 0), (0, 7))
 RELAYS = (
-    (((3, 6), (1, 1)), ((3, 6), (0, 1)), ((2, 6), (1, 1))),
+    (((3, 6), (1, 0)), ((3, 6), (0, 1)), ((2, 6), (1, 1))),
     (((3, 0), (0, 1)), ACROSS, ACROSS),
 )
 CHUNKS = 3

time: 54.8 us -> 54.3 us (level)
  the two profiles are of different devices: /device:TPU:384 before, /device:TPU:192 now
where the time goes in v7:
time: 54.3 us; the launch traced here: 54 us
  waiting for transfers between devices  19.9 us (37%)
  starting transfers between devices  12.5 us (23%)
  Pallas kernels  10.6 us (20%)
  blocking collectives  10.2 us (19%)
  between operations  0.75 us (1%)
    all_to_all x1, blocking collectives, shards(): sums = lax.all_to_all(sums, 'dp', 0, 0, tiled=True)  10.2 us
    ppermute x1, waiting for transfers between devices, shards(): recv0 = lax.ppermute(send0, AXES, even)  8.99 us
    ppermute x3, waiting for transfers between devices, shards(): lax.ppermute(chunk, AXES, on)  7.76 us
    ppermute x3, starting transfers between devices, shards(): lax.ppermute(chunk, AXES, out)  6.02 us
    ppermute x3, starting transfers between devices, shards(): lax.ppermute(chunk, AXES, on)  3.88 us
    pallas_call x1, Pallas kernels, shards(): call(functools.partial(grad_kernel, heads), 'grads', [VMEM] * 15, [local]...  3.71 us
    ppermute x3, waiting for transfers between devices, shards(): lax.ppermute(chunk, AXES, out)  3.18 us
    pallas_call x1, Pallas kernels, shards(): call(functools.partial(own_kernel, heads), 'own', [HBM] * 7, [shape((BLK,...  2.94 us
  transfers between devices with their start and end apart: 8, of which 6 were waited for; matrix products, arithmetic and copies ran while one was open for 0% of the time, Pallas kernels for 4%

profile of v7, /device:TPU:192, one launch (start us, length us, event | category | flops | bytes accessed | tf_op | source)
XLA Modules:
  0.0 54.0 jit_solution(17297019561324744599)
XLA Ops:
  0.6 2.9 %own.1 = (bf16[128,2688]{1,0:T(8,128)(2,1)S(1)}, bf16[128,2688]{1,0:T(8,128)(2,1)S(1)}, f32[256,512]{1,0:T(8,128)S(1)}, f32[256,128]{1,0:T(8,128)S(1)}, f32[4,25...) custom-call(s32[3,256]{1,0:T(4,128)} %bitcast.2, ...), custom_call_target="tpu_custom_call" | custom-call | tf_op jit(solution)/shard_map/own/pallas_call | solution.py:373
  3.6 3.4 %collective-permute-start.2 = (bf16[128,896]{1,0:T(8,128)(2,1)S(1)}, bf16[128,896]{1,0:T(8,128)(2,1)S(1)}, u32[]{:S(2)}, u32[]{:S(2)}) collective-permute-start(bf16[128,896]{1,0:T(8,128)(2,1)S(1)} %get-tuple-element.39), channel_id=1, source_target_pairs={{186,162},{192,198},{187,163},{193,199},{188,20},{194,218},{189,21... | collective-permute-start | bytes 688136 | tf_op jit(solution)/shard_map/ppermute | solution.py:385
  7.0 1.3 %collective-permute-start.4 = (bf16[128,896]{1,0:T(8,128)(2,1)S(1)}, bf16[128,896]{1,0:T(8,128)(2,1)S(1)}, u32[]{:S(2)}, u32[]{:S(2)}) collective-permute-start(bf16[128,896]{1,0:T(8,128)(2,1)S(1)} %get-tuple-element.40), channel_id=1, source_target_pairs={{186,162},{192,216},{187,163},{193,217},{188,20},{194,362},{189,21... | collective-permute-start | bytes 688136 | tf_op jit(solution)/shard_map/ppermute | solution.py:385
  8.3 1.3 %collective-permute-start.6 = (bf16[128,896]{1,0:T(8,128)(2,1)S(1)}, bf16[128,896]{1,0:T(8,128)(2,1)S(1)}, u32[]{:S(2)}, u32[]{:S(2)}) collective-permute-start(bf16[128,896]{1,0:T(8,128)(2,1)S(1)} %get-tuple-element.41), channel_id=1, source_target_pairs={{186,156},{192,222},{187,157},{193,223},{188,20},{194,362},{189,21... | collective-permute-start | bytes 688136 | tf_op jit(solution)/shard_map/ppermute | solution.py:385
  9.6 1.9 %collective-permute-start = (bf16[128,2688]{1,0:T(8,128)(2,1)S(1)}, bf16[128,2688]{1,0:T(8,128)(2,1)S(1)}, u32[]{:S(2)}, u32[]{:S(2)}) collective-permute-start(bf16[128,2688]{1,0:T(8,128)(2,1)S(1)} %get-tuple-element.35), channel_id=1, source_target_pairs={{0,6},{1,7},{2,8},{3,9},{4,10},{5,11},{12,18},{13,19},{14,20},{15,... | collective-permute-start | bytes 2064392 | tf_op jit(solution)/shard_map/ppermute | solution.py:387
  11.5 0.7 %collective-permute-start.1 = (bf16[128,2688]{1,0:T(8,128)(2,1)S(1)}, bf16[128,2688]{1,0:T(8,128)(2,1)S(1)}, u32[]{:S(2)}, u32[]{:S(2)}) collective-permute-start(bf16[128,2688]{1,0:T(8,128)(2,1)S(1)} %get-tuple-element.37), channel_id=1, source_target_pairs={{6,12},{7,13},{8,14},{9,15},{10,16},{11,17},{18,24},{19,25},{20,26... | collective-permute-start | bytes 2064392 | tf_op jit(solution)/shard_map/ppermute | solution.py:386
  12.3 0.0 collective-permute-done.2.in_ref
  12.3 1.3 %collective-permute-start.3 = (bf16[128,896]{1,0:T(8,128)(2,1)S(1)}, bf16[128,896]{1,0:T(8,128)(2,1)S(1)}, u32[]{:S(2)}, u32[]{:S(2)}) collective-permute-start(bf16[128,896]{1,0:T(8,128)(2,1)S(1)} %hop.3), channel_id=1, source_target_pairs={{162,192},{198,186},{163,193},{199,187},{20,194},{218,188},{21,195... | collective-permute-start | bytes 688136 | tf_op jit(solution)/shard_map/ppermute | solution.py:389
  13.6 0.7 %collective-permute-done.4.in_ref = bf16[128,896]{1,0:T(8,128)(2,1)S(1)} collective-permute-done((bf16[128,896]{1,0:T(8,128)(2,1)S(1)}, bf16[128,896]{1,0:T(8,128)(2,1)S(1)}, u32[]{:S(2)}, u32[]{:S(2)}) %collective-permute-start.4) | collective-permute-done | bytes 229408 | tf_op jit(solution)/shard_map/ppermute | solution.py:385
  14.3 1.3 %collective-permute-start.5 = (bf16[128,896]{1,0:T(8,128)(2,1)S(1)}, bf16[128,896]{1,0:T(8,128)(2,1)S(1)}, u32[]{:S(2)}, u32[]{:S(2)}) collective-permute-start(bf16[128,896]{1,0:T(8,128)(2,1)S(1)} %hop.4), channel_id=1, source_target_pairs={{162,192},{216,186},{163,193},{217,187},{20,194},{362,188},{21,195... | collective-permute-start | bytes 688136 | tf_op jit(solution)/shard_map/ppermute | solution.py:389
  15.6 2.5 %collective-permute-done.6.in_ref = bf16[128,896]{1,0:T(8,128)(2,1)S(1)} collective-permute-done((bf16[128,896]{1,0:T(8,128)(2,1)S(1)}, bf16[128,896]{1,0:T(8,128)(2,1)S(1)}, u32[]{:S(2)}, u32[]{:S(2)}) %collective-permute-start.6) | collective-permute-done | bytes 229408 | tf_op jit(solution)/shard_map/ppermute | solution.py:385
  18.1 1.3 %collective-permute-start.7 = (bf16[128,896]{1,0:T(8,128)(2,1)S(1)}, bf16[128,896]{1,0:T(8,128)(2,1)S(1)}, u32[]{:S(2)}, u32[]{:S(2)}) collective-permute-start(bf16[128,896]{1,0:T(8,128)(2,1)S(1)} %hop.5), channel_id=1, source_target_pairs={{156,192},{222,186},{157,193},{223,187},{20,194},{362,188},{21,195... | collective-permute-start | bytes 688136 | tf_op jit(solution)/shard_map/ppermute | solution.py:389
  19.4 9.0 %collective-permute-done.recv.recv0_ref = bf16[128,2688]{1,0:T(8,128)(2,1)S(1)} collective-permute-done((bf16[128,2688]{1,0:T(8,128)(2,1)S(1)}, bf16[128,2688]{1,0:T(8,128)(2,1)S(1)}, u32[]{:S(2)}, u32[]{:S(2)}) %collective-permute-start) | collective-permute-done | bytes 688160 | tf_op jit(solution)/shard_map/ppermute | solution.py:387
  28.4 1.9 %join_even.1 = (f32[256,512]{1,0:T(8,128)S(1)}, f32[1024,128]{1,0:T(8,128)S(1)}, f32[128,128]{1,0:T(8,128)S(1)}, f32[8,128]{1,0:T(8,128)S(1)}) custom-call(f32[8]{0:T(128)S(1)} %get-tuple-element.32.mask_ref, bf16[256,512]{1,0:T(8,128)(2,1)S(1)} %get-tuple-element.26.q_ref, bf16[256,512]{1,0:T(8,128)(2,1)S(1)} %get-tuple-element.27.k_ref, ...), custom_call_target="tpu_custom_call" | custom-call | flops 1000000 | bytes 524288 | tf_op jit(solution)/shard_map/join_even/pallas_call | solution.py:392
  30.3 0.0 collective-permute-done.1.in_ref
  30.3 0.3 collective-permute-done.3.refs_1_
  30.6 6.2 %collective-permute-done.5.refs_2_ = bf16[128,896]{1,0:T(8,128)(2,1)S(1)} collective-permute-done((bf16[128,896]{1,0:T(8,128)(2,1)S(1)}, bf16[128,896]{1,0:T(8,128)(2,1)S(1)}, u32[]{:S(2)}, u32[]{:S(2)}) %collective-permute-start.5) | collective-permute-done | bytes 229408 | tf_op jit(solution)/shard_map/ppermute | solution.py:389
  36.8 1.3 %collective-permute-done.7.refs_3_ = bf16[128,896]{1,0:T(8,128)(2,1)S(1)} collective-permute-done((bf16[128,896]{1,0:T(8,128)(2,1)S(1)}, bf16[128,896]{1,0:T(8,128)(2,1)S(1)}, u32[]{:S(2)}, u32[]{:S(2)}) %collective-permute-start.7) | collective-permute-done | bytes 229408 | tf_op jit(solution)/shard_map/ppermute | solution.py:389
  38.1 0.1 merge.1.b_ref
  38.2 0.1 odd.1.recv.recv1_ref
  38.2 1.9 %join_odd.1 = (f32[256,512]{1,0:T(8,128)S(1)}, f32[1024,128]{1,0:T(8,128)S(1)}, f32[128,128]{1,0:T(8,128)S(1)}, f32[6,8,128]{2,1,0:T(8,128)S(1)}) custom-call(f32[8]{0:T(128)S(1)} %get-tuple-element.32.mask_ref, bf16[256,512]{1,0:T(8,128)(2,1)S(1)} %get-tuple-element.26.q_ref, bf16[256,512]{1,0:T(8,128)(2,1)S(1)} %get-tuple-element.27.k_ref, ...), custom_call_target="tpu_custom_call" | custom-call | tf_op jit(solution)/shard_map/join_odd/pallas_call | solution.py:403
  40.1 10.2 %all_to_all.5.sums_ref = f32[6,8,128]{2,1,0:T(8,128)S(1)} all-to-all(f32[6,8,128]{2,1,0:T(8,128)S(1)} %get-tuple-element.47), channel_id=1, replica_groups=mesh['curve'=128,'dp'=6] {'dp'}, dimensions={0} | all-to-all | bytes 49152 | tf_op jit(solution)/shard_map/all_to_all | solution.py:406
  50.3 3.7 %grads.1 = (bf16[256,512]{1,0:T(8,128)(2,1)}, bf16[256,512]{1,0:T(8,128)(2,1)}, bf16[256,512]{1,0:T(8,128)(2,1)}, bf16[256,512]{1,0:T(8,128)(2,1)}) custom-call(bf16[256,512]{1,0:T(8,128)(2,1)S(1)} %get-tuple-element.26.q_ref, bf16[256,512]{1,0:T(8,128)(2,1)S(1)} %get-tuple-element.27.k_ref, bf16[256,512]{1,0:T(8,128)(2,1)S(1)} %get-tuple-element.28.v_ref, ...), custom_call_target="tpu_custom_call" | custom-call | tf_op jit(solution)/shard_map/grads/pallas_call | solution.py:407
  (4 shorter events, 0.1 us)
Async XLA Ops:
  3.6 8.7 %collective-permute-start.2 = (bf16[128,896]{1,0:T(8,128)(2,1)S(1)}, bf16[128,896]{1,0:T(8,128)(2,1)S(1)}, u32[]{:S(2)}, u32[]{:S(2)}) collective-permute-start(bf16[128,896]{1,0:T(8,128)(2,1)S(1)} %get-tuple-element.39), channel_id=1, source_target_pairs={{186,162},{192,198},{187,163},{193,199},{188,20},{194,218},{189,21... | collective-permute-start | bytes 688136 | tf_op jit(solution)/shard_map/ppermute | solution.py:385
  7.0 7.3 %collective-permute-start.4 = (bf16[128,896]{1,0:T(8,128)(2,1)S(1)}, bf16[128,896]{1,0:T(8,128)(2,1)S(1)}, u32[]{:S(2)}, u32[]{:S(2)}) collective-permute-start(bf16[128,896]{1,0:T(8,128)(2,1)S(1)} %get-tuple-element.40), channel_id=1, source_target_pairs={{186,162},{192,216},{187,163},{193,217},{188,20},{194,362},{189,21... | collective-permute-start | bytes 688136 | tf_op jit(solution)/shard_map/ppermute | solution.py:385
  8.3 9.8 %collective-permute-start.6 = (bf16[128,896]{1,0:T(8,128)(2,1)S(1)}, bf16[128,896]{1,0:T(8,128)(2,1)S(1)}, u32[]{:S(2)}, u32[]{:S(2)}) collective-permute-start(bf16[128,896]{1,0:T(8,128)(2,1)S(1)} %get-tuple-element.41), channel_id=1, source_target_pairs={{186,156},{192,222},{187,157},{193,223},{188,20},{194,362},{189,21... | collective-permute-start | bytes 688136 | tf_op jit(solution)/shard_map/ppermute | solution.py:385
  9.6 18.8 %collective-permute-start = (bf16[128,2688]{1,0:T(8,128)(2,1)S(1)}, bf16[128,2688]{1,0:T(8,128)(2,1)S(1)}, u32[]{:S(2)}, u32[]{:S(2)}) collective-permute-start(bf16[128,2688]{1,0:T(8,128)(2,1)S(1)} %get-tuple-element.35), channel_id=1, source_target_pairs={{0,6},{1,7},{2,8},{3,9},{4,10},{5,11},{12,18},{13,19},{14,20},{15,... | collective-permute-start | bytes 2064392 | tf_op jit(solution)/shard_map/ppermute | solution.py:387
  11.5 18.7 %collective-permute-start.1 = (bf16[128,2688]{1,0:T(8,128)(2,1)S(1)}, bf16[128,2688]{1,0:T(8,128)(2,1)S(1)}, u32[]{:S(2)}, u32[]{:S(2)}) collective-permute-start(bf16[128,2688]{1,0:T(8,128)(2,1)S(1)} %get-tuple-element.37), channel_id=1, source_target_pairs={{6,12},{7,13},{8,14},{9,15},{10,16},{11,17},{18,24},{19,25},{20,26... | collective-permute-start | bytes 2064392 | tf_op jit(solution)/shard_map/ppermute | solution.py:386
  12.3 18.3 %collective-permute-start.3 = (bf16[128,896]{1,0:T(8,128)(2,1)S(1)}, bf16[128,896]{1,0:T(8,128)(2,1)S(1)}, u32[]{:S(2)}, u32[]{:S(2)}) collective-permute-start(bf16[128,896]{1,0:T(8,128)(2,1)S(1)} %hop.3), channel_id=1, source_target_pairs={{162,192},{198,186},{163,193},{199,187},{20,194},{218,188},{21,195... | collective-permute-start | bytes 688136 | tf_op jit(solution)/shard_map/ppermute | solution.py:389
  14.3 22.5 %collective-permute-start.5 = (bf16[128,896]{1,0:T(8,128)(2,1)S(1)}, bf16[128,896]{1,0:T(8,128)(2,1)S(1)}, u32[]{:S(2)}, u32[]{:S(2)}) collective-permute-start(bf16[128,896]{1,0:T(8,128)(2,1)S(1)} %hop.4), channel_id=1, source_target_pairs={{162,192},{216,186},{163,193},{217,187},{20,194},{362,188},{21,195... | collective-permute-start | bytes 688136 | tf_op jit(solution)/shard_map/ppermute | solution.py:389
  18.1 20.0 %collective-permute-start.7 = (bf16[128,896]{1,0:T(8,128)(2,1)S(1)}, bf16[128,896]{1,0:T(8,128)(2,1)S(1)}, u32[]{:S(2)}, u32[]{:S(2)}) collective-permute-start(bf16[128,896]{1,0:T(8,128)(2,1)S(1)} %hop.5), channel_id=1, source_target_pairs={{156,192},{222,186},{157,193},{223,187},{20,194},{362,188},{21,195... | collective-permute-start | bytes 688136 | tf_op jit(solution)/shard_map/ppermute | solution.py:389
